TPU v7x, 256 devices: a whole 4x4x8 slice. The times are simulated.
256 devices in a mesh: dp: 16 (over z_hi, y), fsdp: 16 (over x, z_lo, core).
Axes of the slice: x: 4, y: 4, z: 8 (z_hi: 4, z_lo: 2; z = z_hi * 2 + z_lo), core: 2. Of those that a mesh axis runs over, the one named last changes fastest.
Arguments:
- features: bfloat16 [49152, 8192], P(('dp', 'fsdp')), may hold values from -6 to 6
- grad_out: bfloat16 [49152, 8192], P(('dp', 'fsdp')), may hold values from -6 to 6
- weight_tiles: bfloat16 [256, 128, 128], P('fsdp'), may hold values from -0.25 to 0.25
- tile_row: int32 [256], replicated, may hold values from 0 to 63, as said below
- tile_column: int32 [256], replicated, may hold values from 0 to 63, as said below
Outputs:
- grad_features: bfloat16 [49152, 8192], P(('dp', 'fsdp'))
- tile_update: float32 [256, 128, 128], P('fsdp')
Inputs may be any that keep to these rules, and one draw needn't show every extreme that they name: `tile_row`: every tile-row holds exactly 4 stored tiles; the tile-columns of tile-row i are i XOR s for the four values s in (0, 2^a, 2^b, 2^a + 2^b), with two distinct bits a, b drawn per run; the stored order is a random permutation of the pattern. Every tile-column holds exactly 4 stored tiles; no (tile_row, tile_column) pair appears twice.
All inputs are finite; a program needn't handle non-finite values.
Results may differ from a plain program's by a relative error of at most 0.0034.
Values may be sent and summed in bfloat16 or wider, within the bound.
No kernel may reach another device: no remote copies, remote signals or barrier semaphores. Data moves between devices by JAX's collectives and lax.ppermute only.
A program may use at most 128 MiB of HBM per device.

v0:
```python
import math

import jax
import jax.numpy as jnp
from jax import lax
from jax.sharding import PartitionSpec as P


def gelu_slope(value):
    root_term = math.sqrt(2.0 / math.pi)
    inner = root_term * (value + 0.044715 * value * value * value)
    hyper = jnp.tanh(inner)
    return 0.5 * (1.0 + hyper) + 0.5 * value * (1.0 - hyper * hyper) * root_term * (
        1.0 + 3.0 * 0.044715 * value * value
    )


def on_device(features, grad_out, weight_tiles, tile_row, tile_column):
    rows_here = features.shape[0]
    side = weight_tiles.shape[1]
    nblocks = features.shape[1] // side
    total_tiles = tile_row.shape[0]
    per_block = total_tiles // nblocks
    feature_blocks = features.reshape(rows_here, nblocks, side)
    grad_blocks = grad_out.reshape(rows_here, nblocks, side)
    order_rows = jnp.argsort(tile_row, stable=True)
    order_columns = jnp.argsort(tile_column, stable=True)
    columns_by_row = tile_column[order_rows].reshape(nblocks, per_block)
    rows_by_column = tile_row[order_columns].reshape(nblocks, per_block)
    whole = lax.all_gather(weight_tiles, "fsdp", axis=0, tiled=True)
    tiles_by_row = whole[order_rows].reshape(nblocks, per_block, side, side)
    taken = feature_blocks[:, columns_by_row]
    preact = jnp.einsum("rnkc,nkcd->rnd", taken, tiles_by_row, preferred_element_type=jnp.float32)
    slope_grad = (grad_blocks.astype(jnp.float32) * gelu_slope(preact)).astype(jnp.bfloat16)
    tiles_by_column = whole[order_columns].reshape(nblocks, per_block, side, side)
    slopes_taken = slope_grad[:, rows_by_column]
    returned = jnp.einsum(
        "rnkd,nkcd->rnc", slopes_taken, tiles_by_column, preferred_element_type=jnp.float32
    )
    grad_features = (
        (grad_blocks.astype(jnp.float32) + returned)
        .astype(jnp.bfloat16)
        .reshape(rows_here, nblocks * side)
    )
    tile_ids = jnp.arange(
        total_tiles // lax.axis_size("fsdp") * lax.axis_size("fsdp"), dtype=jnp.int32
    )
    columns = tile_column[tile_ids]
    row_ids = tile_row[tile_ids]
    picked = jnp.take(feature_blocks, columns, axis=1)
    slopes = jnp.take(slope_grad, row_ids, axis=1)
    summed = lax.psum_scatter(
        jnp.einsum("rnc,rnd->ncd", picked, slopes, preferred_element_type=jnp.float32),
        "fsdp",
        scatter_dimension=0,
        tiled=True,
    )
    weight_grad = lax.psum(summed, "dp")
    tile_update = weight_grad * lax.rsqrt(
        jnp.mean(weight_grad * weight_grad, axis=(1, 2), keepdims=True) + 1e-06
    )
    return (grad_features, tile_update)


def solution(mesh):
    return jax.shard_map(
        on_device,
        mesh=mesh,
        in_specs=(
            P(("dp", "fsdp"), None),
            P(("dp", "fsdp"), None),
            P("fsdp", None, None),
            P(),
            P(),
        ),
        out_specs=(P(("dp", "fsdp"), None), P("fsdp", None, None)),
        check_vma=False,
    )
```

profile of v0, /device:TPU:32, one launch (start us, length us, event | category | flops | bytes accessed | tf_op | source)
XLA Modules:
  0.0 481.2 jit_solution(4299826176216152528)
XLA Ops:
  7.2 0.0 copy-start
  7.2 0.0 all-gather.2.cloned.1.call-start
  7.2 0.7 all-gather.2.cloned.1.call-update
  7.9 0.0 reduce-scatter.2.cloned.1.call-start
  8.0 4.0 sort.32
  12.0 2.0 gather_fusion.7
  13.9 2.0 gather_fusion.6
  16.0 2.0 gather_fusion.2
  17.9 0.1 reshape.97
  18.1 0.1 reshape.143
  18.2 0.0 copy-done
  18.2 2.6 copy_bitcast_fusion.1
  20.7 0.0 copy-start.4
  20.7 13.0 %gather_fusion.3 = bf16[256,192,128]{2,1,0:T(8,128)(2,1)} fusion(bf16[192,64,128]{2,0,1:T(8,128)(2,1)} %copy_bitcast_fusion.1, s32[1024]{0:T(1024)S(1)} %pad_clamp_fusion.4), kind=kCustom, calls=%fused_computation.5 | custom fusion | bytes 25166848 | tf_op jit(solution)/shard_map/gather | solution.py:32
  33.8 0.0 copy-done.4
  33.8 10.8 %gather_fusion.8 = bf16[256,192,128]{2,1,0:T(8,128)(2,1)} fusion(bf16[192,64,128]{2,0,1:T(8,128)(2,1)S(1)} %copy-done.4, s32[1024]{0:T(1024)S(1)} %pad_clamp_fusion.1), kind=kCustom, calls=%fused_computation.clone | custom fusion | bytes 25166848 | tf_op jit(solution)/shard_map/jit(_take)/gather | solution.py:50
  44.6 22.6 %all-gather.2.cloned.1.call-done = bf16[256,128,128]{2,1,0:T(8,128)(2,1)} async-done(((bf16[16,128,128]{2,1,0:T(8,128)(2,1)}), bf16[256,128,128]{2,1,0:T(8,128)(2,1)}) %all-gather.2.cloned.1.call-update) | async-done | bytes 8388624 | tf_op jit(solution)/shard_map/all_gather | solution.py:30
  67.2 12.1 %gather_fusion.1 = bf16[256,128,128]{2,1,0:T(8,128)(2,1)} fusion(bf16[256,128,128]{2,1,0:T(8,128)(2,1)} %all-gather.2.cloned.1.call-done, s32[1024]{0:T(1024)S(1)} %pad_clamp_fusion.5), kind=kCustom, calls=%fused_computation.3 | custom fusion | bytes 16778240 | tf_op jit(solution)/shard_map/gather | solution.py:31
  79.3 11.0 %fusion.13 = bf16[192,64,128]{2,0,1:T(8,128)(2,1)S(1)} fusion(bf16[192,64,4,128]{3,0,2,1:T(8,128)(2,1)} %bitcast.65, bf16[64,4,128,128]{3,2,1,0:T(8,128)(2,1)} %bitcast.68, bf16[192,8192]{1,0:T(8,128)(2,1)} %param.8), kind=kOutput, calls=%fused_computation.25 | convolution fusion | flops 1642070016 | bytes 27262976 | tf_op jit(solution)/shard_map/rnkc,nkcd->rnd/dot_general | solution.py:33
  90.3 0.0 copy-start.5
  90.3 10.7 %gather_fusion.9 = bf16[256,192,128]{2,1,0:T(8,128)(2,1)} fusion(bf16[192,64,128]{2,0,1:T(8,128)(2,1)S(1)} %fusion.13, s32[1024]{0:T(1024)S(1)} %pad_clamp_fusion), kind=kCustom, calls=%fused_computation.1.clone | custom fusion | bytes 25166848 | tf_op jit(solution)/shard_map/jit(_take)/gather | solution.py:51
  101.0 0.0 copy-done.5
  101.0 14.6 %fusion = f32[256,128,128]{2,1,0:T(8,128)} fusion(bf16[256,192,128]{2,1,0:T(8,128)(2,1)} %gather_fusion.9, bf16[256,192,128]{2,1,0:T(8,128)(2,1)} %gather_fusion.8, pred[256]{0:T(512)(128)(4,1)S(1)} %get-tuple-element.7, pred[256]{0:T(512)(128)(4,1)S(1)} %get-tuple-element.8), kind=kOutput, calls=%fused_computation.10 | convolution fusion | flops 1623195648 | bytes 41943552 | tf_op jit(solution)/shard_map/rnc,rnd->ncd/dot_general | solution.py:53
  115.6 0.0 copy-start.2
  115.6 0.0 copy-start.3
  115.6 0.0 reduce-scatter.2.cloned.1.call-update
  115.7 0.0 all-reduce.2.cloned.1.call-start
  115.7 0.6 copy-done.2
  116.3 3.2 sort.31
  119.5 0.0 copy-done.3
  119.5 2.2 gather_fusion.4
  121.7 0.1 reshape.98
  121.8 0.1 reshape.159
  122.0 12.6 %gather_fusion.5 = bf16[256,192,128]{2,1,0:T(8,128)(2,1)} fusion(bf16[192,64,128]{2,0,1:T(8,128)(2,1)} %copy-done.5, s32[1024]{0:T(1024)S(1)} %pad_clamp_fusion.3), kind=kCustom, calls=%fused_computation.7 | custom fusion | bytes 25166848 | tf_op jit(solution)/shard_map/gather | solution.py:36
  134.5 12.3 %gather_fusion = bf16[256,128,128]{2,1,0:T(8,128)(2,1)} fusion(bf16[256,128,128]{2,1,0:T(8,128)(2,1)} %all-gather.2.cloned.1.call-done, s32[1024]{0:T(1024)S(1)} %pad_clamp_fusion.6), kind=kCustom, calls=%fused_computation.2 | custom fusion | bytes 16778240 | tf_op jit(solution)/shard_map/gather | solution.py:35
  146.8 151.0 %reduce-scatter.2.cloned.1.call-done = f32[16,128,128]{2,1,0:T(8,128)} async-done(((f32[256,128,128]{2,1,0:T(8,128)}), f32[16,128,128]{2,1,0:T(8,128)}) %reduce-scatter.2.cloned.1.call-update) | async-done | bytes 1048592 | tf_op jit(solution)/shard_map/reduce_scatter | solution.py:52
  297.8 0.0 all-reduce.2.cloned.1.call-update
  297.8 0.0 copy-start.1
  297.8 12.5 %fusion.18 = bf16[64,24,8,128]{3,2,1,0:T(8,128)(2,1)} fusion(bf16[64,4,128,128]{3,2,1,0:T(8,128)(2,1)} %bitcast.67, bf16[192,64,4,128]{3,0,2,1:T(8,128)(2,1)} %bitcast.66, bf16[192,8192]{1,0:T(8,128)(2,1)} %param.8), kind=kOutput, calls=%fused_computation.33 | convolution fusion | flops 1615331328 | bytes 27262976 | tf_op jit(solution)/shard_map/rnkd,nkcd->rnc/dot_general | solution.py:37
  310.4 4.4 copy.32
  314.8 156.1 %all-reduce.2.cloned.1.call-done = f32[16,128,128]{2,1,0:T(8,128)} async-done(((f32[16,128,128]{2,1,0:T(8,128)}), f32[16,128,128]{2,1,0:T(8,128)}) %all-reduce.2.cloned.1.call-update) | async-done | bytes 1048592 | tf_op jit(solution)/shard_map/psum | solution.py:58
  470.9 1.4 multiply_reduce_fusion
  472.3 2.3 broadcast_multiply_fusion
  474.6 0.0 copy-done.1
  (18 shorter events, 0.1 us)
Async XLA Ops:
  7.2 11.0 %copy-start = (bf16[192,8192]{1,0:T(8,128)(2,1)S(1)}, bf16[192,8192]{1,0:T(8,128)(2,1)}, u32[]{:S(2)}) copy-start(bf16[192,8192]{1,0:T(8,128)(2,1)} %param.7) | copy-start | bytes 9437188
  7.2 60.0 %all-gather.2.cloned.1.call-start = ((), (), s32[]{:S(2)}) async-start(), calls=%async_computation.1 | async-start | bytes 8912896 | tf_op jit(solution)/shard_map/all_gather | solution.py:30
  7.9 289.9 %reduce-scatter.2.cloned.1.call-start = ((), (), s32[]{:S(2)}) async-start(), calls=%async_computation.2 | async-start | bytes 17825792 | tf_op jit(solution)/shard_map/reduce_scatter | solution.py:52
  20.7 13.0 %copy-start.4 = (bf16[192,64,128]{2,0,1:T(8,128)(2,1)S(1)}, bf16[192,64,128]{2,0,1:T(8,128)(2,1)}, u32[]{:S(2)}) copy-start(bf16[192,64,128]{2,0,1:T(8,128)(2,1)} %copy_bitcast_fusion.1) | copy-start | bytes 9437188
  90.3 10.7 %copy-start.5 = (bf16[192,64,128]{2,0,1:T(8,128)(2,1)}, bf16[192,64,128]{2,0,1:T(8,128)(2,1)S(1)}, u32[]{:S(2)}) copy-start(bf16[192,64,128]{2,0,1:T(8,128)(2,1)S(1)} %fusion.13) | copy-start | bytes 9437188
  115.6 0.7 copy-start.2
  115.6 3.9 copy-start.3
  115.7 355.2 %all-reduce.2.cloned.1.call-start = ((), (), s32[]{:S(2)}) async-start(), calls=%async_computation.3 | async-start | bytes 2097152 | tf_op jit(solution)/shard_map/psum | solution.py:58
  297.8 176.8 %copy-start.1 = (bf16[192,8192]{1,0:T(8,128)(2,1)S(1)}, bf16[192,8192]{1,0:T(8,128)(2,1)}, u32[]{:S(2)}) copy-start(bf16[192,8192]{1,0:T(8,128)(2,1)} %param.7) | copy-start | bytes 9437188
Sparse Core Ops, SparseCore 0:
  9.9 57.2 all-gather.1
  115.8 181.9 reduce-scatter.1
  300.4 170.3 all-reduce.1
where the time goes:
time: 483 us; the launch traced here: 481 us
  waiting for transfers between devices  330 us (68%)
  local copies, waits for them, and re-layouts  87.6 us (18%)
  matrix products  38.2 us (8%)
  between operations  13.9 us (3%)
  other arithmetic  11 us (2%)
    psum x1, waiting for transfers between devices, on_device(): weight_grad = lax.psum(summed, 'dp')  156 us
    reduce_scatter x1, waiting for transfers between devices, on_device(): lax.psum_scatter(jnp.einsum('rnc,rnd->ncd', picked, slopes, preferred_ele...  151 us
    all_gather x1, waiting for transfers between devices, on_device(): whole = lax.all_gather(weight_tiles, 'fsdp', axis=0, tiled=True)  22.6 us
    dot_general x1, matrix products, on_device(): jnp.einsum('rnc,rnd->ncd', picked, slopes, preferred_element_type=jnp.flo...  14.6 us
    gather x1, local copies, waits for them, and re-layouts, on_device(): taken = feature_blocks[:, columns_by_row]  13 us
    gather x1, local copies, waits for them, and re-layouts, on_device(): slopes_taken = slope_grad[:, rows_by_column]  12.6 us
    dot_general x1, matrix products, on_device(): jnp.einsum('rnkd,nkcd->rnc', slopes_taken, tiles_by_column, preferred_ele...  12.5 us
    gather x1, local copies, waits for them, and re-layouts, on_device(): whole[order_columns].reshape(nblocks, per_block, side, side)  12.3 us
  transfers between devices with their start and end apart: 3, of which 3 were waited for; matrix products, arithmetic and copies ran while one was open for 17% of the time, Pallas kernels for 0%

commit v1 on v0

v1 whole, which is shorter than its diff:
```python
import functools
import math

import jax
import jax.numpy as jnp
from jax import lax
from jax.experimental import pallas as pl
from jax.experimental.pallas import tpu as pltpu
from jax.sharding import Mesh
from jax.sharding import PartitionSpec as P

AXES = ("zh", "y", "x", "zl", "core")
SIZES = (4, 4, 4, 2, 2)
SIDE = 128
ROOT = math.sqrt(2.0 / math.pi)
CUBIC = 0.044715

VMEM = pl.BlockSpec(memory_space=pltpu.VMEM)
SMEM = pl.BlockSpec(memory_space=pltpu.SMEM)
PARAMS = pltpu.CompilerParams(vmem_limit_bytes=52 * 1024 * 1024)


def shape(dims, dtype):
    return jax.ShapeDtypeStruct(dims, dtype)


def lanes(block):
    return pl.ds(pl.multiple_of(block * SIDE, SIDE), SIDE)


def slope_times(value, cotangent):
    square = value * value
    hyper = jnp.tanh(value * (ROOT + (ROOT * CUBIC) * square))
    slope = 0.5 * (1.0 + hyper) + (0.5 * value) * (1.0 - hyper * hyper) * (
        ROOT + (3.0 * ROOT * CUBIC) * square
    )
    return cotangent * slope


def forward_kernel(place, blocks, x_ref, g_ref, w_ref, s_ref):
    def one(group, carry):
        ids = [blocks[group * 4 + m] for m in range(4)]
        x = jnp.concatenate([x_ref[:, lanes(b)] for b in ids], axis=1)
        for first in (0, 2):
            pair = (first, first + 1)
            w = jnp.concatenate(
                [
                    jnp.concatenate([w_ref[place[ids[n] * 4 + (n ^ m)]] for n in pair], axis=1)
                    for m in range(4)
                ],
                axis=0,
            )
            pre = jnp.dot(x, w, preferred_element_type=jnp.float32)
            for k, n in enumerate(pair):
                cot = g_ref[:, lanes(ids[n])].astype(jnp.float32)
                out = slope_times(pre[:, k * SIDE : (k + 1) * SIDE], cot)
                s_ref[ids[n]] = out.astype(jnp.bfloat16)
        return carry

    lax.fori_loop(0, 16, one, 0)


def backward_kernel(place, blocks, g_ref, w_ref, s_ref, o_ref):
    def one(group, carry):
        ids = [blocks[group * 4 + m] for m in range(4)]
        s = jnp.concatenate([s_ref[b] for b in ids], axis=1)
        for first in (0, 2):
            pair = (first, first + 1)
            w = jnp.concatenate(
                [
                    jnp.concatenate(
                        [w_ref[place[ids[n] * 4 + (n ^ m)]] for n in range(4)], axis=1
                    )
                    for m in pair
                ],
                axis=0,
            )
            back = lax.dot_general(
                s, w, (((1,), (1,)), ((), ())), preferred_element_type=jnp.float32
            )
            for k, m in enumerate(pair):
                cot = g_ref[:, lanes(ids[m])].astype(jnp.float32)
                total = cot + back[:, k * SIDE : (k + 1) * SIDE]
                o_ref[:, lanes(ids[m])] = total.astype(jnp.bfloat16)
        return carry

    lax.fori_loop(0, 16, one, 0)


def transpose_kernel(mine_ref, other_ref, xt_ref):
    def one(block, carry):
        rows = jnp.concatenate([mine_ref[:, lanes(block)], other_ref[:, lanes(block)]], axis=0)
        xt_ref[block] = rows.T
        return carry

    lax.fori_loop(0, 64, one, 0)


GROUPS = (("x", 0), ("x", 1), ("y", 0), ("y", 1))
SENT = ((1, 2), (3, 2))
KEPT = ((0, 3), (0, 1))


def partial_kernel(which, splits, rows, cols, where, xt_ref, s_ref, t_ref, *outs):
    x, y, zl, core = where[0], where[1], where[2], where[3]
    for group, (axis, half) in enumerate(GROUPS):
        for p, rel in enumerate(which[half]):
            for other in range(4):
                for low in range(2):
                    rx, ry = (rel, other) if axis == "x" else (other, rel)
                    to_zl = (1 - zl) if axis == "x" else zl
                    k = (y ^ ry) * 4 + half * 2 + low
                    tile = (((x ^ rx) * 2 + to_zl) * 2 + core) * 16 + k
                    row, col = rows[tile], cols[tile]
                    s = jnp.concatenate([s_ref[row], t_ref[row]], axis=0)
                    value = jnp.dot(xt_ref[col], s, preferred_element_type=jnp.float32)
                    if splits:
                        out, at = outs[group * 2 + p], other * 2 + low
                    else:
                        out, at = outs[group], p * 8 + other * 2 + low
                    out[at] = value.astype(out.dtype)


def finish_kernel(where, *refs):
    out = refs[-1]
    y = where[1]
    for r in range(4):
        for k in range(4):
            grad = refs[r][k]
            mean = jnp.mean(grad * grad)
            out[(y ^ r) * 4 + k] = grad * lax.rsqrt(mean + 1e-06)


def sum_four_kernel(a, b, c, d, out):
    f32 = jnp.float32
    out[...] = (a[...].astype(f32) + b[...].astype(f32)) + (
        c[...].astype(f32) + d[...].astype(f32)
    )


def swap(value, axis, mask):
    size = SIZES[AXES.index(axis)]
    return lax.ppermute(value, axis, [(i, i ^ mask) for i in range(size)])


def tables(tile_row, tile_column):
    differ = tile_row ^ tile_column
    both = lax.reduce(differ, jnp.int32(0), lax.bitwise_or, (0,))
    low = both & -both
    high = both ^ low
    kind = jnp.where((differ & low) != 0, 1, 0) + jnp.where((differ & high) != 0, 2, 0)
    slot = tile_row * 4 + kind
    index = jnp.arange(256, dtype=jnp.int32)
    place = jnp.sum(jnp.where(slot[None, :] == index[:, None], index[None, :], 0), axis=1)
    group = jnp.arange(16, dtype=jnp.int32)
    base = group + (group & ~(low - 1))
    base = base + (base & ~(high - 1))
    member = jnp.stack([0 * low, low, high, both])
    blocks = (base[:, None] ^ member[None, :]).reshape(64)
    return place.astype(jnp.int32), blocks.astype(jnp.int32)


def on_device(features, grad_out, weight_tiles, tile_row, tile_column):
    bf16, f32 = jnp.bfloat16, jnp.float32
    tile_row = tile_row.astype(jnp.int32)
    tile_column = tile_column.astype(jnp.int32)
    rows_here = features.shape[0]
    where = jnp.stack([lax.axis_index(a) for a in ("x", "y", "zl", "core")]).astype(jnp.int32)
    whole = lax.all_gather(weight_tiles, ("x", "zl", "core"), axis=0, tiled=True)
    others = swap(features, "core", 1)
    xt = pl.pallas_call(
        transpose_kernel,
        out_shape=shape((64, SIDE, 2 * rows_here), bf16),
        in_specs=[VMEM, VMEM],
        out_specs=VMEM,
        compiler_params=PARAMS,
    )(features, others)
    place, blocks = tables(tile_row, tile_column)
    slopes = pl.pallas_call(
        forward_kernel,
        out_shape=shape((64, rows_here, SIDE), bf16),
        in_specs=[SMEM, SMEM, VMEM, VMEM, VMEM],
        out_specs=VMEM,
        compiler_params=PARAMS,
    )(place, blocks, features, grad_out, whole)
    other_slopes = swap(slopes, "core", 1)
    operands = (tile_row, tile_column, where, xt, slopes, other_slopes)
    sent = pl.pallas_call(
        functools.partial(partial_kernel, SENT, False),
        out_shape=[shape((16, SIDE, SIDE), bf16)] * 4,
        in_specs=[SMEM] * 3 + [VMEM] * 3,
        out_specs=[VMEM] * 4,
        compiler_params=PARAMS,
    )(*operands)
    got = [
        swap(value, axis, (1, 3)[half]) for value, (axis, half) in zip(sent, GROUPS, strict=True)
    ]
    kept = pl.pallas_call(
        functools.partial(partial_kernel, KEPT, True),
        out_shape=[shape((8, SIDE, SIDE), f32)] * 8,
        in_specs=[SMEM] * 3 + [VMEM] * 3,
        out_specs=[VMEM] * 8,
        compiler_params=PARAMS,
    )(*operands)
    grad_features = pl.pallas_call(
        backward_kernel,
        out_shape=shape(features.shape, bf16),
        in_specs=[SMEM, SMEM, VMEM, VMEM, VMEM],
        out_specs=VMEM,
        compiler_params=PARAMS,
    )(place, blocks, grad_out, whole, slopes)

    second = [
        swap((kept[2 * i + 1] + got[i][8:].astype(f32)).astype(bf16), axis, (3, 1)[half])
        for i, (axis, half) in enumerate(GROUPS)
    ]
    held = [
        kept[2 * i] + got[i][:8].astype(f32) + second[i].astype(f32) for i in range(4)
    ]
    pieces = []
    for i, axis in ((0, "y"), (2, "x")):
        both = jnp.concatenate(
            [held[i].reshape(4, 2, SIDE, SIDE), held[i + 1].reshape(4, 2, SIDE, SIDE)], axis=1
        )
        away = [swap(both[r].astype(bf16), axis, r) for r in (1, 3, 2)]
        pieces.append(
            both[0] + (away[0].astype(f32) + away[1].astype(f32)) + away[2].astype(f32)
        )
    mine = (pieces[1] + swap(pieces[0], "zl", 1)).astype(bf16)
    across = [swap(mine, "zh", r) for r in (1, 2, 3)]
    summed = pl.pallas_call(
        sum_four_kernel,
        out_shape=shape((4, SIDE, SIDE), f32),
        in_specs=[VMEM] * 4,
        out_specs=VMEM,
        compiler_params=PARAMS,
    )(mine, *across)
    gathered = [swap(summed, "y", r) for r in (1, 2, 3)]
    tile_update = pl.pallas_call(
        finish_kernel,
        out_shape=shape((16, SIDE, SIDE), f32),
        in_specs=[SMEM] + [VMEM] * 4,
        out_specs=VMEM,
        compiler_params=PARAMS,
    )(where, summed, *gathered)
    return grad_features, tile_update


def solution(mesh):
    grid = Mesh(mesh.devices.reshape(SIZES), AXES)
    return jax.shard_map(
        on_device,
        mesh=grid,
        in_specs=(P(AXES, None), P(AXES, None), P(("x", "zl", "core"), None, None), P(), P()),
        out_specs=(P(AXES, None), P(("x", "zl", "core"), None, None)),
        check_vma=False,
    )
```

time: 483 us -> 192 us (0.40)
  waiting for transfers between devices: 330 us -> 76.4 us
  local copies, waits for them, and re-layouts: 87.6 us -> 1.83 us
  Pallas kernels: 0 us -> 55.7 us
  matrix products: 38.2 us -> 0 us
  starting transfers between devices: 0.12 us -> 34.2 us
  other arithmetic: 11 us -> 6.03 us
    psum x1 -> x0, waiting for transfers between devices: 156 us -> none  [on_device(): weight_grad = lax.psum(summed, 'dp')]
    reduce_scatter x1 -> x0, waiting for transfers between devices: 151 us -> none  [on_device(): lax.psum_scatter(jnp.einsum('rnc,rnd->ncd', picked, slopes, preferred_ele...]
    gather x10 -> x0, local copies, waits for them, and re-layouts: 79.6 us -> none  [the longest x1 13 us: on_device(): taken = feature_blocks[:, columns_by_row]]
    pallas_call x0 -> x7, Pallas kernels: none -> 55.7 us  [the longest x1 14.3 us: on_device(): pl.pallas_call(forward_kernel, out_shape=shape((64, rows_here, SIDE), bf1...]
    dot_general x3 -> x0, matrix products: 38.2 us -> none  [the longest x1 14.6 us: on_device(): jnp.einsum('rnc,rnd->ncd', picked, slopes, preferred_element_type=jnp.flo...]
    ppermute x0 -> x23, starting transfers between devices: none -> 34.2 us  [swap(): return lax.ppermute(value, axis, [(i, i ^ mask) for i in range(size)])]
    all_gather x1, waiting for transfers between devices: 22.6 us -> 54.1 us  [on_device(): lax.all_gather(weight_tiles, ('x', 'zl', 'core'), axis=0, tiled=True)]
    ppermute x0 -> x23, waiting for transfers between devices: none -> 21.6 us  [swap(): return lax.ppermute(value, axis, [(i, i ^ mask) for i in range(size)])]
  transfers between devices with their start and end apart: 3 -> 24, of which waited for: 3 -> 11; matrix products, arithmetic and copies ran while one was open for 17% -> 3% of each run, Pallas kernels for 0% -> 24%
where the time goes in v1:
time: 192 us; the launch traced here: 190 us
  waiting for transfers between devices  76.4 us (40%)
  Pallas kernels  55.7 us (29%)
  starting transfers between devices  34.2 us (18%)
  between operations  16.1 us (8%)
  other arithmetic  6.03 us (3%)
    all_gather x1, waiting for transfers between devices, on_device(): lax.all_gather(weight_tiles, ('x', 'zl', 'core'), axis=0, tiled=True)  54.1 us
    ppermute x23, starting transfers between devices, swap(): return lax.ppermute(value, axis, [(i, i ^ mask) for i in range(size)])  34.2 us
    ppermute x23, waiting for transfers between devices, swap(): return lax.ppermute(value, axis, [(i, i ^ mask) for i in range(size)])  21.6 us
    pallas_call x1, Pallas kernels, on_device(): pl.pallas_call(forward_kernel, out_shape=shape((64, rows_here, SIDE), bf1...  14.3 us
    pallas_call x1, Pallas kernels, on_device(): pl.pallas_call(backward_kernel, out_shape=shape(features.shape, bf16), in...  12.6 us
    pallas_call x1, Pallas kernels, on_device(): pl.pallas_call(transpose_kernel, out_shape=shape((64, SIDE, 2 * rows_here...  11.3 us
    pallas_call x1, Pallas kernels, on_device(): pl.pallas_call(functools.partial(partial_kernel, KEPT, True), out_shape=[...  7.75 us
    pallas_call x1, Pallas kernels, on_device(): pl.pallas_call(functools.partial(partial_kernel, SENT, False), out_shape=...  7.28 us
  transfers between devices with their start and end apart: 24, of which 11 were waited for; matrix products, arithmetic and copies ran while one was open for 3% of the time, Pallas kernels for 24%

profile of v1, /device:TPU:32, one launch (start us, length us, event | category | flops | bytes accessed | tf_op | source)
XLA Modules:
  0.0 190.3 jit_solution(3364350924990573835)
XLA Ops:
  7.2 0.7 all-gather.2.cloned.1.call-update
  7.9 0.1 collective-permute-start
  8.0 1.3 fusion.14
  11.3 0.7 pad_add_fusion
  12.2 0.7 fusion.13
  12.9 0.1 select_reduce_fusion.place
  13.0 54.1 %all-gather.2.cloned.1.call-done.w_ref = bf16[256,128,128]{2,1,0:T(8,128)(2,1)} async-done(((bf16[16,128,128]{2,1,0:T(8,128)(2,1)}), bf16[256,128,128]{2,1,0:T(8,128)(2,1)}) %all-gather.2.cloned.1.call-update) | async-done | bytes 8388624 | tf_op jit(solution)/shard_map/all_gather | solution.py:169
  67.1 14.3 %shard_map.68.s_ref = bf16[64,192,128]{2,1,0:T(8,128)(2,1)} custom-call(s32[256]{0:T(256)S(1)} %select_reduce_fusion.place, s32[64]{0:T(128)S(1)} %xor.28.blocks, bf16[192,8192]{1,0:T(8,128)(2,1)} %mine_ref.1, bf16[192,8192]{1,0:T(8,128)(2,1)} %g_ref.3, bf16[256,128,128]{2,1,0:T(8,128)(2,1)} %all-gather.2.cloned.1.call-done.w_ref), custom_call_target="tpu_custom_call" | custom-call | tf_op jit(solution)/shard_map/pallas_call | solution.py:179
  81.4 0.3 collective-permute-start.1
  81.8 11.3 %shard_map.70.xt_ref = bf16[64,128,384]{2,1,0:T(8,128)(2,1)} custom-call(bf16[192,8192]{1,0:T(8,128)(2,1)} %mine_ref.1, bf16[192,8192]{1,0:T(8,128)(2,1)} %collective-permute-done.other_ref), custom_call_target="tpu_custom_call" | custom-call | tf_op jit(solution)/shard_map/pallas_call | solution.py:171
  93.1 1.7 copy-done.2
  94.8 7.3 %shard_map.72 = (bf16[16,128,128]{2,1,0:T(8,128)(2,1)S(1)}, bf16[16,128,128]{2,1,0:T(8,128)(2,1)S(1)}, bf16[16,128,128]{2,1,0:T(8,128)(2,1)S(1)}, bf16[16,128,128]{2,1,0:T(8,128)(2,1)}) custom-call(s32[256]{0:T(256)S(1)} %copy-done, s32[256]{0:T(256)S(1)} %copy-done.1, s32[4]{0:T(128)S(1)} %pad_add_fusion.1.where, bf16[64,128,384]{2,1,0:T(8,128)(2,1)} %shard_map.70.xt_ref, ...), custom_call_target="tpu_custom_call" | custom-call | tf_op jit(solution)/shard_map/pallas_call | solution.py:188
  102.0 1.5 collective-permute-start.2
  103.5 1.5 collective-permute-start.9
  105.0 2.1 %collective-permute-start.4 = (bf16[16,128,128]{2,1,0:T(8,128)(2,1)}, bf16[16,128,128]{2,1,0:T(8,128)(2,1)S(1)}, u32[]{:S(2)}, u32[]{:S(2)}) collective-permute-start(bf16[16,128,128]{2,1,0:T(8,128)(2,1)} %get-tuple-element.18), channel_id=1, source_target_pairs={{0,48},{16,32},{32,16},{48,0},{1,49},{17,33},{33,17},{49,1},{2,50}... | collective-permute-start | bytes 1572872 | tf_op jit(solution)/shard_map/ppermute | solution.py:143
  107.1 1.8 collective-permute-start.11
  108.9 7.7 %shard_map.71 = (f32[8,128,128]{2,1,0:T(8,128)S(1)}, f32[8,128,128]{2,1,0:T(8,128)S(1)}, f32[8,128,128]{2,1,0:T(8,128)S(1)}, f32[8,128,128]{2,1,0:T(8,128)}, f32...) custom-call(s32[256]{0:T(256)S(1)} %copy-done, ...), custom_call_target="tpu_custom_call" | custom-call | tf_op jit(solution)/shard_map/pallas_call | solution.py:198
  116.6 1.2 add_convert_fusion.3
  117.8 2.3 %collective-permute-start.3 = (bf16[8,128,128]{2,1,0:T(8,128)(2,1)S(1)}, bf16[8,128,128]{2,1,0:T(8,128)(2,1)S(1)}, u32[]{:S(2)}, u32[]{:S(2)}) collective-permute-start(bf16[8,128,128]{2,1,0:T(8,128)(2,1)S(1)} %add_convert_fusion.3), channel_id=1, source_target_pairs={{0,48},{16,32},{32,16},{48,0},{1,49},{17,33},{33,17},{49,1},{2,50}... | collective-permute-start | bytes 786440 | tf_op jit(solution)/shard_map/ppermute | solution.py:143
  120.1 2.1 %collective-permute-start.10 = (bf16[8,128,128]{2,1,0:T(8,128)(2,1)S(1)}, bf16[8,128,128]{2,1,0:T(8,128)(2,1)S(1)}, u32[]{:S(2)}, u32[]{:S(2)}) collective-permute-start(bf16[8,128,128]{2,1,0:T(8,128)(2,1)S(1)} %add_convert_fusion.1), channel_id=1, source_target_pairs={{0,12},{4,8},{8,4},{12,0},{1,13},{5,9},{9,5},{13,1},{2,14},{6,10},... | collective-permute-start | bytes 786440 | tf_op jit(solution)/shard_map/ppermute | solution.py:143
  122.2 1.1 add_convert_fusion.2
  123.3 0.3 collective-permute-start.5
  123.7 0.7 collective-permute-start.12
  124.5 4.4 %collective-permute-done.10 = bf16[8,128,128]{2,1,0:T(8,128)(2,1)S(1)} collective-permute-done((bf16[8,128,128]{2,1,0:T(8,128)(2,1)S(1)}, bf16[8,128,128]{2,1,0:T(8,128)(2,1)S(1)}, u32[]{:S(2)}, u32[]{:S(2)}) %collective-permute-start.10) | collective-permute-done | bytes 262176 | tf_op jit(solution)/shard_map/ppermute | solution.py:143
  128.9 1.8 collective-permute-done.12
  130.9 1.8 collective-permute-start.13
  132.7 0.8 collective-permute-start.15
  133.5 2.2 %collective-permute-start.14 = (bf16[4,128,128]{2,1,0:T(8,128)(2,1)S(1)}, bf16[4,128,128]{2,1,0:T(8,128)(2,1)S(1)}, u32[]{:S(2)}, u32[]{:S(2)}) collective-permute-start(bf16[4,128,128]{2,1,0:T(8,128)(2,1)S(1)} %get-tuple-element.33), channel_id=1, source_target_pairs={{0,48},{16,32},{32,16},{48,0},{1,49},{17,33},{33,17},{49,1},{2,50}... | collective-permute-start | bytes 393224 | tf_op jit(solution)/shard_map/ppermute | solution.py:143
  136.0 3.3 %collective-permute-done.15 = bf16[4,128,128]{2,1,0:T(8,128)(2,1)S(1)} collective-permute-done((bf16[4,128,128]{2,1,0:T(8,128)(2,1)S(1)}, bf16[4,128,128]{2,1,0:T(8,128)(2,1)S(1)}, u32[]{:S(2)}, u32[]{:S(2)}) %collective-permute-start.15) | collective-permute-done | bytes 131104 | tf_op jit(solution)/shard_map/ppermute | solution.py:143
  139.3 1.3 collective-permute-done.14
  140.7 1.3 collective-permute-start.16
  142.0 0.4 collective-permute-start.6
  142.3 1.8 collective-permute-start.8
  144.1 2.6 %collective-permute-start.7 = (bf16[4,128,128]{2,1,0:T(8,128)(2,1)S(1)}, bf16[4,128,128]{2,1,0:T(8,128)(2,1)S(1)}, u32[]{:S(2)}, u32[]{:S(2)}) collective-permute-start(bf16[4,128,128]{2,1,0:T(8,128)(2,1)S(1)} %get-tuple-element.30), channel_id=1, source_target_pairs={{0,12},{4,8},{8,4},{12,0},{1,13},{5,9},{9,5},{13,1},{2,14},{6,10},... | collective-permute-start | bytes 393224 | tf_op jit(solution)/shard_map/ppermute | solution.py:143
  146.8 0.3 collective-permute-done.6
  147.0 1.8 collective-permute-done.8
  148.8 1.5 collective-permute-done.7
  150.4 4.0 %collective-permute-start.19 = (bf16[4,128,128]{2,1,0:T(8,128)(2,1)S(1)}, bf16[4,128,128]{2,1,0:T(8,128)(2,1)S(1)}, u32[]{:S(2)}, u32[]{:S(2)}) collective-permute-start(bf16[4,128,128]{2,1,0:T(8,128)(2,1)S(1)} %fusion.11.a), channel_id=1, source_target_pairs={{0,192},{64,128},{128,64},{192,0},{1,193},{65,129},{129,65},{193,1... | collective-permute-start | bytes 393224 | tf_op jit(solution)/shard_map/ppermute | solution.py:143
  154.5 2.1 %collective-permute-start.18 = (bf16[4,128,128]{2,1,0:T(8,128)(2,1)S(1)}, bf16[4,128,128]{2,1,0:T(8,128)(2,1)S(1)}, u32[]{:S(2)}, u32[]{:S(2)}) collective-permute-start(bf16[4,128,128]{2,1,0:T(8,128)(2,1)S(1)} %fusion.11.a), channel_id=1, source_target_pairs={{0,128},{64,192},{128,0},{192,64},{1,129},{65,193},{129,1},{193,65... | collective-permute-start | bytes 393224 | tf_op jit(solution)/shard_map/ppermute | solution.py:143
  156.6 0.4 collective-permute-start.17
  157.0 4.0 %collective-permute-done.19.d = bf16[4,128,128]{2,1,0:T(8,128)(2,1)S(1)} collective-permute-done((bf16[4,128,128]{2,1,0:T(8,128)(2,1)S(1)}, bf16[4,128,128]{2,1,0:T(8,128)(2,1)S(1)}, u32[]{:S(2)}, u32[]{:S(2)}) %collective-permute-start.19) | collective-permute-done | bytes 131104 | tf_op jit(solution)/shard_map/ppermute | solution.py:143
  161.0 2.6 %collective-permute-done.18.c = bf16[4,128,128]{2,1,0:T(8,128)(2,1)S(1)} collective-permute-done((bf16[4,128,128]{2,1,0:T(8,128)(2,1)S(1)}, bf16[4,128,128]{2,1,0:T(8,128)(2,1)S(1)}, u32[]{:S(2)}, u32[]{:S(2)}) %collective-permute-start.18) | collective-permute-done | bytes 131104 | tf_op jit(solution)/shard_map/ppermute | solution.py:143
  163.6 0.6 collective-permute-done.17.b
  164.3 1.4 collective-permute-start.22
  165.7 1.0 collective-permute-start.21
  166.6 1.8 collective-permute-start.20
  168.5 12.6 %shard_map.69 = bf16[192,8192]{1,0:T(8,128)(2,1)} custom-call(s32[256]{0:T(256)S(1)} %select_reduce_fusion.place, s32[64]{0:T(128)S(1)} %xor.28.blocks, bf16[192,8192]{1,0:T(8,128)(2,1)} %g_ref.3, bf16[256,128,128]{2,1,0:T(8,128)(2,1)} %all-gather.2.cloned.1.call-done.w_ref, bf16[64,192,128]{2,1,0:T(8,128)(2,1)} %shard_map.68.s_ref), custom_call_target="tpu_custom_call" | custom-call | tf_op jit(solution)/shard_map/pallas_call | solution.py:205
  181.1 2.3 %shard_map.74 = f32[16,128,128]{2,1,0:T(8,128)} custom-call(s32[4]{0:T(128)S(1)} %pad_add_fusion.1.where, f32[4,128,128]{2,1,0:T(8,128)S(1)} %shard_map.73.refs_0_, f32[4,128,128]{2,1,0:T(8,128)S(1)} %collective-permute-done.20.refs_1_, f32[4,128,128]{2,1,0:T(8,128)S(1)} %collective-permute-done.21.refs_2_, f32[4,128,128]{2,1,0:T(8,128)S(1)} %collective-permute-done.22.refs_3_), custom_call_target="tpu_custom_call" | custom-call | tf_op jit(solution)/shard_map/pallas_call | solution.py:239
  (42 shorter events, 1.2 us)
Async XLA Ops:
  7.2 60.0 %all-gather.2.cloned.1.call-start = ((), (), s32[]{:S(2)}) async-start(), calls=%async_computation | async-start | bytes 8912896 | tf_op jit(solution)/shard_map/all_gather | solution.py:169
  7.9 73.9 %collective-permute-start = (bf16[192,8192]{1,0:T(8,128)(2,1)}, bf16[192,8192]{1,0:T(8,128)(2,1)}, u32[]{:S(2)}, u32[]{:S(2)}) collective-permute-start(bf16[192,8192]{1,0:T(8,128)(2,1)} %mine_ref.1), channel_id=1, source_target_pairs={{0,1},{1,0},{2,3},{3,2},{4,5},{5,4},{6,7},{7,6},{8,9},{9,8},{10,11... | collective-permute-start | bytes 9437192 | tf_op jit(solution)/shard_map/ppermute | solution.py:143
  81.4 11.7 %collective-permute-start.1 = (bf16[64,192,128]{2,1,0:T(8,128)(2,1)}, bf16[64,192,128]{2,1,0:T(8,128)(2,1)S(1)}, u32[]{:S(2)}, u32[]{:S(2)}) collective-permute-start(bf16[64,192,128]{2,1,0:T(8,128)(2,1)} %shard_map.68.s_ref), channel_id=1, source_target_pairs={{0,1},{1,0},{2,3},{3,2},{4,5},{5,4},{6,7},{7,6},{8,9},{9,8},{10,11... | collective-permute-start | bytes 9437192 | tf_op jit(solution)/shard_map/ppermute | solution.py:143
  81.8 13.0 %copy-start = (s32[256]{0:T(256)S(1)}, s32[256]{0:T(256)}, u32[]{:S(2)}) copy-start(s32[256]{0:T(256)} %rows.3) | copy-start | bytes 3076
  81.8 13.0 %copy-start.1 = (s32[256]{0:T(256)S(1)}, s32[256]{0:T(256)}, u32[]{:S(2)}) copy-start(s32[256]{0:T(256)} %cols.3) | copy-start | bytes 3076
  93.1 1.7 copy-start.2
  102.0 14.6 %collective-permute-start.2 = (bf16[16,128,128]{2,1,0:T(8,128)(2,1)S(1)}, bf16[16,128,128]{2,1,0:T(8,128)(2,1)S(1)}, u32[]{:S(2)}, u32[]{:S(2)}) collective-permute-start(bf16[16,128,128]{2,1,0:T(8,128)(2,1)S(1)} %get-tuple-element.15), channel_id=1, source_target_pairs={{0,16},{16,0},{32,48},{48,32},{1,17},{17,1},{33,49},{49,33},{2,18}... | collective-permute-start | bytes 1572872 | tf_op jit(solution)/shard_map/ppermute | solution.py:143
  103.5 16.6 %collective-permute-start.9 = (bf16[16,128,128]{2,1,0:T(8,128)(2,1)S(1)}, bf16[16,128,128]{2,1,0:T(8,128)(2,1)S(1)}, u32[]{:S(2)}, u32[]{:S(2)}) collective-permute-start(bf16[16,128,128]{2,1,0:T(8,128)(2,1)S(1)} %get-tuple-element.21), channel_id=1, source_target_pairs={{0,4},{4,0},{8,12},{12,8},{1,5},{5,1},{9,13},{13,9},{2,6},{6,2},{1... | collective-permute-start | bytes 1572872 | tf_op jit(solution)/shard_map/ppermute | solution.py:143
  105.0 17.2 %collective-permute-start.4 = (bf16[16,128,128]{2,1,0:T(8,128)(2,1)}, bf16[16,128,128]{2,1,0:T(8,128)(2,1)S(1)}, u32[]{:S(2)}, u32[]{:S(2)}) collective-permute-start(bf16[16,128,128]{2,1,0:T(8,128)(2,1)} %get-tuple-element.18), channel_id=1, source_target_pairs={{0,48},{16,32},{32,16},{48,0},{1,49},{17,33},{33,17},{49,1},{2,50}... | collective-permute-start | bytes 1572872 | tf_op jit(solution)/shard_map/ppermute | solution.py:143
  107.1 16.6 %collective-permute-start.11 = (bf16[16,128,128]{2,1,0:T(8,128)(2,1)S(1)}, bf16[16,128,128]{2,1,0:T(8,128)(2,1)S(1)}, u32[]{:S(2)}, u32[]{:S(2)}) collective-permute-start(bf16[16,128,128]{2,1,0:T(8,128)(2,1)S(1)} %get-tuple-element.24), channel_id=1, source_target_pairs={{0,12},{4,8},{8,4},{12,0},{1,13},{5,9},{9,5},{13,1},{2,14},{6,10},... | collective-permute-start | bytes 1572872 | tf_op jit(solution)/shard_map/ppermute | solution.py:143
  116.6 7.0 %copy-start.5 = (f32[8,128,128]{2,1,0:T(8,128)S(1)}, f32[8,128,128]{2,1,0:T(8,128)}, u32[]{:S(2)}) copy-start(f32[8,128,128]{2,1,0:T(8,128)} %get-tuple-element.25) | copy-start | bytes 1572868
  117.8 17.9 %collective-permute-start.3 = (bf16[8,128,128]{2,1,0:T(8,128)(2,1)S(1)}, bf16[8,128,128]{2,1,0:T(8,128)(2,1)S(1)}, u32[]{:S(2)}, u32[]{:S(2)}) collective-permute-start(bf16[8,128,128]{2,1,0:T(8,128)(2,1)S(1)} %add_convert_fusion.3), channel_id=1, source_target_pairs={{0,48},{16,32},{32,16},{48,0},{1,49},{17,33},{33,17},{49,1},{2,50}... | collective-permute-start | bytes 786440 | tf_op jit(solution)/shard_map/ppermute | solution.py:143
  120.1 8.7 %collective-permute-start.10 = (bf16[8,128,128]{2,1,0:T(8,128)(2,1)S(1)}, bf16[8,128,128]{2,1,0:T(8,128)(2,1)S(1)}, u32[]{:S(2)}, u32[]{:S(2)}) collective-permute-start(bf16[8,128,128]{2,1,0:T(8,128)(2,1)S(1)} %add_convert_fusion.1), channel_id=1, source_target_pairs={{0,12},{4,8},{8,4},{12,0},{1,13},{5,9},{9,5},{13,1},{2,14},{6,10},... | collective-permute-start | bytes 786440 | tf_op jit(solution)/shard_map/ppermute | solution.py:143
  123.3 12.5 %collective-permute-start.5 = (bf16[8,128,128]{2,1,0:T(8,128)(2,1)S(1)}, bf16[8,128,128]{2,1,0:T(8,128)(2,1)S(1)}, u32[]{:S(2)}, u32[]{:S(2)}) collective-permute-start(bf16[8,128,128]{2,1,0:T(8,128)(2,1)S(1)} %add_convert_fusion.2), channel_id=1, source_target_pairs={{0,16},{16,0},{32,48},{48,32},{1,17},{17,1},{33,49},{49,33},{2,18}... | collective-permute-start | bytes 786440 | tf_op jit(solution)/shard_map/ppermute | solution.py:143
  123.7 12.1 %copy-start.4 = (f32[8,128,128]{2,1,0:T(8,128)S(1)}, f32[8,128,128]{2,1,0:T(8,128)}, u32[]{:S(2)}) copy-start(f32[8,128,128]{2,1,0:T(8,128)} %get-tuple-element.14) | copy-start | bytes 1572868
  123.7 7.0 %collective-permute-start.12 = (bf16[8,128,128]{2,1,0:T(8,128)(2,1)S(1)}, bf16[8,128,128]{2,1,0:T(8,128)(2,1)S(1)}, u32[]{:S(2)}, u32[]{:S(2)}) collective-permute-start(bf16[8,128,128]{2,1,0:T(8,128)(2,1)S(1)} %add_convert_fusion), channel_id=1, source_target_pairs={{0,4},{4,0},{8,12},{12,8},{1,5},{5,1},{9,13},{13,9},{2,6},{6,2},{1... | collective-permute-start | bytes 786440 | tf_op jit(solution)/shard_map/ppermute | solution.py:143
  128.9 6.9 %copy-start.3 = (f32[8,128,128]{2,1,0:T(8,128)S(1)}, f32[8,128,128]{2,1,0:T(8,128)}, u32[]{:S(2)}) copy-start(f32[8,128,128]{2,1,0:T(8,128)} %get-tuple-element.17) | copy-start | bytes 1572868
  130.9 5.1 %collective-permute-start.13 = (bf16[4,128,128]{2,1,0:T(8,128)(2,1)S(1)}, bf16[4,128,128]{2,1,0:T(8,128)(2,1)S(1)}, u32[]{:S(2)}, u32[]{:S(2)}) collective-permute-start(bf16[4,128,128]{2,1,0:T(8,128)(2,1)S(1)} %get-tuple-element.31), channel_id=1, source_target_pairs={{0,16},{16,0},{32,48},{48,32},{1,17},{17,1},{33,49},{49,33},{2,18}... | collective-permute-start | bytes 393224 | tf_op jit(solution)/shard_map/ppermute | solution.py:143
  132.7 6.6 %collective-permute-start.15 = (bf16[4,128,128]{2,1,0:T(8,128)(2,1)S(1)}, bf16[4,128,128]{2,1,0:T(8,128)(2,1)S(1)}, u32[]{:S(2)}, u32[]{:S(2)}) collective-permute-start(bf16[4,128,128]{2,1,0:T(8,128)(2,1)S(1)} %get-tuple-element.32), channel_id=1, source_target_pairs={{0,32},{16,48},{32,0},{48,16},{1,33},{17,49},{33,1},{49,17},{2,34}... | collective-permute-start | bytes 393224 | tf_op jit(solution)/shard_map/ppermute | solution.py:143
  133.5 7.1 %collective-permute-start.14 = (bf16[4,128,128]{2,1,0:T(8,128)(2,1)S(1)}, bf16[4,128,128]{2,1,0:T(8,128)(2,1)S(1)}, u32[]{:S(2)}, u32[]{:S(2)}) collective-permute-start(bf16[4,128,128]{2,1,0:T(8,128)(2,1)S(1)} %get-tuple-element.33), channel_id=1, source_target_pairs={{0,48},{16,32},{32,16},{48,0},{1,49},{17,33},{33,17},{49,1},{2,50}... | collective-permute-start | bytes 393224 | tf_op jit(solution)/shard_map/ppermute | solution.py:143
  140.7 9.7 %collective-permute-start.16 = (f32[4,128,128]{2,1,0:T(8,128)S(1)}, f32[4,128,128]{2,1,0:T(8,128)S(1)}, u32[]{:S(2)}, u32[]{:S(2)}) collective-permute-start(f32[4,128,128]{2,1,0:T(8,128)S(1)} %fusion.5), channel_id=1, source_target_pairs={{0,2},{2,0},{1,3},{3,1},{4,6},{6,4},{5,7},{7,5},{8,10},{10,8},{9,1... | collective-permute-start | bytes 786440 | tf_op jit(solution)/shard_map/ppermute | solution.py:143
  142.0 5.1 %collective-permute-start.6 = (bf16[4,128,128]{2,1,0:T(8,128)(2,1)S(1)}, bf16[4,128,128]{2,1,0:T(8,128)(2,1)S(1)}, u32[]{:S(2)}, u32[]{:S(2)}) collective-permute-start(bf16[4,128,128]{2,1,0:T(8,128)(2,1)S(1)} %get-tuple-element.28), channel_id=1, source_target_pairs={{0,4},{4,0},{8,12},{12,8},{1,5},{5,1},{9,13},{13,9},{2,6},{6,2},{1... | collective-permute-start | bytes 393224 | tf_op jit(solution)/shard_map/ppermute | solution.py:143
  142.3 6.5 %collective-permute-start.8 = (bf16[4,128,128]{2,1,0:T(8,128)(2,1)S(1)}, bf16[4,128,128]{2,1,0:T(8,128)(2,1)S(1)}, u32[]{:S(2)}, u32[]{:S(2)}) collective-permute-start(bf16[4,128,128]{2,1,0:T(8,128)(2,1)S(1)} %get-tuple-element.29), channel_id=1, source_target_pairs={{0,8},{4,12},{8,0},{12,4},{1,9},{5,13},{9,1},{13,5},{2,10},{6,14},... | collective-permute-start | bytes 393224 | tf_op jit(solution)/shard_map/ppermute | solution.py:143
  144.1 6.2 %collective-permute-start.7 = (bf16[4,128,128]{2,1,0:T(8,128)(2,1)S(1)}, bf16[4,128,128]{2,1,0:T(8,128)(2,1)S(1)}, u32[]{:S(2)}, u32[]{:S(2)}) collective-permute-start(bf16[4,128,128]{2,1,0:T(8,128)(2,1)S(1)} %get-tuple-element.30), channel_id=1, source_target_pairs={{0,12},{4,8},{8,4},{12,0},{1,13},{5,9},{9,5},{13,1},{2,14},{6,10},... | collective-permute-start | bytes 393224 | tf_op jit(solution)/shard_map/ppermute | solution.py:143
  150.4 10.6 %collective-permute-start.19 = (bf16[4,128,128]{2,1,0:T(8,128)(2,1)S(1)}, bf16[4,128,128]{2,1,0:T(8,128)(2,1)S(1)}, u32[]{:S(2)}, u32[]{:S(2)}) collective-permute-start(bf16[4,128,128]{2,1,0:T(8,128)(2,1)S(1)} %fusion.11.a), channel_id=1, source_target_pairs={{0,192},{64,128},{128,64},{192,0},{1,193},{65,129},{129,65},{193,1... | collective-permute-start | bytes 393224 | tf_op jit(solution)/shard_map/ppermute | solution.py:143
  154.5 9.1 %collective-permute-start.18 = (bf16[4,128,128]{2,1,0:T(8,128)(2,1)S(1)}, bf16[4,128,128]{2,1,0:T(8,128)(2,1)S(1)}, u32[]{:S(2)}, u32[]{:S(2)}) collective-permute-start(bf16[4,128,128]{2,1,0:T(8,128)(2,1)S(1)} %fusion.11.a), channel_id=1, source_target_pairs={{0,128},{64,192},{128,0},{192,64},{1,129},{65,193},{129,1},{193,65... | collective-permute-start | bytes 393224 | tf_op jit(solution)/shard_map/ppermute | solution.py:143
  156.6 7.6 %collective-permute-start.17 = (bf16[4,128,128]{2,1,0:T(8,128)(2,1)S(1)}, bf16[4,128,128]{2,1,0:T(8,128)(2,1)S(1)}, u32[]{:S(2)}, u32[]{:S(2)}) collective-permute-start(bf16[4,128,128]{2,1,0:T(8,128)(2,1)S(1)} %fusion.11.a), channel_id=1, source_target_pairs={{0,64},{64,0},{128,192},{192,128},{1,65},{65,1},{129,193},{193,129... | collective-permute-start | bytes 393224 | tf_op jit(solution)/shard_map/ppermute | solution.py:143
  164.3 16.8 %collective-permute-start.22 = (f32[4,128,128]{2,1,0:T(8,128)S(1)}, f32[4,128,128]{2,1,0:T(8,128)S(1)}, u32[]{:S(2)}, u32[]{:S(2)}) collective-permute-start(f32[4,128,128]{2,1,0:T(8,128)S(1)} %shard_map.73.refs_0_), channel_id=1, source_target_pairs={{0,48},{16,32},{32,16},{48,0},{1,49},{17,33},{33,17},{49,1},{2,50}... | collective-permute-start | bytes 786440 | tf_op jit(solution)/shard_map/ppermute | solution.py:143
  165.7 15.5 %collective-permute-start.21 = (f32[4,128,128]{2,1,0:T(8,128)S(1)}, f32[4,128,128]{2,1,0:T(8,128)S(1)}, u32[]{:S(2)}, u32[]{:S(2)}) collective-permute-start(f32[4,128,128]{2,1,0:T(8,128)S(1)} %shard_map.73.refs_0_), channel_id=1, source_target_pairs={{0,32},{16,48},{32,0},{48,16},{1,33},{17,49},{33,1},{49,17},{2,34}... | collective-permute-start | bytes 786440 | tf_op jit(solution)/shard_map/ppermute | solution.py:143
  166.6 14.5 %collective-permute-start.20 = (f32[4,128,128]{2,1,0:T(8,128)S(1)}, f32[4,128,128]{2,1,0:T(8,128)S(1)}, u32[]{:S(2)}, u32[]{:S(2)}) collective-permute-start(f32[4,128,128]{2,1,0:T(8,128)S(1)} %shard_map.73.refs_0_), channel_id=1, source_target_pairs={{0,16},{16,0},{32,48},{48,32},{1,17},{17,1},{33,49},{49,33},{2,18}... | collective-permute-start | bytes 786440 | tf_op jit(solution)/shard_map/ppermute | solution.py:143
Sparse Core Ops, SparseCore 0:
  9.8 57.2 all-gather.1

commit v2 on v1

--- a/solution.py
+++ b/solution.py
@@ -14,14 +14,25 @@
 SIDE = 128
 ROOT = math.sqrt(2.0 / math.pi)
 CUBIC = 0.044715
+UNROLL = 2
 
 VMEM = pl.BlockSpec(memory_space=pltpu.VMEM)
 SMEM = pl.BlockSpec(memory_space=pltpu.SMEM)
-PARAMS = pltpu.CompilerParams(vmem_limit_bytes=52 * 1024 * 1024)
+ANY = pl.BlockSpec(memory_space=pl.ANY)
+Z = ("zh", "zl")
+PARAMS = pltpu.CompilerParams(vmem_limit_bytes=8 * 1024 * 1024)
 
 
 def shape(dims, dtype):
     return jax.ShapeDtypeStruct(dims, dtype)
+
+
+def near(value):
+    return pltpu.with_memory_space_constraint(value, pltpu.VMEM)
+
+
+def stored(value):
+    return pltpu.with_memory_space_constraint(value, pltpu.HBM)
 
 
 def lanes(block):
@@ -37,8 +48,39 @@
     return cotangent * slope
 
 
-def forward_kernel(place, blocks, x_ref, g_ref, w_ref, s_ref):
-    def one(group, carry):
+PIECES = tuple(
+    (x, zl, core, first, size)
+    for core in (0, 1)
+    for x, zl, first, size in (
+        (0, 0, 0, 16),
+        (3, 0, 0, 16),
+        (1, 0, 0, 16),
+        (0, 1, 0, 16),
+        (3, 1, 0, 16),
+        (1, 1, 0, 16),
+        (2, 0, 0, 16),
+        (2, 1, 0, 8),
+        (2, 1, 8, 8),
+    )
+)
+
+
+def forward_kernel(where, place, blocks, x_ref, g_ref, *refs):
+    pieces, (s_ref, w_ref, sems) = refs[: len(PIECES)], refs[len(PIECES) :]
+    copies = []
+    for i, (x, zl, core, first, size) in enumerate(PIECES):
+        owner = (lax.rem(where[0] + x, 4) * 2 + (where[2] ^ zl)) * 2 + (where[3] ^ core)
+        copies.append(
+            pltpu.make_async_copy(
+                pieces[i], w_ref.at[pl.ds(owner * 16 + first, size)], sems.at[i]
+            )
+        )
+    for copy in copies:
+        copy.start()
+    for copy in copies:
+        copy.wait()
+
+    def one(group):
         ids = [blocks[group * 4 + m] for m in range(4)]
         x = jnp.concatenate([x_ref[:, lanes(b)] for b in ids], axis=1)
         for first in (0, 2):
@@ -55,9 +97,13 @@
                 cot = g_ref[:, lanes(ids[n])].astype(jnp.float32)
                 out = slope_times(pre[:, k * SIDE : (k + 1) * SIDE], cot)
                 s_ref[ids[n]] = out.astype(jnp.bfloat16)
+
+    def some(step, carry):
+        for k in range(UNROLL):
+            one(step * UNROLL + k)
         return carry
 
-    lax.fori_loop(0, 16, one, 0)
+    lax.fori_loop(0, 16 // UNROLL, some, 0)
 
 
 def backward_kernel(place, blocks, g_ref, w_ref, s_ref, o_ref):
@@ -143,6 +189,12 @@
     return lax.ppermute(value, axis, [(i, i ^ mask) for i in range(size)])
 
 
+def turn(value, axes, by):
+    names = axes if isinstance(axes, tuple) else (axes,)
+    size = math.prod(SIZES[AXES.index(name)] for name in names)
+    return lax.ppermute(value, axes, [(i, (i + by) % size) for i in range(size)])
+
+
 def tables(tile_row, tile_column):
     differ = tile_row ^ tile_column
     both = lax.reduce(differ, jnp.int32(0), lax.bitwise_or, (0,))
@@ -166,25 +218,39 @@
     tile_column = tile_column.astype(jnp.int32)
     rows_here = features.shape[0]
     where = jnp.stack([lax.axis_index(a) for a in ("x", "y", "zl", "core")]).astype(jnp.int32)
-    whole = lax.all_gather(weight_tiles, ("x", "zl", "core"), axis=0, tiled=True)
+    place, blocks = tables(tile_row, tile_column)
+    own = weight_tiles
+    left, right = turn(own, "x", 1), turn(own, "x", 3)
+    beside = swap(own, "zl", 1)
     others = swap(features, "core", 1)
+    far = turn(left, "x", 1)
+    beside_left, beside_right = turn(left, Z, 1), turn(right, Z, 7)
+    features_near, grad_out = near(features), near(grad_out)
+    beside_far = (turn(far[:8], Z, 1), turn(far[8:], Z, 7))
+    mine = (own, left, right, beside, beside_left, beside_right, far, *beside_far)
+    pieces = (*mine, *(swap(piece, "core", 1) for piece in mine))
+    pieces = [stored(piece) for piece in pieces]
+    slopes, whole = pl.pallas_call(
+        forward_kernel,
+        out_shape=[
+            pltpu.VMEM((64, rows_here, SIDE), bf16),
+            pltpu.VMEM((256, SIDE, SIDE), bf16),
+        ],
+        in_specs=[SMEM] * 3 + [VMEM] * 2 + [ANY] * len(pieces),
+        out_specs=[VMEM, VMEM],
+        scratch_shapes=[pltpu.SemaphoreType.DMA((len(pieces),))],
+        compiler_params=PARAMS,
+    )(where, place, blocks, features_near, grad_out, *pieces)
+    slopes, others = lax.optimization_barrier((slopes, others))
+    other_slopes = swap(slopes, "core", 1)
     xt = pl.pallas_call(
         transpose_kernel,
-        out_shape=shape((64, SIDE, 2 * rows_here), bf16),
+        out_shape=pltpu.VMEM((64, SIDE, 2 * rows_here), bf16),
         in_specs=[VMEM, VMEM],
         out_specs=VMEM,
         compiler_params=PARAMS,
-    )(features, others)
-    place, blocks = tables(tile_row, tile_column)
-    slopes = pl.pallas_call(
-        forward_kernel,
-        out_shape=shape((64, rows_here, SIDE), bf16),
-        in_specs=[SMEM, SMEM, VMEM, VMEM, VMEM],
-        out_specs=VMEM,
-        compiler_params=PARAMS,
-    )(place, blocks, features, grad_out, whole)
-    other_slopes = swap(slopes, "core", 1)
-    operands = (tile_row, tile_column, where, xt, slopes, other_slopes)
+    )(features_near, near(others))
+    operands = (tile_row, tile_column, where, near(xt), near(slopes), near(other_slopes))
     sent = pl.pallas_call(
         functools.partial(partial_kernel, SENT, False),
         out_shape=[shape((16, SIDE, SIDE), bf16)] * 4,
@@ -208,7 +274,7 @@
         in_specs=[SMEM, SMEM, VMEM, VMEM, VMEM],
         out_specs=VMEM,
         compiler_params=PARAMS,
-    )(place, blocks, grad_out, whole, slopes)
+    )(place, blocks, grad_out, near(whole), near(slopes))
 
     second = [
         swap((kept[2 * i + 1] + got[i][8:].astype(f32)).astype(bf16), axis, (3, 1)[half])
@@ -217,16 +283,17 @@
     held = [
         kept[2 * i] + got[i][:8].astype(f32) + second[i].astype(f32) for i in range(4)
     ]
-    pieces = []
-    for i, axis in ((0, "y"), (2, "x")):
-        both = jnp.concatenate(
+    rest = [
+        jnp.concatenate(
             [held[i].reshape(4, 2, SIDE, SIDE), held[i + 1].reshape(4, 2, SIDE, SIDE)], axis=1
         )
-        away = [swap(both[r].astype(bf16), axis, r) for r in (1, 3, 2)]
-        pieces.append(
-            both[0] + (away[0].astype(f32) + away[1].astype(f32)) + away[2].astype(f32)
-        )
-    mine = (pieces[1] + swap(pieces[0], "zl", 1)).astype(bf16)
+        for i in (0, 2)
+    ]
+    away = [swap(rest[0][r].astype(bf16), "y", r) for r in (1, 2, 3)]
+    away += [swap(rest[1][r].astype(bf16), "x", r) for r in (1, 2, 3)]
+    away = [piece.astype(f32) for piece in lax.optimization_barrier(away)]
+    sums = [rest[i][0] + (away[3 * i] + away[3 * i + 2]) + away[3 * i + 1] for i in (0, 1)]
+    mine = (sums[1] + swap(sums[0], "zl", 1)).astype(bf16)
     across = [swap(mine, "zh", r) for r in (1, 2, 3)]
     summed = pl.pallas_call(
         sum_four_kernel,

time: 192 us -> 155 us (0.81)
  Pallas kernels: 55.7 us -> 30.9 us
  between operations: 16.1 us -> 2.8 us
  starting transfers between devices: 34.2 us -> 47.3 us
  waiting for transfers between devices: 76.4 us -> 64 us
  local copies, waits for them, and re-layouts: 1.83 us -> 6.28 us
  other arithmetic: 6.03 us -> 3.84 us
    all_gather x1 -> x0, waiting for transfers between devices: 54.1 us -> none  [on_device(): lax.all_gather(weight_tiles, ('x', 'zl', 'core'), axis=0, tiled=True)]
    ppermute x0 -> x7, waiting for transfers between devices: none -> 31.9 us  [turn(): lax.ppermute(value, axes, [(i, (i + by) % size) for i in range(size)])]
    ppermute x23 -> x33, waiting for transfers between devices: 21.6 us -> 32.1 us  [swap(): return lax.ppermute(value, axis, [(i, i ^ mask) for i in range(size)])]
    pallas_call x2, Pallas kernels: 25.6 us -> 15.7 us  [the longest x1 9.96 us: on_device(): pl.pallas_call(forward_kernel, out_shape=[pltpu.VMEM((64, rows_here, SIDE...]
    ppermute x0 -> x7, starting transfers between devices: none -> 9.06 us  [turn(): lax.ppermute(value, axes, [(i, (i + by) % size) for i in range(size)])]
    pallas_call x1, Pallas kernels: 7.75 us -> 2.38 us  [on_device(): pl.pallas_call(functools.partial(partial_kernel, KEPT, True), out_shape=[...]
    pallas_call x1, Pallas kernels: 7.28 us -> 2.39 us  [on_device(): pl.pallas_call(functools.partial(partial_kernel, SENT, False), out_shape=...]
    pallas_call x1, Pallas kernels: 12.6 us -> 8.02 us  [on_device(): pl.pallas_call(backward_kernel, out_shape=shape(features.shape, bf16), in...]
  transfers between devices with their start and end apart: 24 -> 40, of which waited for: 11 -> 19; matrix products, arithmetic and copies ran while one was open for 3% -> 3% of each run, Pallas kernels for 24% -> 17%
where the time goes in v2:
time: 155 us
  waiting for transfers between devices  64 us (41%)
  starting transfers between devices  47.3 us (31%)
  Pallas kernels  30.9 us (20%)
  local copies, waits for them, and re-layouts  6.28 us (4%)
  other arithmetic  3.84 us (2%)
  between operations  2.8 us (2%)
    ppermute x33, starting transfers between devices, swap(): return lax.ppermute(value, axis, [(i, i ^ mask) for i in range(size)])  38.2 us
    ppermute x33, waiting for transfers between devices, swap(): return lax.ppermute(value, axis, [(i, i ^ mask) for i in range(size)])  32.1 us
    ppermute x7, waiting for transfers between devices, turn(): lax.ppermute(value, axes, [(i, (i + by) % size) for i in range(size)])  31.9 us
    pallas_call x1, Pallas kernels, on_device(): pl.pallas_call(forward_kernel, out_shape=[pltpu.VMEM((64, rows_here, SIDE...  9.96 us
    ppermute x7, starting transfers between devices, turn(): lax.ppermute(value, axes, [(i, (i + by) % size) for i in range(size)])  9.06 us
    pallas_call x1, Pallas kernels, on_device(): pl.pallas_call(backward_kernel, out_shape=shape(features.shape, bf16), in...  8.02 us
    pallas_call x1, Pallas kernels, on_device(): pl.pallas_call(transpose_kernel, out_shape=pltpu.VMEM((64, SIDE, 2 * rows...  5.76 us
    unnamed x24, local copies, waits for them, and re-layouts  5.3 us
  transfers between devices with their start and end apart: 40, of which 19 were waited for; matrix products, arithmetic and copies ran while one was open for 3% of the time, Pallas kernels for 17%

profile of v2, /device:TPU:32, one launch (start us, length us, event | category | flops | bytes accessed | tf_op | source)
XLA Modules:
  0.0 155.1 jit_solution(12638583224543626013)
XLA Ops:
  0.7 1.6 %collective-permute-start = (bf16[16,128,128]{2,1,0:T(8,128)(2,1)}, bf16[16,128,128]{2,1,0:T(8,128)(2,1)S(1)}, u32[]{:S(2)}, u32[]{:S(2)}) collective-permute-start(bf16[16,128,128]{2,1,0:T(8,128)(2,1)} %refs_0_.1), channel_id=1, source_target_pairs={{0,4},{4,8},{8,12},{12,0},{1,5},{5,9},{9,13},{13,1},{2,6},{6,10},{... | collective-permute-start | bytes 1572872 | tf_op jit(solution)/shard_map/ppermute | solution.py:195
  2.3 1.7 %collective-permute-start.1 = (bf16[16,128,128]{2,1,0:T(8,128)(2,1)}, bf16[16,128,128]{2,1,0:T(8,128)(2,1)}, u32[]{:S(2)}, u32[]{:S(2)}) collective-permute-start(bf16[16,128,128]{2,1,0:T(8,128)(2,1)} %refs_0_.1), channel_id=1, source_target_pairs={{0,12},{4,0},{8,4},{12,8},{1,13},{5,1},{9,5},{13,9},{2,14},{6,2},{... | collective-permute-start | bytes 1572872 | tf_op jit(solution)/shard_map/ppermute | solution.py:195
  4.0 1.8 %collective-permute-start.2 = (bf16[16,128,128]{2,1,0:T(8,128)(2,1)}, bf16[16,128,128]{2,1,0:T(8,128)(2,1)}, u32[]{:S(2)}, u32[]{:S(2)}) collective-permute-start(bf16[16,128,128]{2,1,0:T(8,128)(2,1)} %refs_0_.1), channel_id=1, source_target_pairs={{0,2},{2,0},{1,3},{3,1},{4,6},{6,4},{5,7},{7,5},{8,10},{10,8},{9,1... | collective-permute-start | bytes 1572872 | tf_op jit(solution)/shard_map/ppermute | solution.py:189
  5.9 10.6 %collective-permute-done.refs_1_ = bf16[16,128,128]{2,1,0:T(8,128)(2,1)S(1)} collective-permute-done((bf16[16,128,128]{2,1,0:T(8,128)(2,1)}, bf16[16,128,128]{2,1,0:T(8,128)(2,1)S(1)}, u32[]{:S(2)}, u32[]{:S(2)}) %collective-permute-start) | collective-permute-done | bytes 524320 | tf_op jit(solution)/shard_map/ppermute | solution.py:195
  16.5 1.9 %collective-permute-start.3 = (bf16[16,128,128]{2,1,0:T(8,128)(2,1)S(1)}, bf16[16,128,128]{2,1,0:T(8,128)(2,1)}, u32[]{:S(2)}, u32[]{:S(2)}) collective-permute-start(bf16[16,128,128]{2,1,0:T(8,128)(2,1)S(1)} %collective-permute-done.refs_1_), channel_id=1, source_target_pairs={{0,2},{2,64},{64,66},{66,128},{128,130},{130,192},{192,194},{194,0... | collective-permute-start | bytes 1572872 | tf_op jit(solution)/shard_map/ppermute | solution.py:195
  18.7 1.2 collective-permute-start.4
  19.9 10.2 %collective-permute-done.3.refs_4_ = bf16[16,128,128]{2,1,0:T(8,128)(2,1)} collective-permute-done((bf16[16,128,128]{2,1,0:T(8,128)(2,1)S(1)}, bf16[16,128,128]{2,1,0:T(8,128)(2,1)}, u32[]{:S(2)}, u32[]{:S(2)}) %collective-permute-start.3) | collective-permute-done | bytes 524320 | tf_op jit(solution)/shard_map/ppermute | solution.py:195
  30.2 2.6 %collective-permute-done.5.refs_6_ = bf16[16,128,128]{2,1,0:T(8,128)(2,1)S(1)} collective-permute-done((bf16[16,128,128]{2,1,0:T(8,128)(2,1)S(1)}, bf16[16,128,128]{2,1,0:T(8,128)(2,1)S(1)}, u32[]{:S(2)}, u32[]{:S(2)}) %collective-permute-start.5) | collective-permute-done | bytes 524320 | tf_op jit(solution)/shard_map/ppermute | solution.py:195
  32.8 0.8 copy-done.6
  33.6 0.8 fusion.15
  34.5 2.0 %collective-permute-start.6 = (bf16[8,128,128]{2,1,0:T(8,128)(2,1)}, bf16[8,128,128]{2,1,0:T(8,128)(2,1)S(1)}, u32[]{:S(2)}, u32[]{:S(2)}) collective-permute-start(bf16[8,128,128]{2,1,0:T(8,128)(2,1)} %get-tuple-element.55), channel_id=1, source_target_pairs={{0,2},{2,64},{64,66},{66,128},{128,130},{130,192},{192,194},{194,0... | collective-permute-start | bytes 786440 | tf_op jit(solution)/shard_map/ppermute | solution.py:195
  36.6 0.7 copy-done.10
  37.3 1.3 fusion.14
  40.8 0.7 pad_add_fusion
  41.8 1.4 collective-permute-done.6.refs_7_
  43.3 7.0 %collective-permute-done.7.refs_8_ = bf16[8,128,128]{2,1,0:T(8,128)(2,1)} collective-permute-done((bf16[8,128,128]{2,1,0:T(8,128)(2,1)}, bf16[8,128,128]{2,1,0:T(8,128)(2,1)}, u32[]{:S(2)}, u32[]{:S(2)}) %collective-permute-start.7) | collective-permute-done | bytes 262176 | tf_op jit(solution)/shard_map/ppermute | solution.py:195
  50.8 0.7 fusion.13
  52.5 1.9 %copy-done = bf16[192,8192]{1,0:T(8,128)(2,1)S(1)} copy-done((bf16[192,8192]{1,0:T(8,128)(2,1)S(1)}, bf16[192,8192]{1,0:T(8,128)(2,1)}, u32[]{:S(2)}) %copy-start) | copy-done | bytes 3145752
  54.4 1.9 %copy-done.2 = bf16[192,8192]{1,0:T(8,128)(2,1)S(1)} copy-done((bf16[192,8192]{1,0:T(8,128)(2,1)S(1)}, bf16[192,8192]{1,0:T(8,128)(2,1)}, u32[]{:S(2)}) %copy-start.2) | copy-done | bytes 3145752
  56.3 10.0 %shard_map.68 = (bf16[64,192,128]{2,1,0:T(8,128)(2,1)S(1)}, bf16[256,128,128]{2,1,0:T(8,128)(2,1)S(1)}) custom-call(s32[4]{0:T(128)S(1)} %pad_add_fusion.1.where, s32[256]{0:T(256)S(1)} %select_reduce_fusion.place, s32[64]{0:T(128)S(1)} %xor.28.blocks, bf16[192,8192]{1,0:T(8,128)(2,1)S(1)} %copy-done, bf16[192,8192]{1,0:T(8,128)(2,1)S(1)} %copy-done.2, ...), custom_call_target="tpu_custom_call" | custom-call | tf_op jit(solution)/shard_map/pallas_call | solution.py:233
  66.6 5.8 %shard_map.70.xt_ref = bf16[64,128,384]{2,1,0:T(8,128)(2,1)S(1)} custom-call(bf16[192,8192]{1,0:T(8,128)(2,1)S(1)} %copy-done.1, bf16[192,8192]{1,0:T(8,128)(2,1)S(1)} %collective-permute-done.17.other_ref), custom_call_target="tpu_custom_call" | custom-call | tf_op jit(solution)/shard_map/pallas_call | solution.py:246
  72.4 2.4 %shard_map.72 = (bf16[16,128,128]{2,1,0:T(8,128)(2,1)S(1)}, bf16[16,128,128]{2,1,0:T(8,128)(2,1)S(1)}, bf16[16,128,128]{2,1,0:T(8,128)(2,1)S(1)}, bf16[16,128,128]{2,1,0:T(8,128)(2,1)S(1)}) custom-call(s32[256]{0:T(256)S(1)} %copy-done.4, s32[256]{0:T(256)S(1)} %copy-done.5, s32[4]{0:T(128)S(1)} %pad_add_fusion.1.where, ...), custom_call_target="tpu_custom_call" | custom-call | tf_op jit(solution)/shard_map/pallas_call | solution.py:254
  75.0 1.8 %collective-permute-start.25 = (bf16[16,128,128]{2,1,0:T(8,128)(2,1)S(1)}, bf16[16,128,128]{2,1,0:T(8,128)(2,1)S(1)}, u32[]{:S(2)}, u32[]{:S(2)}) collective-permute-start(bf16[16,128,128]{2,1,0:T(8,128)(2,1)S(1)} %get-tuple-element.38), channel_id=1, source_target_pairs={{0,12},{4,8},{8,4},{12,0},{1,13},{5,9},{9,5},{13,1},{2,14},{6,10},... | collective-permute-start | bytes 1572872 | tf_op jit(solution)/shard_map/ppermute | solution.py:189
  76.8 3.0 %collective-permute-start.21 = (bf16[16,128,128]{2,1,0:T(8,128)(2,1)S(1)}, bf16[16,128,128]{2,1,0:T(8,128)(2,1)S(1)}, u32[]{:S(2)}, u32[]{:S(2)}) collective-permute-start(bf16[16,128,128]{2,1,0:T(8,128)(2,1)S(1)} %get-tuple-element.32), channel_id=1, source_target_pairs={{0,48},{16,32},{32,16},{48,0},{1,49},{17,33},{33,17},{49,1},{2,50}... | collective-permute-start | bytes 1572872 | tf_op jit(solution)/shard_map/ppermute | solution.py:189
  79.9 2.4 %shard_map.71 = (f32[8,128,128]{2,1,0:T(8,128)S(1)}, f32[8,128,128]{2,1,0:T(8,128)S(1)}, f32[8,128,128]{2,1,0:T(8,128)S(1)}, f32[8,128,128]{2,1,0:T(8,128)S(1)},...) custom-call(s32[256]{0:T(256)S(1)} %copy-done.4, ...), custom_call_target="tpu_custom_call" | custom-call | tf_op jit(solution)/shard_map/pallas_call | solution.py:264
  82.3 6.8 %collective-permute-done.23 = bf16[16,128,128]{2,1,0:T(8,128)(2,1)S(1)} collective-permute-done((bf16[16,128,128]{2,1,0:T(8,128)(2,1)S(1)}, bf16[16,128,128]{2,1,0:T(8,128)(2,1)S(1)}, u32[]{:S(2)}, u32[]{:S(2)}) %collective-permute-start.23) | collective-permute-done | bytes 524320 | tf_op jit(solution)/shard_map/ppermute | solution.py:189
  89.1 1.5 collective-permute-start.24
  91.0 0.7 collective-permute-done.21
  91.7 1.0 collective-permute-start.22
  93.2 1.8 %collective-permute-start.20 = (bf16[8,128,128]{2,1,0:T(8,128)(2,1)S(1)}, bf16[8,128,128]{2,1,0:T(8,128)(2,1)S(1)}, u32[]{:S(2)}, u32[]{:S(2)}) collective-permute-start(bf16[8,128,128]{2,1,0:T(8,128)(2,1)S(1)} %add_convert_fusion.3), channel_id=1, source_target_pairs={{0,48},{16,32},{32,16},{48,0},{1,49},{17,33},{33,17},{49,1},{2,50}... | collective-permute-start | bytes 786440 | tf_op jit(solution)/shard_map/ppermute | solution.py:189
  95.0 3.2 %collective-permute-done.24 = bf16[8,128,128]{2,1,0:T(8,128)(2,1)S(1)} collective-permute-done((bf16[8,128,128]{2,1,0:T(8,128)(2,1)S(1)}, bf16[8,128,128]{2,1,0:T(8,128)(2,1)S(1)}, u32[]{:S(2)}, u32[]{:S(2)}) %collective-permute-start.24) | collective-permute-done | bytes 262176 | tf_op jit(solution)/shard_map/ppermute | solution.py:189
  98.5 1.7 %collective-permute-start.27 = (bf16[4,128,128]{2,1,0:T(8,128)(2,1)S(1)}, bf16[4,128,128]{2,1,0:T(8,128)(2,1)S(1)}, u32[]{:S(2)}, u32[]{:S(2)}) collective-permute-start(bf16[4,128,128]{2,1,0:T(8,128)(2,1)S(1)} %get-tuple-element.53), channel_id=1, source_target_pairs={{0,16},{16,0},{32,48},{48,32},{1,17},{17,1},{33,49},{49,33},{2,18}... | collective-permute-start | bytes 393224 | tf_op jit(solution)/shard_map/ppermute | solution.py:189
  100.2 2.9 %collective-permute-start.28 = (bf16[4,128,128]{2,1,0:T(8,128)(2,1)S(1)}, bf16[4,128,128]{2,1,0:T(8,128)(2,1)S(1)}, u32[]{:S(2)}, u32[]{:S(2)}) collective-permute-start(bf16[4,128,128]{2,1,0:T(8,128)(2,1)S(1)} %get-tuple-element.52), channel_id=1, source_target_pairs={{0,32},{16,48},{32,0},{48,16},{1,33},{17,49},{33,1},{49,17},{2,34}... | collective-permute-start | bytes 393224 | tf_op jit(solution)/shard_map/ppermute | solution.py:189
  104.2 3.0 %collective-permute-start.31 = (bf16[4,128,128]{2,1,0:T(8,128)(2,1)S(1)}, bf16[4,128,128]{2,1,0:T(8,128)(2,1)S(1)}, u32[]{:S(2)}, u32[]{:S(2)}) collective-permute-start(bf16[4,128,128]{2,1,0:T(8,128)(2,1)S(1)} %get-tuple-element.49), channel_id=1, source_target_pairs={{0,8},{4,12},{8,0},{12,4},{1,9},{5,13},{9,1},{13,5},{2,10},{6,14},... | collective-permute-start | bytes 393224 | tf_op jit(solution)/shard_map/ppermute | solution.py:189
  107.1 1.5 collective-permute-start.32
  108.6 0.8 collective-permute-done.29
  109.4 2.1 %collective-permute-done.31 = bf16[4,128,128]{2,1,0:T(8,128)(2,1)S(1)} collective-permute-done((bf16[4,128,128]{2,1,0:T(8,128)(2,1)S(1)}, bf16[4,128,128]{2,1,0:T(8,128)(2,1)S(1)}, u32[]{:S(2)}, u32[]{:S(2)}) %collective-permute-start.31) | collective-permute-done | bytes 131104 | tf_op jit(solution)/shard_map/ppermute | solution.py:189
  111.5 1.8 %collective-permute-done.32 = bf16[4,128,128]{2,1,0:T(8,128)(2,1)S(1)} collective-permute-done((bf16[4,128,128]{2,1,0:T(8,128)(2,1)S(1)}, bf16[4,128,128]{2,1,0:T(8,128)(2,1)S(1)}, u32[]{:S(2)}, u32[]{:S(2)}) %collective-permute-start.32) | collective-permute-done | bytes 131104 | tf_op jit(solution)/shard_map/ppermute | solution.py:189
  113.5 6.8 %collective-permute-done.33 = f32[4,128,128]{2,1,0:T(8,128)S(1)} collective-permute-done((f32[4,128,128]{2,1,0:T(8,128)S(1)}, f32[4,128,128]{2,1,0:T(8,128)S(1)}, u32[]{:S(2)}, u32[]{:S(2)}) %collective-permute-start.33) | collective-permute-done | bytes 262176 | tf_op jit(solution)/shard_map/ppermute | solution.py:189
  120.4 6.7 %collective-permute-start.34 = (bf16[4,128,128]{2,1,0:T(8,128)(2,1)S(1)}, bf16[4,128,128]{2,1,0:T(8,128)(2,1)S(1)}, u32[]{:S(2)}, u32[]{:S(2)}) collective-permute-start(bf16[4,128,128]{2,1,0:T(8,128)(2,1)S(1)} %fusion.11.a), channel_id=1, source_target_pairs={{0,64},{64,0},{128,192},{192,128},{1,65},{65,1},{129,193},{193,129... | collective-permute-start | bytes 393224 | tf_op jit(solution)/shard_map/ppermute | solution.py:189
  127.2 3.6 %collective-permute-start.36 = (bf16[4,128,128]{2,1,0:T(8,128)(2,1)S(1)}, bf16[4,128,128]{2,1,0:T(8,128)(2,1)S(1)}, u32[]{:S(2)}, u32[]{:S(2)}) collective-permute-start(bf16[4,128,128]{2,1,0:T(8,128)(2,1)S(1)} %fusion.11.a), channel_id=1, source_target_pairs={{0,192},{64,128},{128,64},{192,0},{1,193},{65,129},{129,65},{193,1... | collective-permute-start | bytes 393224 | tf_op jit(solution)/shard_map/ppermute | solution.py:189
  130.7 3.0 %collective-permute-done.34.b = bf16[4,128,128]{2,1,0:T(8,128)(2,1)S(1)} collective-permute-done((bf16[4,128,128]{2,1,0:T(8,128)(2,1)S(1)}, bf16[4,128,128]{2,1,0:T(8,128)(2,1)S(1)}, u32[]{:S(2)}, u32[]{:S(2)}) %collective-permute-start.34) | collective-permute-done | bytes 131104 | tf_op jit(solution)/shard_map/ppermute | solution.py:189
  133.7 3.5 %collective-permute-done.35.c = bf16[4,128,128]{2,1,0:T(8,128)(2,1)S(1)} collective-permute-done((bf16[4,128,128]{2,1,0:T(8,128)(2,1)S(1)}, bf16[4,128,128]{2,1,0:T(8,128)(2,1)S(1)}, u32[]{:S(2)}, u32[]{:S(2)}) %collective-permute-start.35) | collective-permute-done | bytes 131104 | tf_op jit(solution)/shard_map/ppermute | solution.py:189
  137.5 0.8 collective-permute-start.37
  138.3 4.5 %collective-permute-start.38 = (f32[4,128,128]{2,1,0:T(8,128)S(1)}, f32[4,128,128]{2,1,0:T(8,128)S(1)}, u32[]{:S(2)}, u32[]{:S(2)}) collective-permute-start(f32[4,128,128]{2,1,0:T(8,128)S(1)} %shard_map.73.refs_0_), channel_id=1, source_target_pairs={{0,32},{16,48},{32,0},{48,16},{1,33},{17,49},{33,1},{49,17},{2,34}... | collective-permute-start | bytes 786440 | tf_op jit(solution)/shard_map/ppermute | solution.py:189
  142.8 8.0 %shard_map.69 = bf16[192,8192]{1,0:T(8,128)(2,1)} custom-call(s32[256]{0:T(256)S(1)} %select_reduce_fusion.place, s32[64]{0:T(128)S(1)} %xor.28.blocks, bf16[192,8192]{1,0:T(8,128)(2,1)S(1)} %copy-done.3, bf16[256,128,128]{2,1,0:T(8,128)(2,1)S(1)} %get-tuple-element.24.w_ref, bf16[64,192,128]{2,1,0:T(8,128)(2,1)S(1)} %get-tuple-element.26.s_ref), custom_call_target="tpu_custom_call" | custom-call | tf_op jit(solution)/shard_map/pallas_call | solution.py:271
  150.8 1.9 %collective-permute-done.39.refs_3_ = f32[4,128,128]{2,1,0:T(8,128)S(1)} collective-permute-done((f32[4,128,128]{2,1,0:T(8,128)S(1)}, f32[4,128,128]{2,1,0:T(8,128)S(1)}, u32[]{:S(2)}, u32[]{:S(2)}) %collective-permute-start.39) | collective-permute-done | bytes 262176 | tf_op jit(solution)/shard_map/ppermute | solution.py:189
  152.8 2.3 %shard_map.74 = f32[16,128,128]{2,1,0:T(8,128)} custom-call(s32[4]{0:T(128)S(1)} %pad_add_fusion.1.where, f32[4,128,128]{2,1,0:T(8,128)S(1)} %shard_map.73.refs_0_, f32[4,128,128]{2,1,0:T(8,128)S(1)} %collective-permute-done.37.refs_1_, f32[4,128,128]{2,1,0:T(8,128)S(1)} %collective-permute-done.38.refs_2_, f32[4,128,128]{2,1,0:T(8,128)S(1)} %collective-permute-done.39.refs_3_), custom_call_target="tpu_custom_call" | custom-call | tf_op jit(solution)/shard_map/pallas_call | solution.py:306
  (86 shorter events, 6.2 us)
Async XLA Ops:
  0.6 65.7 %collective-permute-start.17 = (bf16[192,8192]{1,0:T(8,128)(2,1)}, bf16[192,8192]{1,0:T(8,128)(2,1)S(1)}, u32[]{:S(2)}, u32[]{:S(2)}) collective-permute-start(bf16[192,8192]{1,0:T(8,128)(2,1)} %mine_ref.1), channel_id=1, source_target_pairs={{0,1},{1,0},{2,3},{3,2},{4,5},{5,4},{6,7},{7,6},{8,9},{9,8},{10,11... | collective-permute-start | bytes 9437192 | tf_op jit(solution)/shard_map/ppermute | solution.py:189
  0.7 15.8 %collective-permute-start = (bf16[16,128,128]{2,1,0:T(8,128)(2,1)}, bf16[16,128,128]{2,1,0:T(8,128)(2,1)S(1)}, u32[]{:S(2)}, u32[]{:S(2)}) collective-permute-start(bf16[16,128,128]{2,1,0:T(8,128)(2,1)} %refs_0_.1), channel_id=1, source_target_pairs={{0,4},{4,8},{8,12},{12,0},{1,5},{5,9},{9,13},{13,1},{2,6},{6,10},{... | collective-permute-start | bytes 1572872 | tf_op jit(solution)/shard_map/ppermute | solution.py:195
  2.3 16.1 %collective-permute-start.1 = (bf16[16,128,128]{2,1,0:T(8,128)(2,1)}, bf16[16,128,128]{2,1,0:T(8,128)(2,1)}, u32[]{:S(2)}, u32[]{:S(2)}) collective-permute-start(bf16[16,128,128]{2,1,0:T(8,128)(2,1)} %refs_0_.1), channel_id=1, source_target_pairs={{0,12},{4,0},{8,4},{12,8},{1,13},{5,1},{9,5},{13,9},{2,14},{6,2},{... | collective-permute-start | bytes 1572872 | tf_op jit(solution)/shard_map/ppermute | solution.py:195
  4.0 14.7 %collective-permute-start.2 = (bf16[16,128,128]{2,1,0:T(8,128)(2,1)}, bf16[16,128,128]{2,1,0:T(8,128)(2,1)}, u32[]{:S(2)}, u32[]{:S(2)}) collective-permute-start(bf16[16,128,128]{2,1,0:T(8,128)(2,1)} %refs_0_.1), channel_id=1, source_target_pairs={{0,2},{2,0},{1,3},{3,1},{4,6},{6,4},{5,7},{7,5},{8,10},{10,8},{9,1... | collective-permute-start | bytes 1572872 | tf_op jit(solution)/shard_map/ppermute | solution.py:189
  5.9 14.0 %collective-permute-start.8 = (bf16[16,128,128]{2,1,0:T(8,128)(2,1)}, bf16[16,128,128]{2,1,0:T(8,128)(2,1)S(1)}, u32[]{:S(2)}, u32[]{:S(2)}) collective-permute-start(bf16[16,128,128]{2,1,0:T(8,128)(2,1)} %refs_0_.1), channel_id=1, source_target_pairs={{0,1},{1,0},{2,3},{3,2},{4,5},{5,4},{6,7},{7,6},{8,9},{9,8},{10,11... | collective-permute-start | bytes 1572872 | tf_op jit(solution)/shard_map/ppermute | solution.py:189
  16.5 18.0 %copy-start.7 = (bf16[16,128,128]{2,1,0:T(8,128)(2,1)}, bf16[16,128,128]{2,1,0:T(8,128)(2,1)S(1)}, u32[]{:S(2)}) copy-start(bf16[16,128,128]{2,1,0:T(8,128)(2,1)S(1)} %collective-permute-done.refs_1_) | copy-start | bytes 1572868
  16.5 13.7 %collective-permute-start.3 = (bf16[16,128,128]{2,1,0:T(8,128)(2,1)S(1)}, bf16[16,128,128]{2,1,0:T(8,128)(2,1)}, u32[]{:S(2)}, u32[]{:S(2)}) collective-permute-start(bf16[16,128,128]{2,1,0:T(8,128)(2,1)S(1)} %collective-permute-done.refs_1_), channel_id=1, source_target_pairs={{0,2},{2,64},{64,66},{66,128},{128,130},{130,192},{192,194},{194,0... | collective-permute-start | bytes 1572872 | tf_op jit(solution)/shard_map/ppermute | solution.py:195
  18.4 14.4 %collective-permute-start.5 = (bf16[16,128,128]{2,1,0:T(8,128)(2,1)S(1)}, bf16[16,128,128]{2,1,0:T(8,128)(2,1)S(1)}, u32[]{:S(2)}, u32[]{:S(2)}) collective-permute-start(bf16[16,128,128]{2,1,0:T(8,128)(2,1)S(1)} %collective-permute-done.refs_1_), channel_id=1, source_target_pairs={{0,4},{4,8},{8,12},{12,0},{1,5},{5,9},{9,13},{13,1},{2,6},{6,10},{... | collective-permute-start | bytes 1572872 | tf_op jit(solution)/shard_map/ppermute | solution.py:195
  18.7 15.7 %collective-permute-start.4 = (bf16[16,128,128]{2,1,0:T(8,128)(2,1)}, bf16[16,128,128]{2,1,0:T(8,128)(2,1)S(1)}, u32[]{:S(2)}, u32[]{:S(2)}) collective-permute-start(bf16[16,128,128]{2,1,0:T(8,128)(2,1)} %collective-permute-done.1.refs_2_), channel_id=1, source_target_pairs={{0,194},{2,0},{64,2},{66,64},{128,66},{130,128},{192,130},{194,192... | collective-permute-start | bytes 1572872 | tf_op jit(solution)/shard_map/ppermute | solution.py:195
  19.9 12.9 %copy-start.8 = (bf16[16,128,128]{2,1,0:T(8,128)(2,1)}, bf16[16,128,128]{2,1,0:T(8,128)(2,1)S(1)}, u32[]{:S(2)}) copy-start(bf16[16,128,128]{2,1,0:T(8,128)(2,1)S(1)} %collective-permute-done.8.refs_9_) | copy-start | bytes 1572868
  19.9 16.5 %collective-permute-start.9 = (bf16[16,128,128]{2,1,0:T(8,128)(2,1)S(1)}, bf16[16,128,128]{2,1,0:T(8,128)(2,1)S(1)}, u32[]{:S(2)}, u32[]{:S(2)}) collective-permute-start(bf16[16,128,128]{2,1,0:T(8,128)(2,1)S(1)} %collective-permute-done.refs_1_), channel_id=1, source_target_pairs={{0,1},{1,0},{2,3},{3,2},{4,5},{5,4},{6,7},{7,6},{8,9},{9,8},{10,11... | collective-permute-start | bytes 1572872 | tf_op jit(solution)/shard_map/ppermute | solution.py:189
  30.2 10.3 %collective-permute-start.10 = (bf16[16,128,128]{2,1,0:T(8,128)(2,1)}, bf16[16,128,128]{2,1,0:T(8,128)(2,1)}, u32[]{:S(2)}, u32[]{:S(2)}) collective-permute-start(bf16[16,128,128]{2,1,0:T(8,128)(2,1)} %collective-permute-done.1.refs_2_), channel_id=1, source_target_pairs={{0,1},{1,0},{2,3},{3,2},{4,5},{5,4},{6,7},{7,6},{8,9},{9,8},{10,11... | collective-permute-start | bytes 1572872 | tf_op jit(solution)/shard_map/ppermute | solution.py:189
  32.8 8.7 %collective-permute-start.11 = (bf16[16,128,128]{2,1,0:T(8,128)(2,1)}, bf16[16,128,128]{2,1,0:T(8,128)(2,1)}, u32[]{:S(2)}, u32[]{:S(2)}) collective-permute-start(bf16[16,128,128]{2,1,0:T(8,128)(2,1)} %collective-permute-done.2.refs_3_), channel_id=1, source_target_pairs={{0,1},{1,0},{2,3},{3,2},{4,5},{5,4},{6,7},{7,6},{8,9},{9,8},{10,11... | collective-permute-start | bytes 1572872 | tf_op jit(solution)/shard_map/ppermute | solution.py:189
  34.4 2.0 %copy-start.9 = (bf16[16,128,128]{2,1,0:T(8,128)(2,1)}, bf16[16,128,128]{2,1,0:T(8,128)(2,1)S(1)}, u32[]{:S(2)}) copy-start(bf16[16,128,128]{2,1,0:T(8,128)(2,1)S(1)} %collective-permute-done.4.refs_5_) | copy-start | bytes 1572868
  34.5 8.7 %collective-permute-start.6 = (bf16[8,128,128]{2,1,0:T(8,128)(2,1)}, bf16[8,128,128]{2,1,0:T(8,128)(2,1)S(1)}, u32[]{:S(2)}, u32[]{:S(2)}) collective-permute-start(bf16[8,128,128]{2,1,0:T(8,128)(2,1)} %get-tuple-element.55), channel_id=1, source_target_pairs={{0,2},{2,64},{64,66},{66,128},{128,130},{130,192},{192,194},{194,0... | collective-permute-start | bytes 786440 | tf_op jit(solution)/shard_map/ppermute | solution.py:195
  36.5 13.8 %collective-permute-start.12 = (bf16[16,128,128]{2,1,0:T(8,128)(2,1)}, bf16[16,128,128]{2,1,0:T(8,128)(2,1)}, u32[]{:S(2)}, u32[]{:S(2)}) collective-permute-start(bf16[16,128,128]{2,1,0:T(8,128)(2,1)} %collective-permute-done.3.refs_4_), channel_id=1, source_target_pairs={{0,1},{1,0},{2,3},{3,2},{4,5},{5,4},{6,7},{7,6},{8,9},{9,8},{10,11... | collective-permute-start | bytes 1572872 | tf_op jit(solution)/shard_map/ppermute | solution.py:189
  40.5 9.8 %collective-permute-start.7 = (bf16[8,128,128]{2,1,0:T(8,128)(2,1)}, bf16[8,128,128]{2,1,0:T(8,128)(2,1)}, u32[]{:S(2)}, u32[]{:S(2)}) collective-permute-start(bf16[8,128,128]{2,1,0:T(8,128)(2,1)} %get-tuple-element.54), channel_id=1, source_target_pairs={{0,194},{2,0},{64,2},{66,64},{128,66},{130,128},{192,130},{194,192... | collective-permute-start | bytes 786440 | tf_op jit(solution)/shard_map/ppermute | solution.py:195
  41.5 10.2 %collective-permute-start.14 = (bf16[16,128,128]{2,1,0:T(8,128)(2,1)}, bf16[16,128,128]{2,1,0:T(8,128)(2,1)}, u32[]{:S(2)}, u32[]{:S(2)}) collective-permute-start(bf16[16,128,128]{2,1,0:T(8,128)(2,1)} %copy-done.6), channel_id=1, source_target_pairs={{0,1},{1,0},{2,3},{3,2},{4,5},{5,4},{6,7},{7,6},{8,9},{9,8},{10,11... | collective-permute-start | bytes 1572872 | tf_op jit(solution)/shard_map/ppermute | solution.py:189
  43.2 9.3 %copy-start.11 = (bf16[8,128,128]{2,1,0:T(8,128)(2,1)}, bf16[8,128,128]{2,1,0:T(8,128)(2,1)S(1)}, u32[]{:S(2)}) copy-start(bf16[8,128,128]{2,1,0:T(8,128)(2,1)S(1)} %collective-permute-done.6.refs_7_) | copy-start | bytes 786436
  43.2 8.6 %collective-permute-start.13 = (bf16[16,128,128]{2,1,0:T(8,128)(2,1)}, bf16[16,128,128]{2,1,0:T(8,128)(2,1)}, u32[]{:S(2)}, u32[]{:S(2)}) collective-permute-start(bf16[16,128,128]{2,1,0:T(8,128)(2,1)} %copy-done.9), channel_id=1, source_target_pairs={{0,1},{1,0},{2,3},{3,2},{4,5},{5,4},{6,7},{7,6},{8,9},{9,8},{10,11... | collective-permute-start | bytes 1572872 | tf_op jit(solution)/shard_map/ppermute | solution.py:189
  50.3 2.0 %collective-permute-start.15 = (bf16[8,128,128]{2,1,0:T(8,128)(2,1)S(1)}, bf16[8,128,128]{2,1,0:T(8,128)(2,1)}, u32[]{:S(2)}, u32[]{:S(2)}) collective-permute-start(bf16[8,128,128]{2,1,0:T(8,128)(2,1)S(1)} %collective-permute-done.6.refs_7_), channel_id=1, source_target_pairs={{0,1},{1,0},{2,3},{3,2},{4,5},{5,4},{6,7},{7,6},{8,9},{9,8},{10,11... | collective-permute-start | bytes 786440 | tf_op jit(solution)/shard_map/ppermute | solution.py:189
  50.3 2.2 %collective-permute-start.16 = (bf16[8,128,128]{2,1,0:T(8,128)(2,1)}, bf16[8,128,128]{2,1,0:T(8,128)(2,1)}, u32[]{:S(2)}, u32[]{:S(2)}) collective-permute-start(bf16[8,128,128]{2,1,0:T(8,128)(2,1)} %collective-permute-done.7.refs_8_), channel_id=1, source_target_pairs={{0,1},{1,0},{2,3},{3,2},{4,5},{5,4},{6,7},{7,6},{8,9},{9,8},{10,11... | collective-permute-start | bytes 786440 | tf_op jit(solution)/shard_map/ppermute | solution.py:189
  56.3 10.2 %copy-start.1 = (bf16[192,8192]{1,0:T(8,128)(2,1)S(1)}, bf16[192,8192]{1,0:T(8,128)(2,1)}, u32[]{:S(2)}) copy-start(bf16[192,8192]{1,0:T(8,128)(2,1)} %mine_ref.1) | copy-start | bytes 9437188
  66.3 6.0 %copy-start.4 = (s32[256]{0:T(256)S(1)}, s32[256]{0:T(256)}, u32[]{:S(2)}) copy-start(s32[256]{0:T(256)} %rows.3) | copy-start | bytes 3076
  66.3 6.0 %copy-start.5 = (s32[256]{0:T(256)S(1)}, s32[256]{0:T(256)}, u32[]{:S(2)}) copy-start(s32[256]{0:T(256)} %cols.3) | copy-start | bytes 3076
  66.3 6.0 %collective-permute-start.18 = (bf16[64,192,128]{2,1,0:T(8,128)(2,1)S(1)}, bf16[64,192,128]{2,1,0:T(8,128)(2,1)S(1)}, u32[]{:S(2)}, u32[]{:S(2)}) collective-permute-start(bf16[64,192,128]{2,1,0:T(8,128)(2,1)S(1)} %get-tuple-element.26.s_ref), channel_id=1, source_target_pairs={{0,1},{1,0},{2,3},{3,2},{4,5},{5,4},{6,7},{7,6},{8,9},{9,8},{10,11... | collective-permute-start | bytes 9437192 | tf_op jit(solution)/shard_map/ppermute | solution.py:189
  74.8 14.3 %collective-permute-start.23 = (bf16[16,128,128]{2,1,0:T(8,128)(2,1)S(1)}, bf16[16,128,128]{2,1,0:T(8,128)(2,1)S(1)}, u32[]{:S(2)}, u32[]{:S(2)}) collective-permute-start(bf16[16,128,128]{2,1,0:T(8,128)(2,1)S(1)} %get-tuple-element.35), channel_id=1, source_target_pairs={{0,4},{4,0},{8,12},{12,8},{1,5},{5,1},{9,13},{13,9},{2,6},{6,2},{1... | collective-permute-start | bytes 1572872 | tf_op jit(solution)/shard_map/ppermute | solution.py:189
  75.0 15.7 %collective-permute-start.25 = (bf16[16,128,128]{2,1,0:T(8,128)(2,1)S(1)}, bf16[16,128,128]{2,1,0:T(8,128)(2,1)S(1)}, u32[]{:S(2)}, u32[]{:S(2)}) collective-permute-start(bf16[16,128,128]{2,1,0:T(8,128)(2,1)S(1)} %get-tuple-element.38), channel_id=1, source_target_pairs={{0,12},{4,8},{8,4},{12,0},{1,13},{5,9},{9,5},{13,1},{2,14},{6,10},... | collective-permute-start | bytes 1572872 | tf_op jit(solution)/shard_map/ppermute | solution.py:189
  76.8 14.9 %collective-permute-start.21 = (bf16[16,128,128]{2,1,0:T(8,128)(2,1)S(1)}, bf16[16,128,128]{2,1,0:T(8,128)(2,1)S(1)}, u32[]{:S(2)}, u32[]{:S(2)}) collective-permute-start(bf16[16,128,128]{2,1,0:T(8,128)(2,1)S(1)} %get-tuple-element.32), channel_id=1, source_target_pairs={{0,48},{16,32},{32,16},{48,0},{1,49},{17,33},{33,17},{49,1},{2,50}... | collective-permute-start | bytes 1572872 | tf_op jit(solution)/shard_map/ppermute | solution.py:189
  79.8 13.3 %collective-permute-start.19 = (bf16[16,128,128]{2,1,0:T(8,128)(2,1)S(1)}, bf16[16,128,128]{2,1,0:T(8,128)(2,1)S(1)}, u32[]{:S(2)}, u32[]{:S(2)}) collective-permute-start(bf16[16,128,128]{2,1,0:T(8,128)(2,1)S(1)} %get-tuple-element.29), channel_id=1, source_target_pairs={{0,16},{16,0},{32,48},{48,32},{1,17},{17,1},{33,49},{49,33},{2,18}... | collective-permute-start | bytes 1572872 | tf_op jit(solution)/shard_map/ppermute | solution.py:189
  89.1 9.1 %collective-permute-start.24 = (bf16[8,128,128]{2,1,0:T(8,128)(2,1)S(1)}, bf16[8,128,128]{2,1,0:T(8,128)(2,1)S(1)}, u32[]{:S(2)}, u32[]{:S(2)}) collective-permute-start(bf16[8,128,128]{2,1,0:T(8,128)(2,1)S(1)} %add_convert_fusion.1), channel_id=1, source_target_pairs={{0,12},{4,8},{8,4},{12,0},{1,13},{5,9},{9,5},{13,1},{2,14},{6,10},... | collective-permute-start | bytes 786440 | tf_op jit(solution)/shard_map/ppermute | solution.py:189
  90.7 7.6 %collective-permute-start.26 = (bf16[8,128,128]{2,1,0:T(8,128)(2,1)S(1)}, bf16[8,128,128]{2,1,0:T(8,128)(2,1)S(1)}, u32[]{:S(2)}, u32[]{:S(2)}) collective-permute-start(bf16[8,128,128]{2,1,0:T(8,128)(2,1)S(1)} %add_convert_fusion), channel_id=1, source_target_pairs={{0,4},{4,0},{8,12},{12,8},{1,5},{5,1},{9,13},{13,9},{2,6},{6,2},{1... | collective-permute-start | bytes 786440 | tf_op jit(solution)/shard_map/ppermute | solution.py:189
  91.7 11.6 %collective-permute-start.22 = (bf16[8,128,128]{2,1,0:T(8,128)(2,1)S(1)}, bf16[8,128,128]{2,1,0:T(8,128)(2,1)S(1)}, u32[]{:S(2)}, u32[]{:S(2)}) collective-permute-start(bf16[8,128,128]{2,1,0:T(8,128)(2,1)S(1)} %add_convert_fusion.2), channel_id=1, source_target_pairs={{0,16},{16,0},{32,48},{48,32},{1,17},{17,1},{33,49},{49,33},{2,18}... | collective-permute-start | bytes 786440 | tf_op jit(solution)/shard_map/ppermute | solution.py:189
  93.2 10.2 %collective-permute-start.20 = (bf16[8,128,128]{2,1,0:T(8,128)(2,1)S(1)}, bf16[8,128,128]{2,1,0:T(8,128)(2,1)S(1)}, u32[]{:S(2)}, u32[]{:S(2)}) collective-permute-start(bf16[8,128,128]{2,1,0:T(8,128)(2,1)S(1)} %add_convert_fusion.3), channel_id=1, source_target_pairs={{0,48},{16,32},{32,16},{48,0},{1,49},{17,33},{33,17},{49,1},{2,50}... | collective-permute-start | bytes 786440 | tf_op jit(solution)/shard_map/ppermute | solution.py:189
  98.5 8.6 %collective-permute-start.27 = (bf16[4,128,128]{2,1,0:T(8,128)(2,1)S(1)}, bf16[4,128,128]{2,1,0:T(8,128)(2,1)S(1)}, u32[]{:S(2)}, u32[]{:S(2)}) collective-permute-start(bf16[4,128,128]{2,1,0:T(8,128)(2,1)S(1)} %get-tuple-element.53), channel_id=1, source_target_pairs={{0,16},{16,0},{32,48},{48,32},{1,17},{17,1},{33,49},{49,33},{2,18}... | collective-permute-start | bytes 393224 | tf_op jit(solution)/shard_map/ppermute | solution.py:189
  100.2 8.4 %collective-permute-start.28 = (bf16[4,128,128]{2,1,0:T(8,128)(2,1)S(1)}, bf16[4,128,128]{2,1,0:T(8,128)(2,1)S(1)}, u32[]{:S(2)}, u32[]{:S(2)}) collective-permute-start(bf16[4,128,128]{2,1,0:T(8,128)(2,1)S(1)} %get-tuple-element.52), channel_id=1, source_target_pairs={{0,32},{16,48},{32,0},{48,16},{1,33},{17,49},{33,1},{49,17},{2,34}... | collective-permute-start | bytes 393224 | tf_op jit(solution)/shard_map/ppermute | solution.py:189
  103.1 6.3 %collective-permute-start.29 = (bf16[4,128,128]{2,1,0:T(8,128)(2,1)S(1)}, bf16[4,128,128]{2,1,0:T(8,128)(2,1)S(1)}, u32[]{:S(2)}, u32[]{:S(2)}) collective-permute-start(bf16[4,128,128]{2,1,0:T(8,128)(2,1)S(1)} %get-tuple-element.51), channel_id=1, source_target_pairs={{0,48},{16,32},{32,16},{48,0},{1,49},{17,33},{33,17},{49,1},{2,50}... | collective-permute-start | bytes 393224 | tf_op jit(solution)/shard_map/ppermute | solution.py:189
  103.5 39.3 %copy-start.3 = (bf16[192,8192]{1,0:T(8,128)(2,1)S(1)}, bf16[192,8192]{1,0:T(8,128)(2,1)}, u32[]{:S(2)}) copy-start(bf16[192,8192]{1,0:T(8,128)(2,1)} %g_ref.3) | copy-start | bytes 9437188
  103.6 5.8 %collective-permute-start.30 = (bf16[4,128,128]{2,1,0:T(8,128)(2,1)S(1)}, bf16[4,128,128]{2,1,0:T(8,128)(2,1)S(1)}, u32[]{:S(2)}, u32[]{:S(2)}) collective-permute-start(bf16[4,128,128]{2,1,0:T(8,128)(2,1)S(1)} %get-tuple-element.50), channel_id=1, source_target_pairs={{0,4},{4,0},{8,12},{12,8},{1,5},{5,1},{9,13},{13,9},{2,6},{6,2},{1... | collective-permute-start | bytes 393224 | tf_op jit(solution)/shard_map/ppermute | solution.py:189
  104.2 7.3 %collective-permute-start.31 = (bf16[4,128,128]{2,1,0:T(8,128)(2,1)S(1)}, bf16[4,128,128]{2,1,0:T(8,128)(2,1)S(1)}, u32[]{:S(2)}, u32[]{:S(2)}) collective-permute-start(bf16[4,128,128]{2,1,0:T(8,128)(2,1)S(1)} %get-tuple-element.49), channel_id=1, source_target_pairs={{0,8},{4,12},{8,0},{12,4},{1,9},{5,13},{9,1},{13,5},{2,10},{6,14},... | collective-permute-start | bytes 393224 | tf_op jit(solution)/shard_map/ppermute | solution.py:189
  107.1 6.2 %collective-permute-start.32 = (bf16[4,128,128]{2,1,0:T(8,128)(2,1)S(1)}, bf16[4,128,128]{2,1,0:T(8,128)(2,1)S(1)}, u32[]{:S(2)}, u32[]{:S(2)}) collective-permute-start(bf16[4,128,128]{2,1,0:T(8,128)(2,1)S(1)} %get-tuple-element.48), channel_id=1, source_target_pairs={{0,12},{4,8},{8,4},{12,0},{1,13},{5,9},{9,5},{13,1},{2,14},{6,10},... | collective-permute-start | bytes 393224 | tf_op jit(solution)/shard_map/ppermute | solution.py:189
  113.4 6.9 %collective-permute-start.33 = (f32[4,128,128]{2,1,0:T(8,128)S(1)}, f32[4,128,128]{2,1,0:T(8,128)S(1)}, u32[]{:S(2)}, u32[]{:S(2)}) collective-permute-start(f32[4,128,128]{2,1,0:T(8,128)S(1)} %fusion.5), channel_id=1, source_target_pairs={{0,2},{2,0},{1,3},{3,1},{4,6},{6,4},{5,7},{7,5},{8,10},{10,8},{9,1... | collective-permute-start | bytes 786440 | tf_op jit(solution)/shard_map/ppermute | solution.py:189
  120.4 13.3 %collective-permute-start.34 = (bf16[4,128,128]{2,1,0:T(8,128)(2,1)S(1)}, bf16[4,128,128]{2,1,0:T(8,128)(2,1)S(1)}, u32[]{:S(2)}, u32[]{:S(2)}) collective-permute-start(bf16[4,128,128]{2,1,0:T(8,128)(2,1)S(1)} %fusion.11.a), channel_id=1, source_target_pairs={{0,64},{64,0},{128,192},{192,128},{1,65},{65,1},{129,193},{193,129... | collective-permute-start | bytes 393224 | tf_op jit(solution)/shard_map/ppermute | solution.py:189
  127.0 10.2 %collective-permute-start.35 = (bf16[4,128,128]{2,1,0:T(8,128)(2,1)S(1)}, bf16[4,128,128]{2,1,0:T(8,128)(2,1)S(1)}, u32[]{:S(2)}, u32[]{:S(2)}) collective-permute-start(bf16[4,128,128]{2,1,0:T(8,128)(2,1)S(1)} %fusion.11.a), channel_id=1, source_target_pairs={{0,128},{64,192},{128,0},{192,64},{1,129},{65,193},{129,1},{193,65... | collective-permute-start | bytes 393224 | tf_op jit(solution)/shard_map/ppermute | solution.py:189
  127.2 10.3 %collective-permute-start.36 = (bf16[4,128,128]{2,1,0:T(8,128)(2,1)S(1)}, bf16[4,128,128]{2,1,0:T(8,128)(2,1)S(1)}, u32[]{:S(2)}, u32[]{:S(2)}) collective-permute-start(bf16[4,128,128]{2,1,0:T(8,128)(2,1)S(1)} %fusion.11.a), channel_id=1, source_target_pairs={{0,192},{64,128},{128,64},{192,0},{1,193},{65,129},{129,65},{193,1... | collective-permute-start | bytes 393224 | tf_op jit(solution)/shard_map/ppermute | solution.py:189
  137.5 13.3 %collective-permute-start.37 = (f32[4,128,128]{2,1,0:T(8,128)S(1)}, f32[4,128,128]{2,1,0:T(8,128)S(1)}, u32[]{:S(2)}, u32[]{:S(2)}) collective-permute-start(f32[4,128,128]{2,1,0:T(8,128)S(1)} %shard_map.73.refs_0_), channel_id=1, source_target_pairs={{0,16},{16,0},{32,48},{48,32},{1,17},{17,1},{33,49},{49,33},{2,18}... | collective-permute-start | bytes 786440 | tf_op jit(solution)/shard_map/ppermute | solution.py:189
  138.3 12.5 %collective-permute-start.38 = (f32[4,128,128]{2,1,0:T(8,128)S(1)}, f32[4,128,128]{2,1,0:T(8,128)S(1)}, u32[]{:S(2)}, u32[]{:S(2)}) collective-permute-start(f32[4,128,128]{2,1,0:T(8,128)S(1)} %shard_map.73.refs_0_), channel_id=1, source_target_pairs={{0,32},{16,48},{32,0},{48,16},{1,33},{17,49},{33,1},{49,17},{2,34}... | collective-permute-start | bytes 786440 | tf_op jit(solution)/shard_map/ppermute | solution.py:189
  142.8 10.0 %collective-permute-start.39 = (f32[4,128,128]{2,1,0:T(8,128)S(1)}, f32[4,128,128]{2,1,0:T(8,128)S(1)}, u32[]{:S(2)}, u32[]{:S(2)}) collective-permute-start(f32[4,128,128]{2,1,0:T(8,128)S(1)} %shard_map.73.refs_0_), channel_id=1, source_target_pairs={{0,48},{16,32},{32,16},{48,0},{1,49},{17,33},{33,17},{49,1},{2,50}... | collective-permute-start | bytes 786440 | tf_op jit(solution)/shard_map/ppermute | solution.py:189
  (4 other events, 5.4 us)

commit v3 on v2

--- a/solution.py
+++ b/solution.py
@@ -48,37 +48,64 @@
     return cotangent * slope
 
 
-PIECES = tuple(
-    (x, zl, core, first, size)
-    for core in (0, 1)
-    for x, zl, first, size in (
-        (0, 0, 0, 16),
-        (3, 0, 0, 16),
-        (1, 0, 0, 16),
-        (0, 1, 0, 16),
-        (3, 1, 0, 16),
-        (1, 1, 0, 16),
-        (2, 0, 0, 16),
-        (2, 1, 0, 8),
-        (2, 1, 8, 8),
-    )
+ROUNDS = (
+    (0, 0, 0, 16),
+    (3, 0, 0, 16),
+    (1, 0, 0, 16),
+    (0, 1, 0, 16),
+    (3, 1, 0, 16),
+    (1, 1, 0, 16),
+    (2, 0, 0, 8),
+    (2, 0, 8, 8),
+    (2, 1, 0, 8),
+    (2, 1, 8, 8),
 )
-
-
-def forward_kernel(where, place, blocks, x_ref, g_ref, *refs):
-    pieces, (s_ref, w_ref, sems) = refs[: len(PIECES)], refs[len(PIECES) :]
+FIRST = tuple((*ROUNDS[i][:2], 0, *ROUNDS[i][2:]) for i in range(4)) + ((0, 0, 1, 0, 16),)
+MIDDLE = (
+    *((*ROUNDS[i][:2], 0, *ROUNDS[i][2:]) for i in range(4, 8)),
+    *((*ROUNDS[i][:2], 1, *ROUNDS[i][2:]) for i in range(1, 4)),
+    (2, 0, 1, 0, 16),
+)
+LAST = (
+    *((*ROUNDS[i][:2], 0, *ROUNDS[i][2:]) for i in (8, 9)),
+    *((*ROUNDS[i][:2], 1, *ROUNDS[i][2:]) for i in (4, 5, 8, 9)),
+)
+
+
+def place_copies(where, listed, pieces, w_ref, sems):
     copies = []
-    for i, (x, zl, core, first, size) in enumerate(PIECES):
+    for i, (x, zl, core, first, size) in enumerate(listed):
         owner = (lax.rem(where[0] + x, 4) * 2 + (where[2] ^ zl)) * 2 + (where[3] ^ core)
-        copies.append(
-            pltpu.make_async_copy(
-                pieces[i], w_ref.at[pl.ds(owner * 16 + first, size)], sems.at[i]
-            )
-        )
+        to = w_ref.at[pl.ds(owner * 16 + first, size)]
+        copies.append(pltpu.make_async_copy(pieces[i], to, sems.at[i]))
+    return copies
+
+
+def run(copies):
     for copy in copies:
         copy.start()
     for copy in copies:
         copy.wait()
+
+
+def load_kernel(where, x_hbm, g_hbm, *refs):
+    pieces, (x_ref, g_ref, w_ref, sems) = refs[: len(FIRST)], refs[len(FIRST) :]
+    copies = place_copies(where, FIRST, pieces, w_ref, sems)
+    copies.append(pltpu.make_async_copy(x_hbm, x_ref, sems.at[len(FIRST)]))
+    copies.append(pltpu.make_async_copy(g_hbm, g_ref, sems.at[len(FIRST) + 1]))
+    run(copies)
+
+
+def more_kernel(where, given, *refs):
+    del given
+    pieces, (w_ref, sems) = refs[: len(MIDDLE)], refs[len(MIDDLE) :]
+    run(place_copies(where, MIDDLE, pieces, w_ref, sems))
+
+
+def forward_kernel(where, place, blocks, x_ref, g_ref, given, *refs):
+    del given
+    pieces, (s_ref, w_ref, sems) = refs[: len(LAST)], refs[len(LAST) :]
+    run(place_copies(where, LAST, pieces, w_ref, sems))
 
     def one(group):
         ids = [blocks[group * 4 + m] for m in range(4)]
@@ -106,9 +133,14 @@
     lax.fori_loop(0, 16 // UNROLL, some, 0)
 
 
-def backward_kernel(place, blocks, g_ref, w_ref, s_ref, o_ref):
-    def one(group, carry):
-        ids = [blocks[group * 4 + m] for m in range(4)]
+def backward_kernel(half, place, blocks, g_ref, w_ref, s_ref, *refs):
+    o_hbm, out, sems = refs[-3:]
+
+    def write(at, column):
+        return pltpu.make_async_copy(out.at[at], o_hbm.at[:, lanes(column)], sems.at[at])
+
+    def one(step, carry):
+        ids = [blocks[(half * 8 + step) * 4 + m] for m in range(4)]
         s = jnp.concatenate([s_ref[b] for b in ids], axis=1)
         for first in (0, 2):
             pair = (first, first + 1)
@@ -127,10 +159,17 @@
             for k, m in enumerate(pair):
                 cot = g_ref[:, lanes(ids[m])].astype(jnp.float32)
                 total = cot + back[:, k * SIDE : (k + 1) * SIDE]
-                o_ref[:, lanes(ids[m])] = total.astype(jnp.bfloat16)
+                out[step * 4 + m] = total.astype(jnp.bfloat16)
+        for m in range(4):
+            write(step * 4 + m, ids[m]).start()
         return carry
 
-    lax.fori_loop(0, 16, one, 0)
+    def done(at, carry):
+        write(at, blocks[half * 32 + at]).wait()
+        return carry
+
+    lax.fori_loop(0, 8, one, 0)
+    lax.fori_loop(0, 32, done, 0)
 
 
 def transpose_kernel(mine_ref, other_ref, xt_ref):
@@ -167,21 +206,18 @@
                     out[at] = value.astype(out.dtype)
 
 
+def normalize_kernel(a, b, c, d, out):
+    f32 = jnp.float32
+    for k in range(4):
+        grad = (a[k].astype(f32) + b[k].astype(f32)) + (c[k].astype(f32) + d[k].astype(f32))
+        mean = jnp.mean(grad * grad)
+        out[k] = (grad * lax.rsqrt(mean + 1e-06)).astype(jnp.bfloat16)
+
+
 def finish_kernel(where, *refs):
-    out = refs[-1]
-    y = where[1]
     for r in range(4):
         for k in range(4):
-            grad = refs[r][k]
-            mean = jnp.mean(grad * grad)
-            out[(y ^ r) * 4 + k] = grad * lax.rsqrt(mean + 1e-06)
-
-
-def sum_four_kernel(a, b, c, d, out):
-    f32 = jnp.float32
-    out[...] = (a[...].astype(f32) + b[...].astype(f32)) + (
-        c[...].astype(f32) + d[...].astype(f32)
-    )
+            refs[-1][(where[1] ^ r) * 4 + k] = refs[r][k].astype(jnp.float32)
 
 
 def swap(value, axis, mask):
@@ -223,24 +259,58 @@
     left, right = turn(own, "x", 1), turn(own, "x", 3)
     beside = swap(own, "zl", 1)
     others = swap(features, "core", 1)
-    far = turn(left, "x", 1)
-    beside_left, beside_right = turn(left, Z, 1), turn(right, Z, 7)
-    features_near, grad_out = near(features), near(grad_out)
-    beside_far = (turn(far[:8], Z, 1), turn(far[8:], Z, 7))
-    mine = (own, left, right, beside, beside_left, beside_right, far, *beside_far)
-    pieces = (*mine, *(swap(piece, "core", 1) for piece in mine))
-    pieces = [stored(piece) for piece in pieces]
+    own_other = swap(own, "core", 1)
+    left, right, beside, others, own_other, place, blocks = lax.optimization_barrier(
+        (left, right, beside, others, own_other, place, blocks)
+    )
+    features_near, grad_near, whole = pl.pallas_call(
+        load_kernel,
+        out_shape=[
+            pltpu.VMEM(features.shape, bf16),
+            pltpu.VMEM(features.shape, bf16),
+            pltpu.VMEM((256, SIDE, SIDE), bf16),
+        ],
+        in_specs=[SMEM] + [ANY] * (2 + len(FIRST)),
+        out_specs=[VMEM] * 3,
+        scratch_shapes=[pltpu.SemaphoreType.DMA((len(FIRST) + 2,))],
+        compiler_params=PARAMS,
+    )(
+        where,
+        *(stored(v) for v in (features, grad_out, own, left, right, beside, own_other)),
+    )
+    second = [turn(left, Z, 1), turn(right, Z, 7), turn(left[:8], "x", 1), turn(right[8:], "x", 3)]
+    crossed = [swap(left, "core", 1)]
+    second, crossed, whole, right, beside = lax.optimization_barrier(
+        (second, crossed, whole, right, beside)
+    )
+    far = second[2:]
+    beside_far = (turn(far[0], Z, 1), turn(far[1], Z, 7))
+    both_far = jnp.concatenate(far, axis=0)
+    crossed += [swap(piece, "core", 1) for piece in (right, beside, both_far)]
+    whole = pl.pallas_call(
+        more_kernel,
+        out_shape=pltpu.VMEM((256, SIDE, SIDE), bf16),
+        in_specs=[SMEM, VMEM] + [ANY] * len(MIDDLE),
+        out_specs=VMEM,
+        scratch_shapes=[pltpu.SemaphoreType.DMA((len(MIDDLE),))],
+        input_output_aliases={1: 0},
+        compiler_params=PARAMS,
+    )(where, near(whole), *(stored(piece) for piece in (*second, *crossed)))
+    *beside_far, whole = lax.optimization_barrier((*beside_far, whole))
+    crossed = [swap(piece, "core", 1) for piece in (*second[:2], *beside_far)]
+    late = [stored(piece) for piece in (*beside_far, *crossed)]
     slopes, whole = pl.pallas_call(
         forward_kernel,
         out_shape=[
             pltpu.VMEM((64, rows_here, SIDE), bf16),
             pltpu.VMEM((256, SIDE, SIDE), bf16),
         ],
-        in_specs=[SMEM] * 3 + [VMEM] * 2 + [ANY] * len(pieces),
+        in_specs=[SMEM] * 3 + [VMEM] * 3 + [ANY] * len(LAST),
         out_specs=[VMEM, VMEM],
-        scratch_shapes=[pltpu.SemaphoreType.DMA((len(pieces),))],
-        compiler_params=PARAMS,
-    )(where, place, blocks, features_near, grad_out, *pieces)
+        scratch_shapes=[pltpu.SemaphoreType.DMA((len(LAST),))],
+        input_output_aliases={5: 1},
+        compiler_params=PARAMS,
+    )(where, place, blocks, near(features_near), near(grad_near), near(whole), *late)
     slopes, others = lax.optimization_barrier((slopes, others))
     other_slopes = swap(slopes, "core", 1)
     xt = pl.pallas_call(
@@ -249,7 +319,7 @@
         in_specs=[VMEM, VMEM],
         out_specs=VMEM,
         compiler_params=PARAMS,
-    )(features_near, near(others))
+    )(near(features_near), near(others))
     operands = (tile_row, tile_column, where, near(xt), near(slopes), near(other_slopes))
     sent = pl.pallas_call(
         functools.partial(partial_kernel, SENT, False),
@@ -268,13 +338,27 @@
         out_specs=[VMEM] * 8,
         compiler_params=PARAMS,
     )(*operands)
-    grad_features = pl.pallas_call(
-        backward_kernel,
+    kept = list(kept)
+    after, kept[0] = lax.optimization_barrier((place, kept[0]))
+    backward = functools.partial(
+        pl.pallas_call,
         out_shape=shape(features.shape, bf16),
-        in_specs=[SMEM, SMEM, VMEM, VMEM, VMEM],
-        out_specs=VMEM,
-        compiler_params=PARAMS,
-    )(place, blocks, grad_out, near(whole), near(slopes))
+        out_specs=ANY,
+        scratch_shapes=[
+            pltpu.VMEM((32, rows_here, SIDE), bf16),
+            pltpu.SemaphoreType.DMA((32,)),
+        ],
+        compiler_params=PARAMS,
+    )
+    grad_features = backward(
+        functools.partial(backward_kernel, 0), in_specs=[SMEM] * 2 + [VMEM] * 3
+    )(after, blocks, near(grad_near), near(whole), near(slopes))
+    got, kept, grad_features = lax.optimization_barrier((got, kept, grad_features))
+    grad_features = backward(
+        functools.partial(backward_kernel, 1),
+        in_specs=[SMEM] * 2 + [VMEM] * 3 + [ANY],
+        input_output_aliases={5: 0},
+    )(place, blocks, near(grad_near), near(whole), near(slopes), grad_features)
 
     second = [
         swap((kept[2 * i + 1] + got[i][8:].astype(f32)).astype(bf16), axis, (3, 1)[half])
@@ -289,27 +373,28 @@
         )
         for i in (0, 2)
     ]
-    away = [swap(rest[0][r].astype(bf16), "y", r) for r in (1, 2, 3)]
-    away += [swap(rest[1][r].astype(bf16), "x", r) for r in (1, 2, 3)]
-    away = [piece.astype(f32) for piece in lax.optimization_barrier(away)]
-    sums = [rest[i][0] + (away[3 * i] + away[3 * i + 2]) + away[3 * i + 1] for i in (0, 1)]
+    def reduce_last(parts, axis):
+        away = [swap(parts[r].astype(bf16), axis, r).astype(f32) for r in (1, 2, 3)]
+        return parts[0] + (away[0] + away[2]) + away[1]
+
+    sums = [reduce_last(rest[0], "y")]
+    sums[0], rest[1] = lax.optimization_barrier((sums[0], rest[1]))
+    sums.append(reduce_last(rest[1], "x"))
     mine = (sums[1] + swap(sums[0], "zl", 1)).astype(bf16)
-    across = [swap(mine, "zh", r) for r in (1, 2, 3)]
-    summed = pl.pallas_call(
-        sum_four_kernel,
-        out_shape=shape((4, SIDE, SIDE), f32),
+    group = pl.pallas_call(
+        normalize_kernel,
+        out_shape=shape((4, SIDE, SIDE), bf16),
         in_specs=[VMEM] * 4,
         out_specs=VMEM,
         compiler_params=PARAMS,
-    )(mine, *across)
-    gathered = [swap(summed, "y", r) for r in (1, 2, 3)]
+    )(mine, *(swap(mine, "zh", r) for r in (1, 2, 3)))
     tile_update = pl.pallas_call(
         finish_kernel,
         out_shape=shape((16, SIDE, SIDE), f32),
         in_specs=[SMEM] + [VMEM] * 4,
         out_specs=VMEM,
         compiler_params=PARAMS,
-    )(where, summed, *gathered)
+    )(where, group, *(swap(group, "y", r) for r in (1, 2, 3)))
     return grad_features, tile_update
 
 

time: 155 us -> 145 us (0.935); the launches traced: 155 us -> 143 us
  waiting for transfers between devices: 64 us -> 48.4 us
  Pallas kernels: 30.9 us -> 35.5 us
  starting transfers between devices: 47.3 us -> 45.7 us
    ppermute x7 -> x8, waiting for transfers between devices: 31.9 us -> 13.3 us  [turn(): lax.ppermute(value, axes, [(i, (i + by) % size) for i in range(size)])]
    pallas_call x2 -> x5, Pallas kernels: 8.08 us -> 15.6 us  [the longest x1 4.24 us: on_device(): pl.pallas_call(load_kernel, out_shape=[pltpu.VMEM(features.shape, bf16),...]
    unnamed x24, local copies, waits for them, and re-layouts: 5.3 us -> 1.92 us
    ppermute x33, waiting for transfers between devices: 32.1 us -> 35.1 us  [swap(): return lax.ppermute(value, axis, [(i, i ^ mask) for i in range(size)])]
    ppermute x33, starting transfers between devices: 38.2 us -> 35.6 us  [swap(): return lax.ppermute(value, axis, [(i, i ^ mask) for i in range(size)])]
    slice x1 -> x2, local copies, waits for them, and re-layouts: 0.84 us -> 3.37 us  [the longest x1 1.7 us: on_device(): left[:8]]
    pallas_call x1, Pallas kernels: 9.96 us -> 7.71 us  [on_device(): pl.pallas_call(forward_kernel, out_shape=[pltpu.VMEM((64, rows_here, SIDE...]
    ppermute x7 -> x8, starting transfers between devices: 9.06 us -> 10.1 us  [turn(): lax.ppermute(value, axes, [(i, (i + by) % size) for i in range(size)])]
  transfers between devices with their start and end apart: 40 -> 41, of which waited for: 19 -> 24; matrix products, arithmetic and copies ran while one was open for 3% -> 5% of each run, Pallas kernels for 17% -> 16%
where the time goes in v3:
time: 145 us; the launch traced here: 143 us
  waiting for transfers between devices  48.4 us (33%)
  starting transfers between devices  45.7 us (32%)
  Pallas kernels  35.5 us (24%)
  local copies, waits for them, and re-layouts  5.44 us (4%)
  other arithmetic  5.03 us (3%)
  between operations  2.92 us (2%)
    ppermute x33, starting transfers between devices, swap(): return lax.ppermute(value, axis, [(i, i ^ mask) for i in range(size)])  35.6 us
    ppermute x33, waiting for transfers between devices, swap(): return lax.ppermute(value, axis, [(i, i ^ mask) for i in range(size)])  35.1 us
    ppermute x8, waiting for transfers between devices, turn(): lax.ppermute(value, axes, [(i, (i + by) % size) for i in range(size)])  13.3 us
    ppermute x8, starting transfers between devices, turn(): lax.ppermute(value, axes, [(i, (i + by) % size) for i in range(size)])  10.1 us
    pallas_call x1, Pallas kernels, on_device(): pl.pallas_call(forward_kernel, out_shape=[pltpu.VMEM((64, rows_here, SIDE...  7.71 us
    pallas_call x1, Pallas kernels, on_device(): pl.pallas_call(transpose_kernel, out_shape=pltpu.VMEM((64, SIDE, 2 * rows...  5.76 us
    pallas_call x1, Pallas kernels, on_device(): pl.pallas_call(load_kernel, out_shape=[pltpu.VMEM(features.shape, bf16),...  4.24 us
    pallas_call x1, Pallas kernels, on_device(): backward(functools.partial(backward_kernel, 0), in_specs=[SMEM] * 2 + [VM...  4.21 us
  transfers between devices with their start and end apart: 41, of which 24 were waited for; matrix products, arithmetic and copies ran while one was open for 5% of the time, Pallas kernels for 16%

profile of v3, /device:TPU:32, one launch (start us, length us, event | category | flops | bytes accessed | tf_op | source)
XLA Modules:
  0.0 143.0 jit_solution(415948459577471694)
XLA Ops:
  0.7 1.9 %collective-permute-start.2 = (bf16[16,128,128]{2,1,0:T(8,128)(2,1)}, bf16[16,128,128]{2,1,0:T(8,128)(2,1)}, u32[]{:S(2)}, u32[]{:S(2)}) collective-permute-start(bf16[16,128,128]{2,1,0:T(8,128)(2,1)} %refs_0_.1), channel_id=1, source_target_pairs={{0,2},{2,0},{1,3},{3,1},{4,6},{6,4},{5,7},{7,5},{8,10},{10,8},{9,1... | collective-permute-start | bytes 1572872 | tf_op jit(solution)/shard_map/ppermute | solution.py:225
  2.7 1.0 collective-permute-start.1
  4.7 1.3 fusion.10
  9.7 5.8 %collective-permute-done.2.refs_3_ = bf16[16,128,128]{2,1,0:T(8,128)(2,1)} collective-permute-done((bf16[16,128,128]{2,1,0:T(8,128)(2,1)}, bf16[16,128,128]{2,1,0:T(8,128)(2,1)}, u32[]{:S(2)}, u32[]{:S(2)}) %collective-permute-start.2) | collective-permute-done | bytes 524320 | tf_op jit(solution)/shard_map/ppermute | solution.py:225
  15.5 1.5 %collective-permute-done.1.refs_2_ = bf16[16,128,128]{2,1,0:T(8,128)(2,1)} collective-permute-done((bf16[16,128,128]{2,1,0:T(8,128)(2,1)}, bf16[16,128,128]{2,1,0:T(8,128)(2,1)}, u32[]{:S(2)}, u32[]{:S(2)}) %collective-permute-start.1) | collective-permute-done | bytes 524320 | tf_op jit(solution)/shard_map/ppermute | solution.py:231
  17.0 2.1 %collective-permute-done.refs_1_ = bf16[16,128,128]{2,1,0:T(8,128)(2,1)} collective-permute-done((bf16[16,128,128]{2,1,0:T(8,128)(2,1)}, bf16[16,128,128]{2,1,0:T(8,128)(2,1)}, u32[]{:S(2)}, u32[]{:S(2)}) %collective-permute-start) | collective-permute-done | bytes 524320 | tf_op jit(solution)/shard_map/ppermute | solution.py:231
  19.1 3.6 %collective-permute-start.5 = (bf16[16,128,128]{2,1,0:T(8,128)(2,1)}, bf16[16,128,128]{2,1,0:T(8,128)(2,1)}, u32[]{:S(2)}, u32[]{:S(2)}) collective-permute-start(bf16[16,128,128]{2,1,0:T(8,128)(2,1)} %collective-permute-done.refs_1_), channel_id=1, source_target_pairs={{0,2},{2,64},{64,66},{66,128},{128,130},{130,192},{192,194},{194,0... | collective-permute-start | bytes 1572872 | tf_op jit(solution)/shard_map/ppermute | solution.py:231
  22.7 1.7 %slice.60 = bf16[8,128,128]{2,1,0:T(8,128)(2,1)} slice(bf16[16,128,128]{2,1,0:T(8,128)(2,1)} %collective-permute-done.refs_1_), slice={[0:8], [0:128], [0:128]} | slice | bytes 524288 | tf_op jit(solution)/shard_map/slice | solution.py:281
  24.4 1.7 %slice.61 = bf16[8,128,128]{2,1,0:T(8,128)(2,1)} slice(bf16[16,128,128]{2,1,0:T(8,128)(2,1)} %collective-permute-done.1.refs_2_), slice={[8:16], [0:128], [0:128]} | slice | bytes 524288 | tf_op jit(solution)/shard_map/slice | solution.py:281
  26.5 1.6 %collective-permute-start.7 = (bf16[8,128,128]{2,1,0:T(8,128)(2,1)}, bf16[8,128,128]{2,1,0:T(8,128)(2,1)}, u32[]{:S(2)}, u32[]{:S(2)}) collective-permute-start(bf16[8,128,128]{2,1,0:T(8,128)(2,1)} %slice.60), channel_id=1, source_target_pairs={{0,4},{4,8},{8,12},{12,0},{1,5},{5,9},{9,13},{13,1},{2,6},{6,10},{... | collective-permute-start | bytes 786440 | tf_op jit(solution)/shard_map/ppermute | solution.py:231
  28.2 4.2 %shard_map.68 = (bf16[192,8192]{1,0:T(8,128)(2,1)S(1)}, bf16[192,8192]{1,0:T(8,128)(2,1)S(1)}, bf16[256,128,128]{2,1,0:T(8,128)(2,1)S(1)}) custom-call(s32[4]{0:T(128)S(1)} %pad_add_fusion.1.where, bf16[192,8192]{1,0:T(8,128)(2,1)} %x_hbm.1, bf16[192,8192]{1,0:T(8,128)(2,1)} %g_hbm.1, bf16[16,128,128]{2,1,0:T(8,128)(2,1)} %refs_0_.1, ...), custom_call_target="tpu_custom_call" | custom-call | tf_op jit(solution)/shard_map/pallas_call | solution.py:266
  32.5 2.2 %collective-permute-done.8.refs_3_ = bf16[8,128,128]{2,1,0:T(8,128)(2,1)S(1)} collective-permute-done((bf16[8,128,128]{2,1,0:T(8,128)(2,1)}, bf16[8,128,128]{2,1,0:T(8,128)(2,1)S(1)}, u32[]{:S(2)}, u32[]{:S(2)}) %collective-permute-start.8) | collective-permute-done | bytes 262176 | tf_op jit(solution)/shard_map/ppermute | solution.py:231
  34.7 1.4 collective-permute-done.7.refs_2_
  38.7 2.4 %collective-permute-start.10 = (bf16[8,128,128]{2,1,0:T(8,128)(2,1)}, bf16[8,128,128]{2,1,0:T(8,128)(2,1)S(1)}, u32[]{:S(2)}, u32[]{:S(2)}) collective-permute-start(bf16[8,128,128]{2,1,0:T(8,128)(2,1)} %collective-permute-done.7.refs_2_), channel_id=1, source_target_pairs={{0,2},{2,64},{64,66},{66,128},{128,130},{130,192},{192,194},{194,0... | collective-permute-start | bytes 786440 | tf_op jit(solution)/shard_map/ppermute | solution.py:231
  43.0 2.6 %shard_map.69.given = bf16[256,128,128]{2,1,0:T(8,128)(2,1)S(1)} custom-call(s32[4]{0:T(128)S(1)} %pad_add_fusion.1.where, bf16[256,128,128]{2,1,0:T(8,128)(2,1)S(1)} %get-tuple-element.67.given, bf16[16,128,128]{2,1,0:T(8,128)(2,1)} %collective-permute-done.5.refs_0_, ...), custom_call_target="tpu_custom_call", output_to_operand_aliasing={{}: (1, {})} | custom-call | tf_op jit(solution)/shard_map/pallas_call | solution.py:290
  45.6 2.4 %collective-permute-done.10.refs_0_ = bf16[8,128,128]{2,1,0:T(8,128)(2,1)S(1)} collective-permute-done((bf16[8,128,128]{2,1,0:T(8,128)(2,1)}, bf16[8,128,128]{2,1,0:T(8,128)(2,1)S(1)}, u32[]{:S(2)}, u32[]{:S(2)}) %collective-permute-start.10) | collective-permute-done | bytes 262176 | tf_op jit(solution)/shard_map/ppermute | solution.py:231
  48.0 2.7 %collective-permute-done.11.refs_1_ = bf16[8,128,128]{2,1,0:T(8,128)(2,1)S(1)} collective-permute-done((bf16[8,128,128]{2,1,0:T(8,128)(2,1)S(1)}, bf16[8,128,128]{2,1,0:T(8,128)(2,1)S(1)}, u32[]{:S(2)}, u32[]{:S(2)}) %collective-permute-start.11) | collective-permute-done | bytes 262176 | tf_op jit(solution)/shard_map/ppermute | solution.py:231
  53.3 7.7 %shard_map.70 = (bf16[64,192,128]{2,1,0:T(8,128)(2,1)S(1)}, bf16[256,128,128]{2,1,0:T(8,128)(2,1)S(1)}) custom-call(s32[4]{0:T(128)S(1)} %pad_add_fusion.1.where, s32[256]{0:T(256)S(1)} %select_reduce_fusion.place, s32[64]{0:T(128)S(1)} %xor.28.blocks, bf16[192,8192]{1,0:T(8,128)(2,1)S(1)} %get-tuple-element.63.x_ref.mine_ref, ...), custom_call_target="tpu_custom_call", output_to_operand_aliasing={{1}: (5, {})} | custom-call | tf_op jit(solution)/shard_map/pallas_call | solution.py:302
  61.3 5.8 %shard_map.71.xt_ref = bf16[64,128,384]{2,1,0:T(8,128)(2,1)S(1)} custom-call(bf16[192,8192]{1,0:T(8,128)(2,1)S(1)} %get-tuple-element.63.x_ref.mine_ref, bf16[192,8192]{1,0:T(8,128)(2,1)S(1)} %collective-permute-done.3.other_ref), custom_call_target="tpu_custom_call" | custom-call | tf_op jit(solution)/shard_map/pallas_call | solution.py:316
  67.1 2.5 %shard_map.72 = (bf16[16,128,128]{2,1,0:T(8,128)(2,1)S(1)}, bf16[16,128,128]{2,1,0:T(8,128)(2,1)S(1)}, bf16[16,128,128]{2,1,0:T(8,128)(2,1)S(1)}, bf16[16,128,128]{2,1,0:T(8,128)(2,1)S(1)}) custom-call(s32[256]{0:T(256)S(1)} %copy-done, s32[256]{0:T(256)S(1)} %copy-done.1, s32[4]{0:T(128)S(1)} %pad_add_fusion.1.where, ...), custom_call_target="tpu_custom_call" | custom-call | tf_op jit(solution)/shard_map/pallas_call | solution.py:324
  70.1 1.6 %collective-permute-start.22 = (bf16[16,128,128]{2,1,0:T(8,128)(2,1)S(1)}, bf16[16,128,128]{2,1,0:T(8,128)(2,1)S(1)}, u32[]{:S(2)}, u32[]{:S(2)}) collective-permute-start(bf16[16,128,128]{2,1,0:T(8,128)(2,1)S(1)} %get-tuple-element.83), channel_id=1, source_target_pairs={{0,16},{16,0},{32,48},{48,32},{1,17},{17,1},{33,49},{49,33},{2,18}... | collective-permute-start | bytes 1572872 | tf_op jit(solution)/shard_map/ppermute | solution.py:225
  71.7 2.2 %collective-permute-start.23 = (bf16[16,128,128]{2,1,0:T(8,128)(2,1)S(1)}, bf16[16,128,128]{2,1,0:T(8,128)(2,1)S(1)}, u32[]{:S(2)}, u32[]{:S(2)}) collective-permute-start(bf16[16,128,128]{2,1,0:T(8,128)(2,1)S(1)} %get-tuple-element.84), channel_id=1, source_target_pairs={{0,48},{16,32},{32,16},{48,0},{1,49},{17,33},{33,17},{49,1},{2,50}... | collective-permute-start | bytes 1572872 | tf_op jit(solution)/shard_map/ppermute | solution.py:225
  73.9 2.4 %shard_map.73 = (f32[8,128,128]{2,1,0:T(8,128)S(1)}, f32[8,128,128]{2,1,0:T(8,128)S(1)}, f32[8,128,128]{2,1,0:T(8,128)S(1)}, f32[8,128,128]{2,1,0:T(8,128)S(1)},...) custom-call(s32[256]{0:T(256)S(1)} %copy-done, ...), custom_call_target="tpu_custom_call" | custom-call | tf_op jit(solution)/shard_map/pallas_call | solution.py:334
  76.3 4.2 %shard_map.74.refs_0_ = bf16[192,8192]{1,0:T(8,128)(2,1)} custom-call(s32[256]{0:T(256)S(1)} %select_reduce_fusion.place, s32[64]{0:T(128)S(1)} %xor.28.blocks, bf16[192,8192]{1,0:T(8,128)(2,1)S(1)} %get-tuple-element.62.g_ref, bf16[256,128,128]{2,1,0:T(8,128)(2,1)S(1)} %get-tuple-element.76.w_ref, bf16[64,192,128]{2,1,0:T(8,128)(2,1)S(1)} %get-tuple-element.79.s_ref), custom_call_target="tpu_custom_call" | custom-call | tf_op jit(solution)/shard_map/pallas_call | solution.py:353
  80.5 3.3 %collective-permute-done.20 = bf16[16,128,128]{2,1,0:T(8,128)(2,1)S(1)} collective-permute-done((bf16[16,128,128]{2,1,0:T(8,128)(2,1)S(1)}, bf16[16,128,128]{2,1,0:T(8,128)(2,1)S(1)}, u32[]{:S(2)}, u32[]{:S(2)}) %collective-permute-start.20) | collective-permute-done | bytes 524320 | tf_op jit(solution)/shard_map/ppermute | solution.py:225
  83.8 1.3 collective-permute-done.21
  85.2 1.4 collective-permute-done.23
  86.9 1.5 %collective-permute-start.25 = (bf16[8,128,128]{2,1,0:T(8,128)(2,1)S(1)}, bf16[8,128,128]{2,1,0:T(8,128)(2,1)S(1)}, u32[]{:S(2)}, u32[]{:S(2)}) collective-permute-start(bf16[8,128,128]{2,1,0:T(8,128)(2,1)S(1)} %add_convert_fusion.2), channel_id=1, source_target_pairs={{0,4},{4,0},{8,12},{12,8},{1,5},{5,1},{9,13},{13,9},{2,6},{6,2},{1... | collective-permute-start | bytes 786440 | tf_op jit(solution)/shard_map/ppermute | solution.py:225
  88.5 2.3 %collective-permute-start.29 = (bf16[8,128,128]{2,1,0:T(8,128)(2,1)S(1)}, bf16[8,128,128]{2,1,0:T(8,128)(2,1)S(1)}, u32[]{:S(2)}, u32[]{:S(2)}) collective-permute-start(bf16[8,128,128]{2,1,0:T(8,128)(2,1)S(1)} %add_convert_fusion.1), channel_id=1, source_target_pairs={{0,48},{16,32},{32,16},{48,0},{1,49},{17,33},{33,17},{49,1},{2,50}... | collective-permute-start | bytes 786440 | tf_op jit(solution)/shard_map/ppermute | solution.py:225
  90.9 2.4 %collective-permute-start.24 = (bf16[8,128,128]{2,1,0:T(8,128)(2,1)S(1)}, bf16[8,128,128]{2,1,0:T(8,128)(2,1)S(1)}, u32[]{:S(2)}, u32[]{:S(2)}) collective-permute-start(bf16[8,128,128]{2,1,0:T(8,128)(2,1)S(1)} %add_convert_fusion.3), channel_id=1, source_target_pairs={{0,12},{4,8},{8,4},{12,0},{1,13},{5,9},{9,5},{13,1},{2,14},{6,10},... | collective-permute-start | bytes 786440 | tf_op jit(solution)/shard_map/ppermute | solution.py:225
  93.3 1.2 collective-permute-done.25
  94.6 4.1 %collective-permute-done.24 = bf16[8,128,128]{2,1,0:T(8,128)(2,1)S(1)} collective-permute-done((bf16[8,128,128]{2,1,0:T(8,128)(2,1)S(1)}, bf16[8,128,128]{2,1,0:T(8,128)(2,1)S(1)}, u32[]{:S(2)}, u32[]{:S(2)}) %collective-permute-start.24) | collective-permute-done | bytes 262176 | tf_op jit(solution)/shard_map/ppermute | solution.py:225
  98.9 1.3 collective-permute-start.26
  100.2 1.3 collective-permute-start.28
  101.5 2.2 %collective-permute-start.27 = (bf16[4,128,128]{2,1,0:T(8,128)(2,1)S(1)}, bf16[4,128,128]{2,1,0:T(8,128)(2,1)S(1)}, u32[]{:S(2)}, u32[]{:S(2)}) collective-permute-start(bf16[4,128,128]{2,1,0:T(8,128)(2,1)S(1)} %get-tuple-element.117), channel_id=1, source_target_pairs={{0,48},{16,32},{32,16},{48,0},{1,49},{17,33},{33,17},{49,1},{2,50}... | collective-permute-start | bytes 393224 | tf_op jit(solution)/shard_map/ppermute | solution.py:225
  104.0 2.7 %collective-permute-done.28 = bf16[4,128,128]{2,1,0:T(8,128)(2,1)S(1)} collective-permute-done((bf16[4,128,128]{2,1,0:T(8,128)(2,1)S(1)}, bf16[4,128,128]{2,1,0:T(8,128)(2,1)S(1)}, u32[]{:S(2)}, u32[]{:S(2)}) %collective-permute-start.28) | collective-permute-done | bytes 131104 | tf_op jit(solution)/shard_map/ppermute | solution.py:225
  106.7 1.4 collective-permute-done.27
  108.8 3.8 %collective-permute-start.33 = (bf16[4,128,128]{2,1,0:T(8,128)(2,1)S(1)}, bf16[4,128,128]{2,1,0:T(8,128)(2,1)S(1)}, u32[]{:S(2)}, u32[]{:S(2)}) collective-permute-start(bf16[4,128,128]{2,1,0:T(8,128)(2,1)S(1)} %get-tuple-element.113), channel_id=1, source_target_pairs={{0,8},{4,12},{8,0},{12,4},{1,9},{5,13},{9,1},{13,5},{2,10},{6,14},... | collective-permute-start | bytes 393224 | tf_op jit(solution)/shard_map/ppermute | solution.py:225
  113.7 3.2 %collective-permute-done.33 = bf16[4,128,128]{2,1,0:T(8,128)(2,1)S(1)} collective-permute-done((bf16[4,128,128]{2,1,0:T(8,128)(2,1)S(1)}, bf16[4,128,128]{2,1,0:T(8,128)(2,1)S(1)}, u32[]{:S(2)}, u32[]{:S(2)}) %collective-permute-start.33) | collective-permute-done | bytes 131104 | tf_op jit(solution)/shard_map/ppermute | solution.py:225
  116.9 1.8 %collective-permute-done.32 = bf16[4,128,128]{2,1,0:T(8,128)(2,1)S(1)} collective-permute-done((bf16[4,128,128]{2,1,0:T(8,128)(2,1)S(1)}, bf16[4,128,128]{2,1,0:T(8,128)(2,1)S(1)}, u32[]{:S(2)}, u32[]{:S(2)}) %collective-permute-start.32) | collective-permute-done | bytes 131104 | tf_op jit(solution)/shard_map/ppermute | solution.py:225
  118.8 2.2 %collective-permute-start.37 = (bf16[4,128,128]{2,1,0:T(8,128)(2,1)S(1)}, bf16[4,128,128]{2,1,0:T(8,128)(2,1)S(1)}, u32[]{:S(2)}, u32[]{:S(2)}) collective-permute-start(bf16[4,128,128]{2,1,0:T(8,128)(2,1)S(1)} %fusion.7.a), channel_id=1, source_target_pairs={{0,192},{64,128},{128,64},{192,0},{1,193},{65,129},{129,65},{193,1... | collective-permute-start | bytes 393224 | tf_op jit(solution)/shard_map/ppermute | solution.py:225
  121.0 4.3 %collective-permute-start.36 = (bf16[4,128,128]{2,1,0:T(8,128)(2,1)S(1)}, bf16[4,128,128]{2,1,0:T(8,128)(2,1)S(1)}, u32[]{:S(2)}, u32[]{:S(2)}) collective-permute-start(bf16[4,128,128]{2,1,0:T(8,128)(2,1)S(1)} %fusion.7.a), channel_id=1, source_target_pairs={{0,128},{64,192},{128,0},{192,64},{1,129},{65,193},{129,1},{193,65... | collective-permute-start | bytes 393224 | tf_op jit(solution)/shard_map/ppermute | solution.py:225
  125.4 5.0 %collective-permute-done.37.d = bf16[4,128,128]{2,1,0:T(8,128)(2,1)S(1)} collective-permute-done((bf16[4,128,128]{2,1,0:T(8,128)(2,1)S(1)}, bf16[4,128,128]{2,1,0:T(8,128)(2,1)S(1)}, u32[]{:S(2)}, u32[]{:S(2)}) %collective-permute-start.37) | collective-permute-done | bytes 131104 | tf_op jit(solution)/shard_map/ppermute | solution.py:225
  131.0 1.6 %collective-permute-done.35.b = bf16[4,128,128]{2,1,0:T(8,128)(2,1)S(1)} collective-permute-done((bf16[4,128,128]{2,1,0:T(8,128)(2,1)S(1)}, bf16[4,128,128]{2,1,0:T(8,128)(2,1)S(1)}, u32[]{:S(2)}, u32[]{:S(2)}) %collective-permute-start.35) | collective-permute-done | bytes 131104 | tf_op jit(solution)/shard_map/ppermute | solution.py:225
  132.9 1.7 %collective-permute-start.40 = (bf16[4,128,128]{2,1,0:T(8,128)(2,1)S(1)}, bf16[4,128,128]{2,1,0:T(8,128)(2,1)S(1)}, u32[]{:S(2)}, u32[]{:S(2)}) collective-permute-start(bf16[4,128,128]{2,1,0:T(8,128)(2,1)S(1)} %shard_map.76.refs_0_), channel_id=1, source_target_pairs={{0,48},{16,32},{32,16},{48,0},{1,49},{17,33},{33,17},{49,1},{2,50}... | collective-permute-start | bytes 393224 | tf_op jit(solution)/shard_map/ppermute | solution.py:225
  135.5 1.6 %collective-permute-start.38 = (bf16[4,128,128]{2,1,0:T(8,128)(2,1)S(1)}, bf16[4,128,128]{2,1,0:T(8,128)(2,1)S(1)}, u32[]{:S(2)}, u32[]{:S(2)}) collective-permute-start(bf16[4,128,128]{2,1,0:T(8,128)(2,1)S(1)} %shard_map.76.refs_0_), channel_id=1, source_target_pairs={{0,16},{16,0},{32,48},{48,32},{1,17},{17,1},{33,49},{49,33},{2,18}... | collective-permute-start | bytes 393224 | tf_op jit(solution)/shard_map/ppermute | solution.py:225
  137.1 4.2 %shard_map.75 = bf16[192,8192]{1,0:T(8,128)(2,1)} custom-call(s32[256]{0:T(256)S(1)} %select_reduce_fusion.place, s32[64]{0:T(128)S(1)} %xor.28.blocks, bf16[192,8192]{1,0:T(8,128)(2,1)S(1)} %get-tuple-element.62.g_ref, bf16[256,128,128]{2,1,0:T(8,128)(2,1)S(1)} %get-tuple-element.76.w_ref, ...), custom_call_target="tpu_custom_call", output_to_operand_aliasing={{}: (5, {})} | custom-call | tf_op jit(solution)/shard_map/pallas_call | solution.py:357
  141.4 1.6 %shard_map.77 = f32[16,128,128]{2,1,0:T(8,128)} custom-call(s32[4]{0:T(128)S(1)} %pad_add_fusion.1.where, bf16[4,128,128]{2,1,0:T(8,128)(2,1)S(1)} %shard_map.76.refs_0_, bf16[4,128,128]{2,1,0:T(8,128)(2,1)S(1)} %collective-permute-done.38.refs_1_, bf16[4,128,128]{2,1,0:T(8,128)(2,1)S(1)} %collective-permute-done.39.refs_2_, ...), custom_call_target="tpu_custom_call" | custom-call | tf_op jit(solution)/shard_map/pallas_call | solution.py:391
  (94 shorter events, 16.0 us)
Async XLA Ops:
  0.6 18.4 %collective-permute-start.3 = (bf16[192,8192]{1,0:T(8,128)(2,1)}, bf16[192,8192]{1,0:T(8,128)(2,1)S(1)}, u32[]{:S(2)}, u32[]{:S(2)}) collective-permute-start(bf16[192,8192]{1,0:T(8,128)(2,1)} %x_hbm.1), channel_id=1, source_target_pairs={{0,1},{1,0},{2,3},{3,2},{4,5},{5,4},{6,7},{7,6},{8,9},{9,8},{10,11... | collective-permute-start | bytes 9437192 | tf_op jit(solution)/shard_map/ppermute | solution.py:225
  0.7 14.7 %collective-permute-start.2 = (bf16[16,128,128]{2,1,0:T(8,128)(2,1)}, bf16[16,128,128]{2,1,0:T(8,128)(2,1)}, u32[]{:S(2)}, u32[]{:S(2)}) collective-permute-start(bf16[16,128,128]{2,1,0:T(8,128)(2,1)} %refs_0_.1), channel_id=1, source_target_pairs={{0,2},{2,0},{1,3},{3,1},{4,6},{6,4},{5,7},{7,5},{8,10},{10,8},{9,1... | collective-permute-start | bytes 1572872 | tf_op jit(solution)/shard_map/ppermute | solution.py:225
  2.7 14.3 %collective-permute-start.1 = (bf16[16,128,128]{2,1,0:T(8,128)(2,1)}, bf16[16,128,128]{2,1,0:T(8,128)(2,1)}, u32[]{:S(2)}, u32[]{:S(2)}) collective-permute-start(bf16[16,128,128]{2,1,0:T(8,128)(2,1)} %refs_0_.1), channel_id=1, source_target_pairs={{0,12},{4,0},{8,4},{12,8},{1,13},{5,1},{9,5},{13,9},{2,14},{6,2},{... | collective-permute-start | bytes 1572872 | tf_op jit(solution)/shard_map/ppermute | solution.py:231
  3.7 15.4 %collective-permute-start = (bf16[16,128,128]{2,1,0:T(8,128)(2,1)}, bf16[16,128,128]{2,1,0:T(8,128)(2,1)}, u32[]{:S(2)}, u32[]{:S(2)}) collective-permute-start(bf16[16,128,128]{2,1,0:T(8,128)(2,1)} %refs_0_.1), channel_id=1, source_target_pairs={{0,4},{4,8},{8,12},{12,0},{1,5},{5,9},{9,13},{13,1},{2,6},{6,10},{... | collective-permute-start | bytes 1572872 | tf_op jit(solution)/shard_map/ppermute | solution.py:231
  4.7 14.4 %collective-permute-start.4 = (bf16[16,128,128]{2,1,0:T(8,128)(2,1)}, bf16[16,128,128]{2,1,0:T(8,128)(2,1)}, u32[]{:S(2)}, u32[]{:S(2)}) collective-permute-start(bf16[16,128,128]{2,1,0:T(8,128)(2,1)} %refs_0_.1), channel_id=1, source_target_pairs={{0,1},{1,0},{2,3},{3,2},{4,5},{5,4},{6,7},{7,6},{8,9},{9,8},{10,11... | collective-permute-start | bytes 1572872 | tf_op jit(solution)/shard_map/ppermute | solution.py:225
  19.1 17.0 %collective-permute-start.9 = (bf16[16,128,128]{2,1,0:T(8,128)(2,1)}, bf16[16,128,128]{2,1,0:T(8,128)(2,1)}, u32[]{:S(2)}, u32[]{:S(2)}) collective-permute-start(bf16[16,128,128]{2,1,0:T(8,128)(2,1)} %collective-permute-done.refs_1_), channel_id=1, source_target_pairs={{0,1},{1,0},{2,3},{3,2},{4,5},{5,4},{6,7},{7,6},{8,9},{9,8},{10,11... | collective-permute-start | bytes 1572872 | tf_op jit(solution)/shard_map/ppermute | solution.py:225
  19.1 17.0 %collective-permute-start.5 = (bf16[16,128,128]{2,1,0:T(8,128)(2,1)}, bf16[16,128,128]{2,1,0:T(8,128)(2,1)}, u32[]{:S(2)}, u32[]{:S(2)}) collective-permute-start(bf16[16,128,128]{2,1,0:T(8,128)(2,1)} %collective-permute-done.refs_1_), channel_id=1, source_target_pairs={{0,2},{2,64},{64,66},{66,128},{128,130},{130,192},{192,194},{194,0... | collective-permute-start | bytes 1572872 | tf_op jit(solution)/shard_map/ppermute | solution.py:231
  22.7 14.3 %collective-permute-start.6 = (bf16[16,128,128]{2,1,0:T(8,128)(2,1)}, bf16[16,128,128]{2,1,0:T(8,128)(2,1)}, u32[]{:S(2)}, u32[]{:S(2)}) collective-permute-start(bf16[16,128,128]{2,1,0:T(8,128)(2,1)} %collective-permute-done.1.refs_2_), channel_id=1, source_target_pairs={{0,194},{2,0},{64,2},{66,64},{128,66},{130,128},{192,130},{194,192... | collective-permute-start | bytes 1572872 | tf_op jit(solution)/shard_map/ppermute | solution.py:231
  26.1 8.6 %collective-permute-start.8 = (bf16[8,128,128]{2,1,0:T(8,128)(2,1)}, bf16[8,128,128]{2,1,0:T(8,128)(2,1)S(1)}, u32[]{:S(2)}, u32[]{:S(2)}) collective-permute-start(bf16[8,128,128]{2,1,0:T(8,128)(2,1)} %slice.61), channel_id=1, source_target_pairs={{0,12},{4,0},{8,4},{12,8},{1,13},{5,1},{9,5},{13,9},{2,14},{6,2},{... | collective-permute-start | bytes 786440 | tf_op jit(solution)/shard_map/ppermute | solution.py:231
  26.5 9.6 %collective-permute-start.7 = (bf16[8,128,128]{2,1,0:T(8,128)(2,1)}, bf16[8,128,128]{2,1,0:T(8,128)(2,1)}, u32[]{:S(2)}, u32[]{:S(2)}) collective-permute-start(bf16[8,128,128]{2,1,0:T(8,128)(2,1)} %slice.60), channel_id=1, source_target_pairs={{0,4},{4,8},{8,12},{12,0},{1,5},{5,9},{9,13},{13,1},{2,6},{6,10},{... | collective-permute-start | bytes 786440 | tf_op jit(solution)/shard_map/ppermute | solution.py:231
  34.7 7.1 %copy-start.2 = (bf16[8,128,128]{2,1,0:T(8,128)(2,1)}, bf16[8,128,128]{2,1,0:T(8,128)(2,1)S(1)}, u32[]{:S(2)}) copy-start(bf16[8,128,128]{2,1,0:T(8,128)(2,1)S(1)} %collective-permute-done.8.refs_3_) | copy-start | bytes 786436
  38.0 3.1 %collective-permute-start.14 = (bf16[16,128,128]{2,1,0:T(8,128)(2,1)S(1)}, bf16[16,128,128]{2,1,0:T(8,128)(2,1)S(1)}, u32[]{:S(2)}, u32[]{:S(2)}) collective-permute-start(bf16[16,128,128]{2,1,0:T(8,128)(2,1)S(1)} %pad_maximum_fusion.2), channel_id=1, source_target_pairs={{0,1},{1,0},{2,3},{3,2},{4,5},{5,4},{6,7},{7,6},{8,9},{9,8},{10,11... | collective-permute-start | bytes 1572872 | tf_op jit(solution)/shard_map/ppermute | solution.py:225
  38.1 3.3 %collective-permute-start.12 = (bf16[16,128,128]{2,1,0:T(8,128)(2,1)}, bf16[16,128,128]{2,1,0:T(8,128)(2,1)S(1)}, u32[]{:S(2)}, u32[]{:S(2)}) collective-permute-start(bf16[16,128,128]{2,1,0:T(8,128)(2,1)} %collective-permute-done.1.refs_2_), channel_id=1, source_target_pairs={{0,1},{1,0},{2,3},{3,2},{4,5},{5,4},{6,7},{7,6},{8,9},{9,8},{10,11... | collective-permute-start | bytes 1572872 | tf_op jit(solution)/shard_map/ppermute | solution.py:225
  38.6 3.1 %collective-permute-start.13 = (bf16[16,128,128]{2,1,0:T(8,128)(2,1)}, bf16[16,128,128]{2,1,0:T(8,128)(2,1)S(1)}, u32[]{:S(2)}, u32[]{:S(2)}) collective-permute-start(bf16[16,128,128]{2,1,0:T(8,128)(2,1)} %collective-permute-done.2.refs_3_), channel_id=1, source_target_pairs={{0,1},{1,0},{2,3},{3,2},{4,5},{5,4},{6,7},{7,6},{8,9},{9,8},{10,11... | collective-permute-start | bytes 1572872 | tf_op jit(solution)/shard_map/ppermute | solution.py:225
  38.7 9.3 %collective-permute-start.10 = (bf16[8,128,128]{2,1,0:T(8,128)(2,1)}, bf16[8,128,128]{2,1,0:T(8,128)(2,1)S(1)}, u32[]{:S(2)}, u32[]{:S(2)}) collective-permute-start(bf16[8,128,128]{2,1,0:T(8,128)(2,1)} %collective-permute-done.7.refs_2_), channel_id=1, source_target_pairs={{0,2},{2,64},{64,66},{66,128},{128,130},{130,192},{192,194},{194,0... | collective-permute-start | bytes 786440 | tf_op jit(solution)/shard_map/ppermute | solution.py:231
  41.1 9.6 %collective-permute-start.11 = (bf16[8,128,128]{2,1,0:T(8,128)(2,1)S(1)}, bf16[8,128,128]{2,1,0:T(8,128)(2,1)S(1)}, u32[]{:S(2)}, u32[]{:S(2)}) collective-permute-start(bf16[8,128,128]{2,1,0:T(8,128)(2,1)S(1)} %collective-permute-done.8.refs_3_), channel_id=1, source_target_pairs={{0,194},{2,0},{64,2},{66,64},{128,66},{130,128},{192,130},{194,192... | collective-permute-start | bytes 786440 | tf_op jit(solution)/shard_map/ppermute | solution.py:231
  41.1 10.1 %collective-permute-start.15 = (bf16[16,128,128]{2,1,0:T(8,128)(2,1)}, bf16[16,128,128]{2,1,0:T(8,128)(2,1)S(1)}, u32[]{:S(2)}, u32[]{:S(2)}) collective-permute-start(bf16[16,128,128]{2,1,0:T(8,128)(2,1)} %collective-permute-done.5.refs_0_), channel_id=1, source_target_pairs={{0,1},{1,0},{2,3},{3,2},{4,5},{5,4},{6,7},{7,6},{8,9},{9,8},{10,11... | collective-permute-start | bytes 1572872 | tf_op jit(solution)/shard_map/ppermute | solution.py:225
  41.4 9.8 %collective-permute-start.16 = (bf16[16,128,128]{2,1,0:T(8,128)(2,1)}, bf16[16,128,128]{2,1,0:T(8,128)(2,1)S(1)}, u32[]{:S(2)}, u32[]{:S(2)}) collective-permute-start(bf16[16,128,128]{2,1,0:T(8,128)(2,1)} %collective-permute-done.6.refs_1_), channel_id=1, source_target_pairs={{0,1},{1,0},{2,3},{3,2},{4,5},{5,4},{6,7},{7,6},{8,9},{9,8},{10,11... | collective-permute-start | bytes 1572872 | tf_op jit(solution)/shard_map/ppermute | solution.py:225
  48.0 4.6 %copy-start.8 = (bf16[8,128,128]{2,1,0:T(8,128)(2,1)}, bf16[8,128,128]{2,1,0:T(8,128)(2,1)S(1)}, u32[]{:S(2)}) copy-start(bf16[8,128,128]{2,1,0:T(8,128)(2,1)S(1)} %collective-permute-done.10.refs_0_) | copy-start | bytes 786436
  50.7 1.9 %copy-start.9 = (bf16[8,128,128]{2,1,0:T(8,128)(2,1)}, bf16[8,128,128]{2,1,0:T(8,128)(2,1)S(1)}, u32[]{:S(2)}) copy-start(bf16[8,128,128]{2,1,0:T(8,128)(2,1)S(1)} %collective-permute-done.11.refs_1_) | copy-start | bytes 786436
  50.7 1.5 %collective-permute-start.17 = (bf16[8,128,128]{2,1,0:T(8,128)(2,1)S(1)}, bf16[8,128,128]{2,1,0:T(8,128)(2,1)S(1)}, u32[]{:S(2)}, u32[]{:S(2)}) collective-permute-start(bf16[8,128,128]{2,1,0:T(8,128)(2,1)S(1)} %collective-permute-done.10.refs_0_), channel_id=1, source_target_pairs={{0,1},{1,0},{2,3},{3,2},{4,5},{5,4},{6,7},{7,6},{8,9},{9,8},{10,11... | collective-permute-start | bytes 786440 | tf_op jit(solution)/shard_map/ppermute | solution.py:225
  50.7 1.9 %collective-permute-start.18 = (bf16[8,128,128]{2,1,0:T(8,128)(2,1)S(1)}, bf16[8,128,128]{2,1,0:T(8,128)(2,1)S(1)}, u32[]{:S(2)}, u32[]{:S(2)}) collective-permute-start(bf16[8,128,128]{2,1,0:T(8,128)(2,1)S(1)} %collective-permute-done.11.refs_1_), channel_id=1, source_target_pairs={{0,1},{1,0},{2,3},{3,2},{4,5},{5,4},{6,7},{7,6},{8,9},{9,8},{10,11... | collective-permute-start | bytes 786440 | tf_op jit(solution)/shard_map/ppermute | solution.py:225
  51.2 1.4 copy-start.3
  51.2 1.4 copy-start.4
  61.0 6.0 %copy-start = (s32[256]{0:T(256)S(1)}, s32[256]{0:T(256)}, u32[]{:S(2)}) copy-start(s32[256]{0:T(256)} %rows.3) | copy-start | bytes 3076
  61.0 6.0 %copy-start.1 = (s32[256]{0:T(256)S(1)}, s32[256]{0:T(256)}, u32[]{:S(2)}) copy-start(s32[256]{0:T(256)} %cols.3) | copy-start | bytes 3076
  61.1 6.0 %collective-permute-start.19 = (bf16[64,192,128]{2,1,0:T(8,128)(2,1)S(1)}, bf16[64,192,128]{2,1,0:T(8,128)(2,1)S(1)}, u32[]{:S(2)}, u32[]{:S(2)}) collective-permute-start(bf16[64,192,128]{2,1,0:T(8,128)(2,1)S(1)} %get-tuple-element.79.s_ref), channel_id=1, source_target_pairs={{0,1},{1,0},{2,3},{3,2},{4,5},{5,4},{6,7},{7,6},{8,9},{9,8},{10,11... | collective-permute-start | bytes 9437192 | tf_op jit(solution)/shard_map/ppermute | solution.py:225
  69.5 14.3 %collective-permute-start.20 = (bf16[16,128,128]{2,1,0:T(8,128)(2,1)S(1)}, bf16[16,128,128]{2,1,0:T(8,128)(2,1)S(1)}, u32[]{:S(2)}, u32[]{:S(2)}) collective-permute-start(bf16[16,128,128]{2,1,0:T(8,128)(2,1)S(1)} %get-tuple-element.81), channel_id=1, source_target_pairs={{0,4},{4,0},{8,12},{12,8},{1,5},{5,1},{9,13},{13,9},{2,6},{6,2},{1... | collective-permute-start | bytes 1572872 | tf_op jit(solution)/shard_map/ppermute | solution.py:225
  69.6 15.5 %collective-permute-start.21 = (bf16[16,128,128]{2,1,0:T(8,128)(2,1)S(1)}, bf16[16,128,128]{2,1,0:T(8,128)(2,1)S(1)}, u32[]{:S(2)}, u32[]{:S(2)}) collective-permute-start(bf16[16,128,128]{2,1,0:T(8,128)(2,1)S(1)} %get-tuple-element.82), channel_id=1, source_target_pairs={{0,12},{4,8},{8,4},{12,0},{1,13},{5,9},{9,5},{13,1},{2,14},{6,10},... | collective-permute-start | bytes 1572872 | tf_op jit(solution)/shard_map/ppermute | solution.py:225
  70.1 15.0 %collective-permute-start.22 = (bf16[16,128,128]{2,1,0:T(8,128)(2,1)S(1)}, bf16[16,128,128]{2,1,0:T(8,128)(2,1)S(1)}, u32[]{:S(2)}, u32[]{:S(2)}) collective-permute-start(bf16[16,128,128]{2,1,0:T(8,128)(2,1)S(1)} %get-tuple-element.83), channel_id=1, source_target_pairs={{0,16},{16,0},{32,48},{48,32},{1,17},{17,1},{33,49},{49,33},{2,18}... | collective-permute-start | bytes 1572872 | tf_op jit(solution)/shard_map/ppermute | solution.py:225
  71.7 14.8 %collective-permute-start.23 = (bf16[16,128,128]{2,1,0:T(8,128)(2,1)S(1)}, bf16[16,128,128]{2,1,0:T(8,128)(2,1)S(1)}, u32[]{:S(2)}, u32[]{:S(2)}) collective-permute-start(bf16[16,128,128]{2,1,0:T(8,128)(2,1)S(1)} %get-tuple-element.84), channel_id=1, source_target_pairs={{0,48},{16,32},{32,16},{48,0},{1,49},{17,33},{33,17},{49,1},{2,50}... | collective-permute-start | bytes 1572872 | tf_op jit(solution)/shard_map/ppermute | solution.py:225
  86.6 17.1 %collective-permute-start.30 = (bf16[8,128,128]{2,1,0:T(8,128)(2,1)S(1)}, bf16[8,128,128]{2,1,0:T(8,128)(2,1)S(1)}, u32[]{:S(2)}, u32[]{:S(2)}) collective-permute-start(bf16[8,128,128]{2,1,0:T(8,128)(2,1)S(1)} %add_convert_fusion), channel_id=1, source_target_pairs={{0,16},{16,0},{32,48},{48,32},{1,17},{17,1},{33,49},{49,33},{2,18}... | collective-permute-start | bytes 786440 | tf_op jit(solution)/shard_map/ppermute | solution.py:225
  86.9 7.6 %collective-permute-start.25 = (bf16[8,128,128]{2,1,0:T(8,128)(2,1)S(1)}, bf16[8,128,128]{2,1,0:T(8,128)(2,1)S(1)}, u32[]{:S(2)}, u32[]{:S(2)}) collective-permute-start(bf16[8,128,128]{2,1,0:T(8,128)(2,1)S(1)} %add_convert_fusion.2), channel_id=1, source_target_pairs={{0,4},{4,0},{8,12},{12,8},{1,5},{5,1},{9,13},{13,9},{2,6},{6,2},{1... | collective-permute-start | bytes 786440 | tf_op jit(solution)/shard_map/ppermute | solution.py:225
  88.5 15.3 %collective-permute-start.29 = (bf16[8,128,128]{2,1,0:T(8,128)(2,1)S(1)}, bf16[8,128,128]{2,1,0:T(8,128)(2,1)S(1)}, u32[]{:S(2)}, u32[]{:S(2)}) collective-permute-start(bf16[8,128,128]{2,1,0:T(8,128)(2,1)S(1)} %add_convert_fusion.1), channel_id=1, source_target_pairs={{0,48},{16,32},{32,16},{48,0},{1,49},{17,33},{33,17},{49,1},{2,50}... | collective-permute-start | bytes 786440 | tf_op jit(solution)/shard_map/ppermute | solution.py:225
  90.9 7.8 %collective-permute-start.24 = (bf16[8,128,128]{2,1,0:T(8,128)(2,1)S(1)}, bf16[8,128,128]{2,1,0:T(8,128)(2,1)S(1)}, u32[]{:S(2)}, u32[]{:S(2)}) collective-permute-start(bf16[8,128,128]{2,1,0:T(8,128)(2,1)S(1)} %add_convert_fusion.3), channel_id=1, source_target_pairs={{0,12},{4,8},{8,4},{12,0},{1,13},{5,9},{9,5},{13,1},{2,14},{6,10},... | collective-permute-start | bytes 786440 | tf_op jit(solution)/shard_map/ppermute | solution.py:225
  98.9 5.1 %collective-permute-start.26 = (bf16[4,128,128]{2,1,0:T(8,128)(2,1)S(1)}, bf16[4,128,128]{2,1,0:T(8,128)(2,1)S(1)}, u32[]{:S(2)}, u32[]{:S(2)}) collective-permute-start(bf16[4,128,128]{2,1,0:T(8,128)(2,1)S(1)} %get-tuple-element.115), channel_id=1, source_target_pairs={{0,16},{16,0},{32,48},{48,32},{1,17},{17,1},{33,49},{49,33},{2,18}... | collective-permute-start | bytes 393224 | tf_op jit(solution)/shard_map/ppermute | solution.py:225
  100.2 6.5 %collective-permute-start.28 = (bf16[4,128,128]{2,1,0:T(8,128)(2,1)S(1)}, bf16[4,128,128]{2,1,0:T(8,128)(2,1)S(1)}, u32[]{:S(2)}, u32[]{:S(2)}) collective-permute-start(bf16[4,128,128]{2,1,0:T(8,128)(2,1)S(1)} %get-tuple-element.116), channel_id=1, source_target_pairs={{0,32},{16,48},{32,0},{48,16},{1,33},{17,49},{33,1},{49,17},{2,34}... | collective-permute-start | bytes 393224 | tf_op jit(solution)/shard_map/ppermute | solution.py:225
  101.5 6.6 %collective-permute-start.27 = (bf16[4,128,128]{2,1,0:T(8,128)(2,1)S(1)}, bf16[4,128,128]{2,1,0:T(8,128)(2,1)S(1)}, u32[]{:S(2)}, u32[]{:S(2)}) collective-permute-start(bf16[4,128,128]{2,1,0:T(8,128)(2,1)S(1)} %get-tuple-element.117), channel_id=1, source_target_pairs={{0,48},{16,32},{32,16},{48,0},{1,49},{17,33},{33,17},{49,1},{2,50}... | collective-permute-start | bytes 393224 | tf_op jit(solution)/shard_map/ppermute | solution.py:225
  108.1 10.6 %collective-permute-start.34 = (f32[4,128,128]{2,1,0:T(8,128)S(1)}, f32[4,128,128]{2,1,0:T(8,128)S(1)}, u32[]{:S(2)}, u32[]{:S(2)}) collective-permute-start(f32[4,128,128]{2,1,0:T(8,128)S(1)} %fusion.4), channel_id=1, source_target_pairs={{0,2},{2,0},{1,3},{3,1},{4,6},{6,4},{5,7},{7,5},{8,10},{10,8},{9,1... | collective-permute-start | bytes 786440 | tf_op jit(solution)/shard_map/ppermute | solution.py:225
  108.7 5.1 %collective-permute-start.31 = (bf16[4,128,128]{2,1,0:T(8,128)(2,1)S(1)}, bf16[4,128,128]{2,1,0:T(8,128)(2,1)S(1)}, u32[]{:S(2)}, u32[]{:S(2)}) collective-permute-start(bf16[4,128,128]{2,1,0:T(8,128)(2,1)S(1)} %get-tuple-element.112), channel_id=1, source_target_pairs={{0,4},{4,0},{8,12},{12,8},{1,5},{5,1},{9,13},{13,9},{2,6},{6,2},{1... | collective-permute-start | bytes 393224 | tf_op jit(solution)/shard_map/ppermute | solution.py:225
  108.8 8.1 %collective-permute-start.33 = (bf16[4,128,128]{2,1,0:T(8,128)(2,1)S(1)}, bf16[4,128,128]{2,1,0:T(8,128)(2,1)S(1)}, u32[]{:S(2)}, u32[]{:S(2)}) collective-permute-start(bf16[4,128,128]{2,1,0:T(8,128)(2,1)S(1)} %get-tuple-element.113), channel_id=1, source_target_pairs={{0,8},{4,12},{8,0},{12,4},{1,9},{5,13},{9,1},{13,5},{2,10},{6,14},... | collective-permute-start | bytes 393224 | tf_op jit(solution)/shard_map/ppermute | solution.py:225
  112.6 6.2 %collective-permute-start.32 = (bf16[4,128,128]{2,1,0:T(8,128)(2,1)S(1)}, bf16[4,128,128]{2,1,0:T(8,128)(2,1)S(1)}, u32[]{:S(2)}, u32[]{:S(2)}) collective-permute-start(bf16[4,128,128]{2,1,0:T(8,128)(2,1)S(1)} %get-tuple-element.114), channel_id=1, source_target_pairs={{0,12},{4,8},{8,4},{12,0},{1,13},{5,9},{9,5},{13,1},{2,14},{6,10},... | collective-permute-start | bytes 393224 | tf_op jit(solution)/shard_map/ppermute | solution.py:225
  118.8 11.6 %collective-permute-start.37 = (bf16[4,128,128]{2,1,0:T(8,128)(2,1)S(1)}, bf16[4,128,128]{2,1,0:T(8,128)(2,1)S(1)}, u32[]{:S(2)}, u32[]{:S(2)}) collective-permute-start(bf16[4,128,128]{2,1,0:T(8,128)(2,1)S(1)} %fusion.7.a), channel_id=1, source_target_pairs={{0,192},{64,128},{128,64},{192,0},{1,193},{65,129},{129,65},{193,1... | collective-permute-start | bytes 393224 | tf_op jit(solution)/shard_map/ppermute | solution.py:225
  121.0 9.9 %collective-permute-start.36 = (bf16[4,128,128]{2,1,0:T(8,128)(2,1)S(1)}, bf16[4,128,128]{2,1,0:T(8,128)(2,1)S(1)}, u32[]{:S(2)}, u32[]{:S(2)}) collective-permute-start(bf16[4,128,128]{2,1,0:T(8,128)(2,1)S(1)} %fusion.7.a), channel_id=1, source_target_pairs={{0,128},{64,192},{128,0},{192,64},{1,129},{65,193},{129,1},{193,65... | collective-permute-start | bytes 393224 | tf_op jit(solution)/shard_map/ppermute | solution.py:225
  125.4 7.2 %collective-permute-start.35 = (bf16[4,128,128]{2,1,0:T(8,128)(2,1)S(1)}, bf16[4,128,128]{2,1,0:T(8,128)(2,1)S(1)}, u32[]{:S(2)}, u32[]{:S(2)}) collective-permute-start(bf16[4,128,128]{2,1,0:T(8,128)(2,1)S(1)} %fusion.7.a), channel_id=1, source_target_pairs={{0,64},{64,0},{128,192},{192,128},{1,65},{65,1},{129,193},{193,129... | collective-permute-start | bytes 393224 | tf_op jit(solution)/shard_map/ppermute | solution.py:225
  132.9 8.4 %collective-permute-start.40 = (bf16[4,128,128]{2,1,0:T(8,128)(2,1)S(1)}, bf16[4,128,128]{2,1,0:T(8,128)(2,1)S(1)}, u32[]{:S(2)}, u32[]{:S(2)}) collective-permute-start(bf16[4,128,128]{2,1,0:T(8,128)(2,1)S(1)} %shard_map.76.refs_0_), channel_id=1, source_target_pairs={{0,48},{16,32},{32,16},{48,0},{1,49},{17,33},{33,17},{49,1},{2,50}... | collective-permute-start | bytes 393224 | tf_op jit(solution)/shard_map/ppermute | solution.py:225
  134.7 6.7 %collective-permute-start.39 = (bf16[4,128,128]{2,1,0:T(8,128)(2,1)S(1)}, bf16[4,128,128]{2,1,0:T(8,128)(2,1)S(1)}, u32[]{:S(2)}, u32[]{:S(2)}) collective-permute-start(bf16[4,128,128]{2,1,0:T(8,128)(2,1)S(1)} %shard_map.76.refs_0_), channel_id=1, source_target_pairs={{0,32},{16,48},{32,0},{48,16},{1,33},{17,49},{33,1},{49,17},{2,34}... | collective-permute-start | bytes 393224 | tf_op jit(solution)/shard_map/ppermute | solution.py:225
  135.5 5.9 %collective-permute-start.38 = (bf16[4,128,128]{2,1,0:T(8,128)(2,1)S(1)}, bf16[4,128,128]{2,1,0:T(8,128)(2,1)S(1)}, u32[]{:S(2)}, u32[]{:S(2)}) collective-permute-start(bf16[4,128,128]{2,1,0:T(8,128)(2,1)S(1)} %shard_map.76.refs_0_), channel_id=1, source_target_pairs={{0,16},{16,0},{32,48},{48,32},{1,17},{17,1},{33,49},{49,33},{2,18}... | collective-permute-start | bytes 393224 | tf_op jit(solution)/shard_map/ppermute | solution.py:225
  (5 other events, 3.8 us)

commit v4 on v3

--- a/solution.py
+++ b/solution.py
@@ -14,7 +14,7 @@
 SIDE = 128
 ROOT = math.sqrt(2.0 / math.pi)
 CUBIC = 0.044715
-UNROLL = 2
+UNROLL = 4
 
 VMEM = pl.BlockSpec(memory_space=pltpu.VMEM)
 SMEM = pl.BlockSpec(memory_space=pltpu.SMEM)
@@ -86,6 +86,15 @@
         copy.start()
     for copy in copies:
         copy.wait()
+
+
+def halves_kernel(left, right, low, high, sems):
+    run(
+        [
+            pltpu.make_async_copy(left.at[pl.ds(0, 8)], low, sems.at[0]),
+            pltpu.make_async_copy(right.at[pl.ds(8, 8)], high, sems.at[1]),
+        ]
+    )
 
 
 def load_kernel(where, x_hbm, g_hbm, *refs):
@@ -276,9 +285,18 @@
         compiler_params=PARAMS,
     )(
         where,
-        *(stored(v) for v in (features, grad_out, own, left, right, beside, own_other)),
-    )
-    second = [turn(left, Z, 1), turn(right, Z, 7), turn(left[:8], "x", 1), turn(right[8:], "x", 3)]
+        *(stored(v) for v in (features, grad_out, own)),
+        *(near(v) for v in (left, right, beside, own_other)),
+    )
+    low, high = pl.pallas_call(
+        halves_kernel,
+        out_shape=[pltpu.VMEM((8, SIDE, SIDE), bf16)] * 2,
+        in_specs=[ANY] * 2,
+        out_specs=[VMEM] * 2,
+        scratch_shapes=[pltpu.SemaphoreType.DMA((2,))],
+        compiler_params=PARAMS,
+    )(near(left), near(right))
+    second = [turn(left, Z, 1), turn(right, Z, 7), turn(low, "x", 1), turn(high, "x", 3)]
     crossed = [swap(left, "core", 1)]
     second, crossed, whole, right, beside = lax.optimization_barrier(
         (second, crossed, whole, right, beside)
@@ -295,10 +313,10 @@
         scratch_shapes=[pltpu.SemaphoreType.DMA((len(MIDDLE),))],
         input_output_aliases={1: 0},
         compiler_params=PARAMS,
-    )(where, near(whole), *(stored(piece) for piece in (*second, *crossed)))
+    )(where, near(whole), *(near(piece) for piece in (*second, *crossed)))
     *beside_far, whole = lax.optimization_barrier((*beside_far, whole))
     crossed = [swap(piece, "core", 1) for piece in (*second[:2], *beside_far)]
-    late = [stored(piece) for piece in (*beside_far, *crossed)]
+    late = [near(piece) for piece in (*beside_far, *crossed)]
     slopes, whole = pl.pallas_call(
         forward_kernel,
         out_shape=[
@@ -354,12 +372,6 @@
         functools.partial(backward_kernel, 0), in_specs=[SMEM] * 2 + [VMEM] * 3
     )(after, blocks, near(grad_near), near(whole), near(slopes))
     got, kept, grad_features = lax.optimization_barrier((got, kept, grad_features))
-    grad_features = backward(
-        functools.partial(backward_kernel, 1),
-        in_specs=[SMEM] * 2 + [VMEM] * 3 + [ANY],
-        input_output_aliases={5: 0},
-    )(place, blocks, near(grad_near), near(whole), near(slopes), grad_features)
-
     second = [
         swap((kept[2 * i + 1] + got[i][8:].astype(f32)).astype(bf16), axis, (3, 1)[half])
         for i, (axis, half) in enumerate(GROUPS)
@@ -381,13 +393,21 @@
     sums[0], rest[1] = lax.optimization_barrier((sums[0], rest[1]))
     sums.append(reduce_last(rest[1], "x"))
     mine = (sums[1] + swap(sums[0], "zl", 1)).astype(bf16)
+    place, mine = lax.optimization_barrier((place, mine))
+    grad_features = backward(
+        functools.partial(backward_kernel, 1),
+        in_specs=[SMEM] * 2 + [VMEM] * 3 + [ANY],
+        input_output_aliases={5: 0},
+    )(place, blocks, near(grad_near), near(whole), near(slopes), grad_features)
+    across = [swap(mine, "zh", r) for r in (1, 2, 3)]
+    across, grad_features = lax.optimization_barrier((across, grad_features))
     group = pl.pallas_call(
         normalize_kernel,
         out_shape=shape((4, SIDE, SIDE), bf16),
         in_specs=[VMEM] * 4,
         out_specs=VMEM,
         compiler_params=PARAMS,
-    )(mine, *(swap(mine, "zh", r) for r in (1, 2, 3)))
+    )(mine, *across)
     tile_update = pl.pallas_call(
         finish_kernel,
         out_shape=shape((16, SIDE, SIDE), f32),

time: 145 us -> 142 us (0.979)
  local copies, waits for them, and re-layouts: 5.44 us -> 0.16 us
  waiting for transfers between devices: 48.4 us -> 50.4 us
  starting transfers between devices: 45.7 us -> 47.3 us
    slice x2 -> x0, local copies, waits for them, and re-layouts: 3.37 us -> none  [the longest x1 1.7 us: on_device(): left[:8]]
    ppermute x8, waiting for transfers between devices: 13.3 us -> 15.5 us  [turn(): lax.ppermute(value, axes, [(i, (i + by) % size) for i in range(size)])]
    unnamed x24 -> x4, local copies, waits for them, and re-layouts: 1.92 us -> 0.01 us
    pallas_call x0 -> x1, Pallas kernels: none -> 1.83 us  [on_device(): pl.pallas_call(halves_kernel, out_shape=[pltpu.VMEM((8, SIDE, SIDE), bf16...]
    pallas_call x1, Pallas kernels: 7.71 us -> 5.89 us  [on_device(): pl.pallas_call(forward_kernel, out_shape=[pltpu.VMEM((64, rows_here, SIDE...]
  transfers between devices with their start and end apart: 41 -> 41, of which waited for: 24 -> 26; matrix products, arithmetic and copies ran while one was open for 5% -> 3% of each run, Pallas kernels for 16% -> 18%
where the time goes in v4:
time: 142 us; the launch traced here: 141 us
  waiting for transfers between devices  50.4 us (35%)
  starting transfers between devices  47.3 us (33%)
  Pallas kernels  35 us (25%)
  other arithmetic  5.02 us (4%)
  between operations  2.89 us (2%)
    ppermute x33, starting transfers between devices, swap(): return lax.ppermute(value, axis, [(i, i ^ mask) for i in range(size)])  35.9 us
    ppermute x33, waiting for transfers between devices, swap(): return lax.ppermute(value, axis, [(i, i ^ mask) for i in range(size)])  34.9 us
    ppermute x8, waiting for transfers between devices, turn(): lax.ppermute(value, axes, [(i, (i + by) % size) for i in range(size)])  15.5 us
    ppermute x8, starting transfers between devices, turn(): lax.ppermute(value, axes, [(i, (i + by) % size) for i in range(size)])  11.4 us
    pallas_call x1, Pallas kernels, on_device(): pl.pallas_call(forward_kernel, out_shape=[pltpu.VMEM((64, rows_here, SIDE...  5.89 us
    pallas_call x1, Pallas kernels, on_device(): pl.pallas_call(transpose_kernel, out_shape=pltpu.VMEM((64, SIDE, 2 * rows...  5.76 us
    pallas_call x1, Pallas kernels, on_device(): pl.pallas_call(load_kernel, out_shape=[pltpu.VMEM(features.shape, bf16),...  4.24 us
    pallas_call x1, Pallas kernels, on_device(): backward(functools.partial(backward_kernel, 0), in_specs=[SMEM] * 2 + [VM...  4.21 us
  transfers between devices with their start and end apart: 41, of which 26 were waited for; matrix products, arithmetic and copies ran while one was open for 3% of the time, Pallas kernels for 18%

profile of v4, /device:TPU:32, one launch (start us, length us, event | category | flops | bytes accessed | tf_op | source)
XLA Modules:
  0.0 140.7 jit_solution(15740869099305588916)
XLA Ops:
  0.7 1.9 %collective-permute-start.2 = (bf16[16,128,128]{2,1,0:T(8,128)(2,1)}, bf16[16,128,128]{2,1,0:T(8,128)(2,1)}, u32[]{:S(2)}, u32[]{:S(2)}) collective-permute-start(bf16[16,128,128]{2,1,0:T(8,128)(2,1)} %refs_0_.1), channel_id=1, source_target_pairs={{0,2},{2,0},{1,3},{3,1},{4,6},{6,4},{5,7},{7,5},{8,10},{10,8},{9,1... | collective-permute-start | bytes 1572872 | tf_op jit(solution)/shard_map/ppermute | solution.py:234
  4.7 1.3 fusion.10
  9.7 5.8 %collective-permute-done.2.refs_3_ = bf16[16,128,128]{2,1,0:T(8,128)(2,1)} collective-permute-done((bf16[16,128,128]{2,1,0:T(8,128)(2,1)}, bf16[16,128,128]{2,1,0:T(8,128)(2,1)}, u32[]{:S(2)}, u32[]{:S(2)}) %collective-permute-start.2) | collective-permute-done | bytes 524320 | tf_op jit(solution)/shard_map/ppermute | solution.py:234
  15.5 1.5 %collective-permute-done.1.refs_2_.right = bf16[16,128,128]{2,1,0:T(8,128)(2,1)} collective-permute-done((bf16[16,128,128]{2,1,0:T(8,128)(2,1)}, bf16[16,128,128]{2,1,0:T(8,128)(2,1)}, u32[]{:S(2)}, u32[]{:S(2)}) %collective-permute-start.1) | collective-permute-done | bytes 524320 | tf_op jit(solution)/shard_map/ppermute | solution.py:240
  17.0 2.1 %collective-permute-done.refs_1_.left = bf16[16,128,128]{2,1,0:T(8,128)(2,1)} collective-permute-done((bf16[16,128,128]{2,1,0:T(8,128)(2,1)}, bf16[16,128,128]{2,1,0:T(8,128)(2,1)}, u32[]{:S(2)}, u32[]{:S(2)}) %collective-permute-start) | collective-permute-done | bytes 524320 | tf_op jit(solution)/shard_map/ppermute | solution.py:240
  19.1 3.6 %collective-permute-start.5 = (bf16[16,128,128]{2,1,0:T(8,128)(2,1)}, bf16[16,128,128]{2,1,0:T(8,128)(2,1)}, u32[]{:S(2)}, u32[]{:S(2)}) collective-permute-start(bf16[16,128,128]{2,1,0:T(8,128)(2,1)} %collective-permute-done.refs_1_.left), channel_id=1, source_target_pairs={{0,2},{2,64},{64,66},{66,128},{128,130},{130,192},{192,194},{194,0... | collective-permute-start | bytes 1572872 | tf_op jit(solution)/shard_map/ppermute | solution.py:240
  22.7 1.8 %shard_map.69 = (bf16[8,128,128]{2,1,0:T(8,128)(2,1)}, bf16[8,128,128]{2,1,0:T(8,128)(2,1)}) custom-call(bf16[16,128,128]{2,1,0:T(8,128)(2,1)} %collective-permute-done.refs_1_.left, bf16[16,128,128]{2,1,0:T(8,128)(2,1)} %collective-permute-done.1.refs_2_.right), custom_call_target="tpu_custom_call" | custom-call | tf_op jit(solution)/shard_map/pallas_call | solution.py:291
  24.7 3.2 %collective-permute-start.8 = (bf16[8,128,128]{2,1,0:T(8,128)(2,1)}, bf16[8,128,128]{2,1,0:T(8,128)(2,1)}, u32[]{:S(2)}, u32[]{:S(2)}) collective-permute-start(bf16[8,128,128]{2,1,0:T(8,128)(2,1)} %get-tuple-element.73), channel_id=1, source_target_pairs={{0,12},{4,0},{8,4},{12,8},{1,13},{5,1},{9,5},{13,9},{2,14},{6,2},{... | collective-permute-start | bytes 786440 | tf_op jit(solution)/shard_map/ppermute | solution.py:240
  28.0 4.2 %shard_map.68 = (bf16[192,8192]{1,0:T(8,128)(2,1)S(1)}, bf16[192,8192]{1,0:T(8,128)(2,1)S(1)}, bf16[256,128,128]{2,1,0:T(8,128)(2,1)S(1)}) custom-call(s32[4]{0:T(128)S(1)} %pad_add_fusion.1.where, bf16[192,8192]{1,0:T(8,128)(2,1)} %x_hbm.1, bf16[192,8192]{1,0:T(8,128)(2,1)} %g_hbm.1, bf16[16,128,128]{2,1,0:T(8,128)(2,1)} %refs_0_.1, ...), custom_call_target="tpu_custom_call" | custom-call | tf_op jit(solution)/shard_map/pallas_call | solution.py:275
  32.2 2.2 %collective-permute-done.7.refs_2_ = bf16[8,128,128]{2,1,0:T(8,128)(2,1)S(1)} collective-permute-done((bf16[8,128,128]{2,1,0:T(8,128)(2,1)}, bf16[8,128,128]{2,1,0:T(8,128)(2,1)S(1)}, u32[]{:S(2)}, u32[]{:S(2)}) %collective-permute-start.7) | collective-permute-done | bytes 262176 | tf_op jit(solution)/shard_map/ppermute | solution.py:240
  34.8 2.2 %collective-permute-done.6.refs_1_ = bf16[16,128,128]{2,1,0:T(8,128)(2,1)} collective-permute-done((bf16[16,128,128]{2,1,0:T(8,128)(2,1)}, bf16[16,128,128]{2,1,0:T(8,128)(2,1)}, u32[]{:S(2)}, u32[]{:S(2)}) %collective-permute-start.6) | collective-permute-done | bytes 524320 | tf_op jit(solution)/shard_map/ppermute | solution.py:240
  38.7 2.4 %collective-permute-start.10 = (bf16[8,128,128]{2,1,0:T(8,128)(2,1)S(1)}, bf16[8,128,128]{2,1,0:T(8,128)(2,1)S(1)}, u32[]{:S(2)}, u32[]{:S(2)}) collective-permute-start(bf16[8,128,128]{2,1,0:T(8,128)(2,1)S(1)} %collective-permute-done.7.refs_2_), channel_id=1, source_target_pairs={{0,2},{2,64},{64,66},{66,128},{128,130},{130,192},{192,194},{194,0... | collective-permute-start | bytes 786440 | tf_op jit(solution)/shard_map/ppermute | solution.py:240
  41.7 2.1 %shard_map.70.given = bf16[256,128,128]{2,1,0:T(8,128)(2,1)S(1)} custom-call(s32[4]{0:T(128)S(1)} %pad_add_fusion.1.where, bf16[256,128,128]{2,1,0:T(8,128)(2,1)S(1)} %get-tuple-element.77.given, bf16[16,128,128]{2,1,0:T(8,128)(2,1)} %collective-permute-done.5.refs_0_, ...), custom_call_target="tpu_custom_call", output_to_operand_aliasing={{}: (1, {})} | custom-call | tf_op jit(solution)/shard_map/pallas_call | solution.py:308
  43.8 3.6 %collective-permute-done.10.refs_0_ = bf16[8,128,128]{2,1,0:T(8,128)(2,1)S(1)} collective-permute-done((bf16[8,128,128]{2,1,0:T(8,128)(2,1)S(1)}, bf16[8,128,128]{2,1,0:T(8,128)(2,1)S(1)}, u32[]{:S(2)}, u32[]{:S(2)}) %collective-permute-start.10) | collective-permute-done | bytes 262176 | tf_op jit(solution)/shard_map/ppermute | solution.py:240
  47.4 3.5 %collective-permute-done.11.refs_1_ = bf16[8,128,128]{2,1,0:T(8,128)(2,1)S(1)} collective-permute-done((bf16[8,128,128]{2,1,0:T(8,128)(2,1)}, bf16[8,128,128]{2,1,0:T(8,128)(2,1)S(1)}, u32[]{:S(2)}, u32[]{:S(2)}) %collective-permute-start.11) | collective-permute-done | bytes 262176 | tf_op jit(solution)/shard_map/ppermute | solution.py:240
  52.8 5.9 %shard_map.71 = (bf16[64,192,128]{2,1,0:T(8,128)(2,1)S(1)}, bf16[256,128,128]{2,1,0:T(8,128)(2,1)S(1)}) custom-call(s32[4]{0:T(128)S(1)} %pad_add_fusion.1.where, s32[256]{0:T(256)S(1)} %select_reduce_fusion.place, s32[64]{0:T(128)S(1)} %xor.28.blocks, bf16[192,8192]{1,0:T(8,128)(2,1)S(1)} %get-tuple-element.69.x_ref.mine_ref, ...), custom_call_target="tpu_custom_call", output_to_operand_aliasing={{1}: (5, {})} | custom-call | tf_op jit(solution)/shard_map/pallas_call | solution.py:320
  59.0 5.8 %shard_map.72.xt_ref = bf16[64,128,384]{2,1,0:T(8,128)(2,1)S(1)} custom-call(bf16[192,8192]{1,0:T(8,128)(2,1)S(1)} %get-tuple-element.69.x_ref.mine_ref, bf16[192,8192]{1,0:T(8,128)(2,1)S(1)} %collective-permute-done.3.other_ref), custom_call_target="tpu_custom_call" | custom-call | tf_op jit(solution)/shard_map/pallas_call | solution.py:334
  64.8 2.5 %shard_map.73 = (bf16[16,128,128]{2,1,0:T(8,128)(2,1)S(1)}, bf16[16,128,128]{2,1,0:T(8,128)(2,1)S(1)}, bf16[16,128,128]{2,1,0:T(8,128)(2,1)S(1)}, bf16[16,128,128]{2,1,0:T(8,128)(2,1)S(1)}) custom-call(s32[256]{0:T(256)S(1)} %copy-done, s32[256]{0:T(256)S(1)} %copy-done.1, s32[4]{0:T(128)S(1)} %pad_add_fusion.1.where, ...), custom_call_target="tpu_custom_call" | custom-call | tf_op jit(solution)/shard_map/pallas_call | solution.py:342
  67.8 1.6 %collective-permute-start.22 = (bf16[16,128,128]{2,1,0:T(8,128)(2,1)S(1)}, bf16[16,128,128]{2,1,0:T(8,128)(2,1)S(1)}, u32[]{:S(2)}, u32[]{:S(2)}) collective-permute-start(bf16[16,128,128]{2,1,0:T(8,128)(2,1)S(1)} %get-tuple-element.92), channel_id=1, source_target_pairs={{0,16},{16,0},{32,48},{48,32},{1,17},{17,1},{33,49},{49,33},{2,18}... | collective-permute-start | bytes 1572872 | tf_op jit(solution)/shard_map/ppermute | solution.py:234
  69.4 2.2 %collective-permute-start.23 = (bf16[16,128,128]{2,1,0:T(8,128)(2,1)S(1)}, bf16[16,128,128]{2,1,0:T(8,128)(2,1)S(1)}, u32[]{:S(2)}, u32[]{:S(2)}) collective-permute-start(bf16[16,128,128]{2,1,0:T(8,128)(2,1)S(1)} %get-tuple-element.93), channel_id=1, source_target_pairs={{0,48},{16,32},{32,16},{48,0},{1,49},{17,33},{33,17},{49,1},{2,50}... | collective-permute-start | bytes 1572872 | tf_op jit(solution)/shard_map/ppermute | solution.py:234
  71.6 2.4 %shard_map.74 = (f32[8,128,128]{2,1,0:T(8,128)S(1)}, f32[8,128,128]{2,1,0:T(8,128)S(1)}, f32[8,128,128]{2,1,0:T(8,128)S(1)}, f32[8,128,128]{2,1,0:T(8,128)S(1)},...) custom-call(s32[256]{0:T(256)S(1)} %copy-done, ...), custom_call_target="tpu_custom_call" | custom-call | tf_op jit(solution)/shard_map/pallas_call | solution.py:352
  74.0 4.2 %shard_map.75.refs_0_ = bf16[192,8192]{1,0:T(8,128)(2,1)} custom-call(s32[256]{0:T(256)S(1)} %select_reduce_fusion.place, s32[64]{0:T(128)S(1)} %xor.28.blocks, bf16[192,8192]{1,0:T(8,128)(2,1)S(1)} %get-tuple-element.71.g_ref, bf16[256,128,128]{2,1,0:T(8,128)(2,1)S(1)} %get-tuple-element.104.w_ref, bf16[64,192,128]{2,1,0:T(8,128)(2,1)S(1)} %get-tuple-element.89.s_ref), custom_call_target="tpu_custom_call" | custom-call | tf_op jit(solution)/shard_map/pallas_call | solution.py:371
  78.2 3.3 %collective-permute-done.20 = bf16[16,128,128]{2,1,0:T(8,128)(2,1)S(1)} collective-permute-done((bf16[16,128,128]{2,1,0:T(8,128)(2,1)S(1)}, bf16[16,128,128]{2,1,0:T(8,128)(2,1)S(1)}, u32[]{:S(2)}, u32[]{:S(2)}) %collective-permute-start.20) | collective-permute-done | bytes 524320 | tf_op jit(solution)/shard_map/ppermute | solution.py:234
  81.5 1.3 collective-permute-done.21
  82.8 1.4 collective-permute-done.23
  84.6 1.5 %collective-permute-start.25 = (bf16[8,128,128]{2,1,0:T(8,128)(2,1)S(1)}, bf16[8,128,128]{2,1,0:T(8,128)(2,1)S(1)}, u32[]{:S(2)}, u32[]{:S(2)}) collective-permute-start(bf16[8,128,128]{2,1,0:T(8,128)(2,1)S(1)} %add_convert_fusion.2), channel_id=1, source_target_pairs={{0,4},{4,0},{8,12},{12,8},{1,5},{5,1},{9,13},{13,9},{2,6},{6,2},{1... | collective-permute-start | bytes 786440 | tf_op jit(solution)/shard_map/ppermute | solution.py:234
  86.2 2.3 %collective-permute-start.29 = (bf16[8,128,128]{2,1,0:T(8,128)(2,1)S(1)}, bf16[8,128,128]{2,1,0:T(8,128)(2,1)S(1)}, u32[]{:S(2)}, u32[]{:S(2)}) collective-permute-start(bf16[8,128,128]{2,1,0:T(8,128)(2,1)S(1)} %add_convert_fusion.1), channel_id=1, source_target_pairs={{0,48},{16,32},{32,16},{48,0},{1,49},{17,33},{33,17},{49,1},{2,50}... | collective-permute-start | bytes 786440 | tf_op jit(solution)/shard_map/ppermute | solution.py:234
  88.6 2.4 %collective-permute-start.24 = (bf16[8,128,128]{2,1,0:T(8,128)(2,1)S(1)}, bf16[8,128,128]{2,1,0:T(8,128)(2,1)S(1)}, u32[]{:S(2)}, u32[]{:S(2)}) collective-permute-start(bf16[8,128,128]{2,1,0:T(8,128)(2,1)S(1)} %add_convert_fusion.3), channel_id=1, source_target_pairs={{0,12},{4,8},{8,4},{12,0},{1,13},{5,9},{9,5},{13,1},{2,14},{6,10},... | collective-permute-start | bytes 786440 | tf_op jit(solution)/shard_map/ppermute | solution.py:234
  91.0 1.2 collective-permute-done.25
  92.3 4.1 %collective-permute-done.24 = bf16[8,128,128]{2,1,0:T(8,128)(2,1)S(1)} collective-permute-done((bf16[8,128,128]{2,1,0:T(8,128)(2,1)S(1)}, bf16[8,128,128]{2,1,0:T(8,128)(2,1)S(1)}, u32[]{:S(2)}, u32[]{:S(2)}) %collective-permute-start.24) | collective-permute-done | bytes 262176 | tf_op jit(solution)/shard_map/ppermute | solution.py:234
  96.6 1.3 collective-permute-start.26
  97.9 1.3 collective-permute-start.28
  99.1 2.2 %collective-permute-start.27 = (bf16[4,128,128]{2,1,0:T(8,128)(2,1)S(1)}, bf16[4,128,128]{2,1,0:T(8,128)(2,1)S(1)}, u32[]{:S(2)}, u32[]{:S(2)}) collective-permute-start(bf16[4,128,128]{2,1,0:T(8,128)(2,1)S(1)} %get-tuple-element.133), channel_id=1, source_target_pairs={{0,48},{16,32},{32,16},{48,0},{1,49},{17,33},{33,17},{49,1},{2,50}... | collective-permute-start | bytes 393224 | tf_op jit(solution)/shard_map/ppermute | solution.py:234
  101.7 2.7 %collective-permute-done.28 = bf16[4,128,128]{2,1,0:T(8,128)(2,1)S(1)} collective-permute-done((bf16[4,128,128]{2,1,0:T(8,128)(2,1)S(1)}, bf16[4,128,128]{2,1,0:T(8,128)(2,1)S(1)}, u32[]{:S(2)}, u32[]{:S(2)}) %collective-permute-start.28) | collective-permute-done | bytes 131104 | tf_op jit(solution)/shard_map/ppermute | solution.py:234
  104.4 1.4 collective-permute-done.27
  106.5 3.4 %collective-permute-start.33 = (bf16[4,128,128]{2,1,0:T(8,128)(2,1)S(1)}, bf16[4,128,128]{2,1,0:T(8,128)(2,1)S(1)}, u32[]{:S(2)}, u32[]{:S(2)}) collective-permute-start(bf16[4,128,128]{2,1,0:T(8,128)(2,1)S(1)} %get-tuple-element.129), channel_id=1, source_target_pairs={{0,8},{4,12},{8,0},{12,4},{1,9},{5,13},{9,1},{13,5},{2,10},{6,14},... | collective-permute-start | bytes 393224 | tf_op jit(solution)/shard_map/ppermute | solution.py:234
  110.0 1.3 collective-permute-start.32
  111.5 2.8 %collective-permute-done.33 = bf16[4,128,128]{2,1,0:T(8,128)(2,1)S(1)} collective-permute-done((bf16[4,128,128]{2,1,0:T(8,128)(2,1)S(1)}, bf16[4,128,128]{2,1,0:T(8,128)(2,1)S(1)}, u32[]{:S(2)}, u32[]{:S(2)}) %collective-permute-start.33) | collective-permute-done | bytes 131104 | tf_op jit(solution)/shard_map/ppermute | solution.py:234
  114.3 1.8 %collective-permute-done.32 = bf16[4,128,128]{2,1,0:T(8,128)(2,1)S(1)} collective-permute-done((bf16[4,128,128]{2,1,0:T(8,128)(2,1)S(1)}, bf16[4,128,128]{2,1,0:T(8,128)(2,1)S(1)}, u32[]{:S(2)}, u32[]{:S(2)}) %collective-permute-start.32) | collective-permute-done | bytes 131104 | tf_op jit(solution)/shard_map/ppermute | solution.py:234
  116.2 2.5 %collective-permute-start.37 = (bf16[4,128,128]{2,1,0:T(8,128)(2,1)S(1)}, bf16[4,128,128]{2,1,0:T(8,128)(2,1)S(1)}, u32[]{:S(2)}, u32[]{:S(2)}) collective-permute-start(bf16[4,128,128]{2,1,0:T(8,128)(2,1)S(1)} %fusion.7.a), channel_id=1, source_target_pairs={{0,192},{64,128},{128,64},{192,0},{1,193},{65,129},{129,65},{193,1... | collective-permute-start | bytes 393224 | tf_op jit(solution)/shard_map/ppermute | solution.py:234
  118.8 4.3 %collective-permute-start.36 = (bf16[4,128,128]{2,1,0:T(8,128)(2,1)S(1)}, bf16[4,128,128]{2,1,0:T(8,128)(2,1)S(1)}, u32[]{:S(2)}, u32[]{:S(2)}) collective-permute-start(bf16[4,128,128]{2,1,0:T(8,128)(2,1)S(1)} %fusion.7.a), channel_id=1, source_target_pairs={{0,128},{64,192},{128,0},{192,64},{1,129},{65,193},{129,1},{193,65... | collective-permute-start | bytes 393224 | tf_op jit(solution)/shard_map/ppermute | solution.py:234
  123.1 4.2 %shard_map.76 = bf16[192,8192]{1,0:T(8,128)(2,1)} custom-call(s32[256]{0:T(256)S(1)} %select_reduce_fusion.place, s32[64]{0:T(128)S(1)} %xor.28.blocks, bf16[192,8192]{1,0:T(8,128)(2,1)S(1)} %get-tuple-element.71.g_ref, bf16[256,128,128]{2,1,0:T(8,128)(2,1)S(1)} %get-tuple-element.104.w_ref, ...), custom_call_target="tpu_custom_call", output_to_operand_aliasing={{}: (5, {})} | custom-call | tf_op jit(solution)/shard_map/pallas_call | solution.py:397
  128.5 1.8 %collective-permute-done.35.b = bf16[4,128,128]{2,1,0:T(8,128)(2,1)S(1)} collective-permute-done((bf16[4,128,128]{2,1,0:T(8,128)(2,1)S(1)}, bf16[4,128,128]{2,1,0:T(8,128)(2,1)S(1)}, u32[]{:S(2)}, u32[]{:S(2)}) %collective-permute-start.35) | collective-permute-done | bytes 131104 | tf_op jit(solution)/shard_map/ppermute | solution.py:234
  130.6 1.7 %collective-permute-start.40 = (bf16[4,128,128]{2,1,0:T(8,128)(2,1)S(1)}, bf16[4,128,128]{2,1,0:T(8,128)(2,1)S(1)}, u32[]{:S(2)}, u32[]{:S(2)}) collective-permute-start(bf16[4,128,128]{2,1,0:T(8,128)(2,1)S(1)} %shard_map.77.refs_0_), channel_id=1, source_target_pairs={{0,48},{16,32},{32,16},{48,0},{1,49},{17,33},{33,17},{49,1},{2,50}... | collective-permute-start | bytes 393224 | tf_op jit(solution)/shard_map/ppermute | solution.py:234
  133.1 1.6 %collective-permute-start.38 = (bf16[4,128,128]{2,1,0:T(8,128)(2,1)S(1)}, bf16[4,128,128]{2,1,0:T(8,128)(2,1)S(1)}, u32[]{:S(2)}, u32[]{:S(2)}) collective-permute-start(bf16[4,128,128]{2,1,0:T(8,128)(2,1)S(1)} %shard_map.77.refs_0_), channel_id=1, source_target_pairs={{0,16},{16,0},{32,48},{48,32},{1,17},{17,1},{33,49},{49,33},{2,18}... | collective-permute-start | bytes 393224 | tf_op jit(solution)/shard_map/ppermute | solution.py:234
  134.8 2.1 %collective-permute-done.40.refs_3_ = bf16[4,128,128]{2,1,0:T(8,128)(2,1)S(1)} collective-permute-done((bf16[4,128,128]{2,1,0:T(8,128)(2,1)S(1)}, bf16[4,128,128]{2,1,0:T(8,128)(2,1)S(1)}, u32[]{:S(2)}, u32[]{:S(2)}) %collective-permute-start.40) | collective-permute-done | bytes 131104 | tf_op jit(solution)/shard_map/ppermute | solution.py:234
  136.9 2.0 %collective-permute-done.39.refs_2_ = bf16[4,128,128]{2,1,0:T(8,128)(2,1)S(1)} collective-permute-done((bf16[4,128,128]{2,1,0:T(8,128)(2,1)S(1)}, bf16[4,128,128]{2,1,0:T(8,128)(2,1)S(1)}, u32[]{:S(2)}, u32[]{:S(2)}) %collective-permute-start.39) | collective-permute-done | bytes 131104 | tf_op jit(solution)/shard_map/ppermute | solution.py:234
  139.1 1.6 %shard_map.78 = f32[16,128,128]{2,1,0:T(8,128)} custom-call(s32[4]{0:T(128)S(1)} %pad_add_fusion.1.where, bf16[4,128,128]{2,1,0:T(8,128)(2,1)S(1)} %shard_map.77.refs_0_, bf16[4,128,128]{2,1,0:T(8,128)(2,1)S(1)} %collective-permute-done.38.refs_1_, bf16[4,128,128]{2,1,0:T(8,128)(2,1)S(1)} %collective-permute-done.39.refs_2_, ...), custom_call_target="tpu_custom_call" | custom-call | tf_op jit(solution)/shard_map/pallas_call | solution.py:411
  (73 shorter events, 14.1 us)
Async XLA Ops:
  0.6 18.4 %collective-permute-start.3 = (bf16[192,8192]{1,0:T(8,128)(2,1)}, bf16[192,8192]{1,0:T(8,128)(2,1)S(1)}, u32[]{:S(2)}, u32[]{:S(2)}) collective-permute-start(bf16[192,8192]{1,0:T(8,128)(2,1)} %x_hbm.1), channel_id=1, source_target_pairs={{0,1},{1,0},{2,3},{3,2},{4,5},{5,4},{6,7},{7,6},{8,9},{9,8},{10,11... | collective-permute-start | bytes 9437192 | tf_op jit(solution)/shard_map/ppermute | solution.py:234
  0.7 14.7 %collective-permute-start.2 = (bf16[16,128,128]{2,1,0:T(8,128)(2,1)}, bf16[16,128,128]{2,1,0:T(8,128)(2,1)}, u32[]{:S(2)}, u32[]{:S(2)}) collective-permute-start(bf16[16,128,128]{2,1,0:T(8,128)(2,1)} %refs_0_.1), channel_id=1, source_target_pairs={{0,2},{2,0},{1,3},{3,1},{4,6},{6,4},{5,7},{7,5},{8,10},{10,8},{9,1... | collective-permute-start | bytes 1572872 | tf_op jit(solution)/shard_map/ppermute | solution.py:234
  2.7 14.3 %collective-permute-start.1 = (bf16[16,128,128]{2,1,0:T(8,128)(2,1)}, bf16[16,128,128]{2,1,0:T(8,128)(2,1)}, u32[]{:S(2)}, u32[]{:S(2)}) collective-permute-start(bf16[16,128,128]{2,1,0:T(8,128)(2,1)} %refs_0_.1), channel_id=1, source_target_pairs={{0,12},{4,0},{8,4},{12,8},{1,13},{5,1},{9,5},{13,9},{2,14},{6,2},{... | collective-permute-start | bytes 1572872 | tf_op jit(solution)/shard_map/ppermute | solution.py:240
  3.7 15.4 %collective-permute-start = (bf16[16,128,128]{2,1,0:T(8,128)(2,1)}, bf16[16,128,128]{2,1,0:T(8,128)(2,1)}, u32[]{:S(2)}, u32[]{:S(2)}) collective-permute-start(bf16[16,128,128]{2,1,0:T(8,128)(2,1)} %refs_0_.1), channel_id=1, source_target_pairs={{0,4},{4,8},{8,12},{12,0},{1,5},{5,9},{9,13},{13,1},{2,6},{6,10},{... | collective-permute-start | bytes 1572872 | tf_op jit(solution)/shard_map/ppermute | solution.py:240
  4.7 14.4 %collective-permute-start.4 = (bf16[16,128,128]{2,1,0:T(8,128)(2,1)}, bf16[16,128,128]{2,1,0:T(8,128)(2,1)}, u32[]{:S(2)}, u32[]{:S(2)}) collective-permute-start(bf16[16,128,128]{2,1,0:T(8,128)(2,1)} %refs_0_.1), channel_id=1, source_target_pairs={{0,1},{1,0},{2,3},{3,2},{4,5},{5,4},{6,7},{7,6},{8,9},{9,8},{10,11... | collective-permute-start | bytes 1572872 | tf_op jit(solution)/shard_map/ppermute | solution.py:234
  19.1 15.4 %collective-permute-start.9 = (bf16[16,128,128]{2,1,0:T(8,128)(2,1)}, bf16[16,128,128]{2,1,0:T(8,128)(2,1)}, u32[]{:S(2)}, u32[]{:S(2)}) collective-permute-start(bf16[16,128,128]{2,1,0:T(8,128)(2,1)} %collective-permute-done.refs_1_.left), channel_id=1, source_target_pairs={{0,1},{1,0},{2,3},{3,2},{4,5},{5,4},{6,7},{7,6},{8,9},{9,8},{10,11... | collective-permute-start | bytes 1572872 | tf_op jit(solution)/shard_map/ppermute | solution.py:234
  19.1 15.8 %collective-permute-start.5 = (bf16[16,128,128]{2,1,0:T(8,128)(2,1)}, bf16[16,128,128]{2,1,0:T(8,128)(2,1)}, u32[]{:S(2)}, u32[]{:S(2)}) collective-permute-start(bf16[16,128,128]{2,1,0:T(8,128)(2,1)} %collective-permute-done.refs_1_.left), channel_id=1, source_target_pairs={{0,2},{2,64},{64,66},{66,128},{128,130},{130,192},{192,194},{194,0... | collective-permute-start | bytes 1572872 | tf_op jit(solution)/shard_map/ppermute | solution.py:240
  22.7 14.3 %collective-permute-start.6 = (bf16[16,128,128]{2,1,0:T(8,128)(2,1)}, bf16[16,128,128]{2,1,0:T(8,128)(2,1)}, u32[]{:S(2)}, u32[]{:S(2)}) collective-permute-start(bf16[16,128,128]{2,1,0:T(8,128)(2,1)} %collective-permute-done.1.refs_2_.right), channel_id=1, source_target_pairs={{0,194},{2,0},{64,2},{66,64},{128,66},{130,128},{192,130},{194,192... | collective-permute-start | bytes 1572872 | tf_op jit(solution)/shard_map/ppermute | solution.py:240
  24.6 9.9 %collective-permute-start.7 = (bf16[8,128,128]{2,1,0:T(8,128)(2,1)}, bf16[8,128,128]{2,1,0:T(8,128)(2,1)S(1)}, u32[]{:S(2)}, u32[]{:S(2)}) collective-permute-start(bf16[8,128,128]{2,1,0:T(8,128)(2,1)} %get-tuple-element.72), channel_id=1, source_target_pairs={{0,4},{4,8},{8,12},{12,0},{1,5},{5,9},{9,13},{13,1},{2,6},{6,10},{... | collective-permute-start | bytes 786440 | tf_op jit(solution)/shard_map/ppermute | solution.py:240
  24.7 9.8 %collective-permute-start.8 = (bf16[8,128,128]{2,1,0:T(8,128)(2,1)}, bf16[8,128,128]{2,1,0:T(8,128)(2,1)}, u32[]{:S(2)}, u32[]{:S(2)}) collective-permute-start(bf16[8,128,128]{2,1,0:T(8,128)(2,1)} %get-tuple-element.73), channel_id=1, source_target_pairs={{0,12},{4,0},{8,4},{12,8},{1,13},{5,1},{9,5},{13,9},{2,14},{6,2},{... | collective-permute-start | bytes 786440 | tf_op jit(solution)/shard_map/ppermute | solution.py:240
  38.0 3.1 %collective-permute-start.14 = (bf16[16,128,128]{2,1,0:T(8,128)(2,1)S(1)}, bf16[16,128,128]{2,1,0:T(8,128)(2,1)S(1)}, u32[]{:S(2)}, u32[]{:S(2)}) collective-permute-start(bf16[16,128,128]{2,1,0:T(8,128)(2,1)S(1)} %pad_maximum_fusion.2), channel_id=1, source_target_pairs={{0,1},{1,0},{2,3},{3,2},{4,5},{5,4},{6,7},{7,6},{8,9},{9,8},{10,11... | collective-permute-start | bytes 1572872 | tf_op jit(solution)/shard_map/ppermute | solution.py:234
  38.1 3.2 %collective-permute-start.12 = (bf16[16,128,128]{2,1,0:T(8,128)(2,1)}, bf16[16,128,128]{2,1,0:T(8,128)(2,1)S(1)}, u32[]{:S(2)}, u32[]{:S(2)}) collective-permute-start(bf16[16,128,128]{2,1,0:T(8,128)(2,1)} %collective-permute-done.1.refs_2_.right), channel_id=1, source_target_pairs={{0,1},{1,0},{2,3},{3,2},{4,5},{5,4},{6,7},{7,6},{8,9},{9,8},{10,11... | collective-permute-start | bytes 1572872 | tf_op jit(solution)/shard_map/ppermute | solution.py:234
  38.6 3.1 %collective-permute-start.13 = (bf16[16,128,128]{2,1,0:T(8,128)(2,1)}, bf16[16,128,128]{2,1,0:T(8,128)(2,1)S(1)}, u32[]{:S(2)}, u32[]{:S(2)}) collective-permute-start(bf16[16,128,128]{2,1,0:T(8,128)(2,1)} %collective-permute-done.2.refs_3_), channel_id=1, source_target_pairs={{0,1},{1,0},{2,3},{3,2},{4,5},{5,4},{6,7},{7,6},{8,9},{9,8},{10,11... | collective-permute-start | bytes 1572872 | tf_op jit(solution)/shard_map/ppermute | solution.py:234
  38.7 8.6 %collective-permute-start.10 = (bf16[8,128,128]{2,1,0:T(8,128)(2,1)S(1)}, bf16[8,128,128]{2,1,0:T(8,128)(2,1)S(1)}, u32[]{:S(2)}, u32[]{:S(2)}) collective-permute-start(bf16[8,128,128]{2,1,0:T(8,128)(2,1)S(1)} %collective-permute-done.7.refs_2_), channel_id=1, source_target_pairs={{0,2},{2,64},{64,66},{66,128},{128,130},{130,192},{192,194},{194,0... | collective-permute-start | bytes 786440 | tf_op jit(solution)/shard_map/ppermute | solution.py:240
  41.1 9.8 %collective-permute-start.11 = (bf16[8,128,128]{2,1,0:T(8,128)(2,1)}, bf16[8,128,128]{2,1,0:T(8,128)(2,1)S(1)}, u32[]{:S(2)}, u32[]{:S(2)}) collective-permute-start(bf16[8,128,128]{2,1,0:T(8,128)(2,1)} %collective-permute-done.8.refs_3_), channel_id=1, source_target_pairs={{0,194},{2,0},{64,2},{66,64},{128,66},{130,128},{192,130},{194,192... | collective-permute-start | bytes 786440 | tf_op jit(solution)/shard_map/ppermute | solution.py:240
  41.1 10.3 %collective-permute-start.15 = (bf16[16,128,128]{2,1,0:T(8,128)(2,1)}, bf16[16,128,128]{2,1,0:T(8,128)(2,1)S(1)}, u32[]{:S(2)}, u32[]{:S(2)}) collective-permute-start(bf16[16,128,128]{2,1,0:T(8,128)(2,1)} %collective-permute-done.5.refs_0_), channel_id=1, source_target_pairs={{0,1},{1,0},{2,3},{3,2},{4,5},{5,4},{6,7},{7,6},{8,9},{9,8},{10,11... | collective-permute-start | bytes 1572872 | tf_op jit(solution)/shard_map/ppermute | solution.py:234
  41.3 10.1 %collective-permute-start.16 = (bf16[16,128,128]{2,1,0:T(8,128)(2,1)}, bf16[16,128,128]{2,1,0:T(8,128)(2,1)S(1)}, u32[]{:S(2)}, u32[]{:S(2)}) collective-permute-start(bf16[16,128,128]{2,1,0:T(8,128)(2,1)} %collective-permute-done.6.refs_1_), channel_id=1, source_target_pairs={{0,1},{1,0},{2,3},{3,2},{4,5},{5,4},{6,7},{7,6},{8,9},{9,8},{10,11... | collective-permute-start | bytes 1572872 | tf_op jit(solution)/shard_map/ppermute | solution.py:234
  50.9 1.5 %collective-permute-start.17 = (bf16[8,128,128]{2,1,0:T(8,128)(2,1)S(1)}, bf16[8,128,128]{2,1,0:T(8,128)(2,1)S(1)}, u32[]{:S(2)}, u32[]{:S(2)}) collective-permute-start(bf16[8,128,128]{2,1,0:T(8,128)(2,1)S(1)} %collective-permute-done.10.refs_0_), channel_id=1, source_target_pairs={{0,1},{1,0},{2,3},{3,2},{4,5},{5,4},{6,7},{7,6},{8,9},{9,8},{10,11... | collective-permute-start | bytes 786440 | tf_op jit(solution)/shard_map/ppermute | solution.py:234
  50.9 1.9 %collective-permute-start.18 = (bf16[8,128,128]{2,1,0:T(8,128)(2,1)S(1)}, bf16[8,128,128]{2,1,0:T(8,128)(2,1)S(1)}, u32[]{:S(2)}, u32[]{:S(2)}) collective-permute-start(bf16[8,128,128]{2,1,0:T(8,128)(2,1)S(1)} %collective-permute-done.11.refs_1_), channel_id=1, source_target_pairs={{0,1},{1,0},{2,3},{3,2},{4,5},{5,4},{6,7},{7,6},{8,9},{9,8},{10,11... | collective-permute-start | bytes 786440 | tf_op jit(solution)/shard_map/ppermute | solution.py:234
  58.7 6.0 %copy-start = (s32[256]{0:T(256)S(1)}, s32[256]{0:T(256)}, u32[]{:S(2)}) copy-start(s32[256]{0:T(256)} %rows.3) | copy-start | bytes 3076
  58.7 6.0 %copy-start.1 = (s32[256]{0:T(256)S(1)}, s32[256]{0:T(256)}, u32[]{:S(2)}) copy-start(s32[256]{0:T(256)} %cols.3) | copy-start | bytes 3076
  58.8 6.0 %collective-permute-start.19 = (bf16[64,192,128]{2,1,0:T(8,128)(2,1)S(1)}, bf16[64,192,128]{2,1,0:T(8,128)(2,1)S(1)}, u32[]{:S(2)}, u32[]{:S(2)}) collective-permute-start(bf16[64,192,128]{2,1,0:T(8,128)(2,1)S(1)} %get-tuple-element.89.s_ref), channel_id=1, source_target_pairs={{0,1},{1,0},{2,3},{3,2},{4,5},{5,4},{6,7},{7,6},{8,9},{9,8},{10,11... | collective-permute-start | bytes 9437192 | tf_op jit(solution)/shard_map/ppermute | solution.py:234
  67.2 14.3 %collective-permute-start.20 = (bf16[16,128,128]{2,1,0:T(8,128)(2,1)S(1)}, bf16[16,128,128]{2,1,0:T(8,128)(2,1)S(1)}, u32[]{:S(2)}, u32[]{:S(2)}) collective-permute-start(bf16[16,128,128]{2,1,0:T(8,128)(2,1)S(1)} %get-tuple-element.90), channel_id=1, source_target_pairs={{0,4},{4,0},{8,12},{12,8},{1,5},{5,1},{9,13},{13,9},{2,6},{6,2},{1... | collective-permute-start | bytes 1572872 | tf_op jit(solution)/shard_map/ppermute | solution.py:234
  67.3 15.5 %collective-permute-start.21 = (bf16[16,128,128]{2,1,0:T(8,128)(2,1)S(1)}, bf16[16,128,128]{2,1,0:T(8,128)(2,1)S(1)}, u32[]{:S(2)}, u32[]{:S(2)}) collective-permute-start(bf16[16,128,128]{2,1,0:T(8,128)(2,1)S(1)} %get-tuple-element.91), channel_id=1, source_target_pairs={{0,12},{4,8},{8,4},{12,0},{1,13},{5,9},{9,5},{13,1},{2,14},{6,10},... | collective-permute-start | bytes 1572872 | tf_op jit(solution)/shard_map/ppermute | solution.py:234
  67.8 15.0 %collective-permute-start.22 = (bf16[16,128,128]{2,1,0:T(8,128)(2,1)S(1)}, bf16[16,128,128]{2,1,0:T(8,128)(2,1)S(1)}, u32[]{:S(2)}, u32[]{:S(2)}) collective-permute-start(bf16[16,128,128]{2,1,0:T(8,128)(2,1)S(1)} %get-tuple-element.92), channel_id=1, source_target_pairs={{0,16},{16,0},{32,48},{48,32},{1,17},{17,1},{33,49},{49,33},{2,18}... | collective-permute-start | bytes 1572872 | tf_op jit(solution)/shard_map/ppermute | solution.py:234
  69.4 14.8 %collective-permute-start.23 = (bf16[16,128,128]{2,1,0:T(8,128)(2,1)S(1)}, bf16[16,128,128]{2,1,0:T(8,128)(2,1)S(1)}, u32[]{:S(2)}, u32[]{:S(2)}) collective-permute-start(bf16[16,128,128]{2,1,0:T(8,128)(2,1)S(1)} %get-tuple-element.93), channel_id=1, source_target_pairs={{0,48},{16,32},{32,16},{48,0},{1,49},{17,33},{33,17},{49,1},{2,50}... | collective-permute-start | bytes 1572872 | tf_op jit(solution)/shard_map/ppermute | solution.py:234
  84.3 17.1 %collective-permute-start.30 = (bf16[8,128,128]{2,1,0:T(8,128)(2,1)S(1)}, bf16[8,128,128]{2,1,0:T(8,128)(2,1)S(1)}, u32[]{:S(2)}, u32[]{:S(2)}) collective-permute-start(bf16[8,128,128]{2,1,0:T(8,128)(2,1)S(1)} %add_convert_fusion), channel_id=1, source_target_pairs={{0,16},{16,0},{32,48},{48,32},{1,17},{17,1},{33,49},{49,33},{2,18}... | collective-permute-start | bytes 786440 | tf_op jit(solution)/shard_map/ppermute | solution.py:234
  84.6 7.5 %collective-permute-start.25 = (bf16[8,128,128]{2,1,0:T(8,128)(2,1)S(1)}, bf16[8,128,128]{2,1,0:T(8,128)(2,1)S(1)}, u32[]{:S(2)}, u32[]{:S(2)}) collective-permute-start(bf16[8,128,128]{2,1,0:T(8,128)(2,1)S(1)} %add_convert_fusion.2), channel_id=1, source_target_pairs={{0,4},{4,0},{8,12},{12,8},{1,5},{5,1},{9,13},{13,9},{2,6},{6,2},{1... | collective-permute-start | bytes 786440 | tf_op jit(solution)/shard_map/ppermute | solution.py:234
  86.2 15.3 %collective-permute-start.29 = (bf16[8,128,128]{2,1,0:T(8,128)(2,1)S(1)}, bf16[8,128,128]{2,1,0:T(8,128)(2,1)S(1)}, u32[]{:S(2)}, u32[]{:S(2)}) collective-permute-start(bf16[8,128,128]{2,1,0:T(8,128)(2,1)S(1)} %add_convert_fusion.1), channel_id=1, source_target_pairs={{0,48},{16,32},{32,16},{48,0},{1,49},{17,33},{33,17},{49,1},{2,50}... | collective-permute-start | bytes 786440 | tf_op jit(solution)/shard_map/ppermute | solution.py:234
  88.6 7.8 %collective-permute-start.24 = (bf16[8,128,128]{2,1,0:T(8,128)(2,1)S(1)}, bf16[8,128,128]{2,1,0:T(8,128)(2,1)S(1)}, u32[]{:S(2)}, u32[]{:S(2)}) collective-permute-start(bf16[8,128,128]{2,1,0:T(8,128)(2,1)S(1)} %add_convert_fusion.3), channel_id=1, source_target_pairs={{0,12},{4,8},{8,4},{12,0},{1,13},{5,9},{9,5},{13,1},{2,14},{6,10},... | collective-permute-start | bytes 786440 | tf_op jit(solution)/shard_map/ppermute | solution.py:234
  96.6 5.1 %collective-permute-start.26 = (bf16[4,128,128]{2,1,0:T(8,128)(2,1)S(1)}, bf16[4,128,128]{2,1,0:T(8,128)(2,1)S(1)}, u32[]{:S(2)}, u32[]{:S(2)}) collective-permute-start(bf16[4,128,128]{2,1,0:T(8,128)(2,1)S(1)} %get-tuple-element.131), channel_id=1, source_target_pairs={{0,16},{16,0},{32,48},{48,32},{1,17},{17,1},{33,49},{49,33},{2,18}... | collective-permute-start | bytes 393224 | tf_op jit(solution)/shard_map/ppermute | solution.py:234
  97.9 6.5 %collective-permute-start.28 = (bf16[4,128,128]{2,1,0:T(8,128)(2,1)S(1)}, bf16[4,128,128]{2,1,0:T(8,128)(2,1)S(1)}, u32[]{:S(2)}, u32[]{:S(2)}) collective-permute-start(bf16[4,128,128]{2,1,0:T(8,128)(2,1)S(1)} %get-tuple-element.132), channel_id=1, source_target_pairs={{0,32},{16,48},{32,0},{48,16},{1,33},{17,49},{33,1},{49,17},{2,34}... | collective-permute-start | bytes 393224 | tf_op jit(solution)/shard_map/ppermute | solution.py:234
  99.1 6.6 %collective-permute-start.27 = (bf16[4,128,128]{2,1,0:T(8,128)(2,1)S(1)}, bf16[4,128,128]{2,1,0:T(8,128)(2,1)S(1)}, u32[]{:S(2)}, u32[]{:S(2)}) collective-permute-start(bf16[4,128,128]{2,1,0:T(8,128)(2,1)S(1)} %get-tuple-element.133), channel_id=1, source_target_pairs={{0,48},{16,32},{32,16},{48,0},{1,49},{17,33},{33,17},{49,1},{2,50}... | collective-permute-start | bytes 393224 | tf_op jit(solution)/shard_map/ppermute | solution.py:234
  105.8 10.3 %collective-permute-start.34 = (f32[4,128,128]{2,1,0:T(8,128)S(1)}, f32[4,128,128]{2,1,0:T(8,128)S(1)}, u32[]{:S(2)}, u32[]{:S(2)}) collective-permute-start(f32[4,128,128]{2,1,0:T(8,128)S(1)} %fusion.4), channel_id=1, source_target_pairs={{0,2},{2,0},{1,3},{3,1},{4,6},{6,4},{5,7},{7,5},{8,10},{10,8},{9,1... | collective-permute-start | bytes 786440 | tf_op jit(solution)/shard_map/ppermute | solution.py:234
  106.4 5.1 %collective-permute-start.31 = (bf16[4,128,128]{2,1,0:T(8,128)(2,1)S(1)}, bf16[4,128,128]{2,1,0:T(8,128)(2,1)S(1)}, u32[]{:S(2)}, u32[]{:S(2)}) collective-permute-start(bf16[4,128,128]{2,1,0:T(8,128)(2,1)S(1)} %get-tuple-element.128), channel_id=1, source_target_pairs={{0,4},{4,0},{8,12},{12,8},{1,5},{5,1},{9,13},{13,9},{2,6},{6,2},{1... | collective-permute-start | bytes 393224 | tf_op jit(solution)/shard_map/ppermute | solution.py:234
  106.5 7.8 %collective-permute-start.33 = (bf16[4,128,128]{2,1,0:T(8,128)(2,1)S(1)}, bf16[4,128,128]{2,1,0:T(8,128)(2,1)S(1)}, u32[]{:S(2)}, u32[]{:S(2)}) collective-permute-start(bf16[4,128,128]{2,1,0:T(8,128)(2,1)S(1)} %get-tuple-element.129), channel_id=1, source_target_pairs={{0,8},{4,12},{8,0},{12,4},{1,9},{5,13},{9,1},{13,5},{2,10},{6,14},... | collective-permute-start | bytes 393224 | tf_op jit(solution)/shard_map/ppermute | solution.py:234
  110.0 6.2 %collective-permute-start.32 = (bf16[4,128,128]{2,1,0:T(8,128)(2,1)S(1)}, bf16[4,128,128]{2,1,0:T(8,128)(2,1)S(1)}, u32[]{:S(2)}, u32[]{:S(2)}) collective-permute-start(bf16[4,128,128]{2,1,0:T(8,128)(2,1)S(1)} %get-tuple-element.130), channel_id=1, source_target_pairs={{0,12},{4,8},{8,4},{12,0},{1,13},{5,9},{9,5},{13,1},{2,14},{6,10},... | collective-permute-start | bytes 393224 | tf_op jit(solution)/shard_map/ppermute | solution.py:234
  116.2 11.1 %collective-permute-start.37 = (bf16[4,128,128]{2,1,0:T(8,128)(2,1)S(1)}, bf16[4,128,128]{2,1,0:T(8,128)(2,1)S(1)}, u32[]{:S(2)}, u32[]{:S(2)}) collective-permute-start(bf16[4,128,128]{2,1,0:T(8,128)(2,1)S(1)} %fusion.7.a), channel_id=1, source_target_pairs={{0,192},{64,128},{128,64},{192,0},{1,193},{65,129},{129,65},{193,1... | collective-permute-start | bytes 393224 | tf_op jit(solution)/shard_map/ppermute | solution.py:234
  118.8 9.7 %collective-permute-start.36 = (bf16[4,128,128]{2,1,0:T(8,128)(2,1)S(1)}, bf16[4,128,128]{2,1,0:T(8,128)(2,1)S(1)}, u32[]{:S(2)}, u32[]{:S(2)}) collective-permute-start(bf16[4,128,128]{2,1,0:T(8,128)(2,1)S(1)} %fusion.7.a), channel_id=1, source_target_pairs={{0,128},{64,192},{128,0},{192,64},{1,129},{65,193},{129,1},{193,65... | collective-permute-start | bytes 393224 | tf_op jit(solution)/shard_map/ppermute | solution.py:234
  123.1 7.2 %collective-permute-start.35 = (bf16[4,128,128]{2,1,0:T(8,128)(2,1)S(1)}, bf16[4,128,128]{2,1,0:T(8,128)(2,1)S(1)}, u32[]{:S(2)}, u32[]{:S(2)}) collective-permute-start(bf16[4,128,128]{2,1,0:T(8,128)(2,1)S(1)} %fusion.7.a), channel_id=1, source_target_pairs={{0,64},{64,0},{128,192},{192,128},{1,65},{65,1},{129,193},{193,129... | collective-permute-start | bytes 393224 | tf_op jit(solution)/shard_map/ppermute | solution.py:234
  130.6 6.3 %collective-permute-start.40 = (bf16[4,128,128]{2,1,0:T(8,128)(2,1)S(1)}, bf16[4,128,128]{2,1,0:T(8,128)(2,1)S(1)}, u32[]{:S(2)}, u32[]{:S(2)}) collective-permute-start(bf16[4,128,128]{2,1,0:T(8,128)(2,1)S(1)} %shard_map.77.refs_0_), channel_id=1, source_target_pairs={{0,48},{16,32},{32,16},{48,0},{1,49},{17,33},{33,17},{49,1},{2,50}... | collective-permute-start | bytes 393224 | tf_op jit(solution)/shard_map/ppermute | solution.py:234
  132.3 6.5 %collective-permute-start.39 = (bf16[4,128,128]{2,1,0:T(8,128)(2,1)S(1)}, bf16[4,128,128]{2,1,0:T(8,128)(2,1)S(1)}, u32[]{:S(2)}, u32[]{:S(2)}) collective-permute-start(bf16[4,128,128]{2,1,0:T(8,128)(2,1)S(1)} %shard_map.77.refs_0_), channel_id=1, source_target_pairs={{0,32},{16,48},{32,0},{48,16},{1,33},{17,49},{33,1},{49,17},{2,34}... | collective-permute-start | bytes 393224 | tf_op jit(solution)/shard_map/ppermute | solution.py:234
  133.1 6.0 %collective-permute-start.38 = (bf16[4,128,128]{2,1,0:T(8,128)(2,1)S(1)}, bf16[4,128,128]{2,1,0:T(8,128)(2,1)S(1)}, u32[]{:S(2)}, u32[]{:S(2)}) collective-permute-start(bf16[4,128,128]{2,1,0:T(8,128)(2,1)S(1)} %shard_map.77.refs_0_), channel_id=1, source_target_pairs={{0,16},{16,0},{32,48},{48,32},{1,17},{17,1},{33,49},{49,33},{2,18}... | collective-permute-start | bytes 393224 | tf_op jit(solution)/shard_map/ppermute | solution.py:234

commit v5 on v4

--- a/solution.py
+++ b/solution.py
@@ -50,11 +50,11 @@
 
 ROUNDS = (
     (0, 0, 0, 16),
+    (1, 0, 0, 16),
     (3, 0, 0, 16),
-    (1, 0, 0, 16),
     (0, 1, 0, 16),
+    (1, 1, 0, 16),
     (3, 1, 0, 16),
-    (1, 1, 0, 16),
     (2, 0, 0, 8),
     (2, 0, 8, 8),
     (2, 1, 0, 8),
@@ -63,19 +63,19 @@
 FIRST = tuple((*ROUNDS[i][:2], 0, *ROUNDS[i][2:]) for i in range(4)) + ((0, 0, 1, 0, 16),)
 MIDDLE = (
     *((*ROUNDS[i][:2], 0, *ROUNDS[i][2:]) for i in range(4, 8)),
-    *((*ROUNDS[i][:2], 1, *ROUNDS[i][2:]) for i in range(1, 4)),
-    (2, 0, 1, 0, 16),
+    *((*ROUNDS[i][:2], 1, *ROUNDS[i][2:]) for i in range(1, 5)),
 )
 LAST = (
     *((*ROUNDS[i][:2], 0, *ROUNDS[i][2:]) for i in (8, 9)),
-    *((*ROUNDS[i][:2], 1, *ROUNDS[i][2:]) for i in (4, 5, 8, 9)),
+    *((*ROUNDS[i][:2], 1, *ROUNDS[i][2:]) for i in (5, 8, 9)),
+    (2, 0, 1, 0, 16),
 )
 
 
 def place_copies(where, listed, pieces, w_ref, sems):
     copies = []
     for i, (x, zl, core, first, size) in enumerate(listed):
-        owner = (lax.rem(where[0] + x, 4) * 2 + (where[2] ^ zl)) * 2 + (where[3] ^ core)
+        owner = ((where[0] ^ x) * 2 + (where[2] ^ zl)) * 2 + (where[3] ^ core)
         to = w_ref.at[pl.ds(owner * 16 + first, size)]
         copies.append(pltpu.make_async_copy(pieces[i], to, sems.at[i]))
     return copies
@@ -234,10 +234,10 @@
     return lax.ppermute(value, axis, [(i, i ^ mask) for i in range(size)])
 
 
-def turn(value, axes, by):
-    names = axes if isinstance(axes, tuple) else (axes,)
-    size = math.prod(SIZES[AXES.index(name)] for name in names)
-    return lax.ppermute(value, axes, [(i, (i + by) % size) for i in range(size)])
+def cross(value):
+    return lax.ppermute(
+        value, Z, [(z, (z + 1) % 8 if z % 2 else (z - 1) % 8) for z in range(8)]
+    )
 
 
 def tables(tile_row, tile_column):
@@ -265,7 +265,7 @@
     where = jnp.stack([lax.axis_index(a) for a in ("x", "y", "zl", "core")]).astype(jnp.int32)
     place, blocks = tables(tile_row, tile_column)
     own = weight_tiles
-    left, right = turn(own, "x", 1), turn(own, "x", 3)
+    left, right = swap(own, "x", 1), swap(own, "x", 3)
     beside = swap(own, "zl", 1)
     others = swap(features, "core", 1)
     own_other = swap(own, "core", 1)
@@ -296,15 +296,15 @@
         scratch_shapes=[pltpu.SemaphoreType.DMA((2,))],
         compiler_params=PARAMS,
     )(near(left), near(right))
-    second = [turn(left, Z, 1), turn(right, Z, 7), turn(low, "x", 1), turn(high, "x", 3)]
+    second = [swap(left, "zl", 1), cross(right), swap(low, "x", 3), swap(high, "x", 1)]
     crossed = [swap(left, "core", 1)]
     second, crossed, whole, right, beside = lax.optimization_barrier(
         (second, crossed, whole, right, beside)
     )
     far = second[2:]
-    beside_far = (turn(far[0], Z, 1), turn(far[1], Z, 7))
+    beside_far = (swap(far[0], "zl", 1), cross(far[1]))
     both_far = jnp.concatenate(far, axis=0)
-    crossed += [swap(piece, "core", 1) for piece in (right, beside, both_far)]
+    crossed += [swap(piece, "core", 1) for piece in (right, beside, second[0])]
     whole = pl.pallas_call(
         more_kernel,
         out_shape=pltpu.VMEM((256, SIDE, SIDE), bf16),
@@ -314,8 +314,8 @@
         input_output_aliases={1: 0},
         compiler_params=PARAMS,
     )(where, near(whole), *(near(piece) for piece in (*second, *crossed)))
-    *beside_far, whole = lax.optimization_barrier((*beside_far, whole))
-    crossed = [swap(piece, "core", 1) for piece in (*second[:2], *beside_far)]
+    *beside_far, whole, both_far = lax.optimization_barrier((*beside_far, whole, both_far))
+    crossed = [swap(piece, "core", 1) for piece in (second[1], *beside_far, both_far)]
     late = [near(piece) for piece in (*beside_far, *crossed)]
     slopes, whole = pl.pallas_call(
         forward_kernel,

time: 142 us -> 140 us (0.986)
  waiting for transfers between devices: 50.4 us -> 47.8 us
    ppermute x8 -> x2, waiting for transfers between devices: 15.5 us -> 2.59 us  [cross(): lax.ppermute(value, Z, [(z, (z + 1) % 8 if z % 2 else (z - 1) % 8) for z...]
    ppermute x33 -> x39, waiting for transfers between devices: 34.9 us -> 45.2 us  [swap(): return lax.ppermute(value, axis, [(i, i ^ mask) for i in range(size)])]
    ppermute x33 -> x39, starting transfers between devices: 35.9 us -> 44.5 us  [swap(): return lax.ppermute(value, axis, [(i, i ^ mask) for i in range(size)])]
    ppermute x8 -> x2, starting transfers between devices: 11.4 us -> 3.07 us  [cross(): lax.ppermute(value, Z, [(z, (z + 1) % 8 if z % 2 else (z - 1) % 8) for z...]
  transfers between devices with their start and end apart: 41 -> 41, of which waited for: 26 -> 25; matrix products, arithmetic and copies ran while one was open for 3% -> 4% of each run, Pallas kernels for 18% -> 18%
where the time goes in v5:
time: 140 us; the launch traced here: 138 us
  waiting for transfers between devices  47.8 us (34%)
  starting transfers between devices  47.5 us (34%)
  Pallas kernels  35 us (25%)
  other arithmetic  5.08 us (4%)
  between operations  2.91 us (2%)
    ppermute x39, waiting for transfers between devices, swap(): return lax.ppermute(value, axis, [(i, i ^ mask) for i in range(size)])  45.2 us
    ppermute x39, starting transfers between devices, swap(): return lax.ppermute(value, axis, [(i, i ^ mask) for i in range(size)])  44.5 us
    pallas_call x1, Pallas kernels, on_device(): pl.pallas_call(forward_kernel, out_shape=[pltpu.VMEM((64, rows_here, SIDE...  5.88 us
    pallas_call x1, Pallas kernels, on_device(): pl.pallas_call(transpose_kernel, out_shape=pltpu.VMEM((64, SIDE, 2 * rows...  5.76 us
    pallas_call x1, Pallas kernels, on_device(): pl.pallas_call(load_kernel, out_shape=[pltpu.VMEM(features.shape, bf16),...  4.24 us
    pallas_call x1, Pallas kernels, on_device(): backward(functools.partial(backward_kernel, 0), in_specs=[SMEM] * 2 + [VM...  4.21 us
    pallas_call x1, Pallas kernels, on_device(): backward(functools.partial(backward_kernel, 1), in_specs=[SMEM] * 2 + [VM...  4.19 us
    ppermute x2, starting transfers between devices, cross(): lax.ppermute(value, Z, [(z, (z + 1) % 8 if z % 2 else (z - 1) % 8) for z...  3.07 us
  transfers between devices with their start and end apart: 41, of which 25 were waited for; matrix products, arithmetic and copies ran while one was open for 4% of the time, Pallas kernels for 18%

profile of v5, /device:TPU:32, one launch (start us, length us, event | category | flops | bytes accessed | tf_op | source)
XLA Modules:
  0.0 138.4 jit_solution(5179063260029585848)
XLA Ops:
  0.7 1.9 %collective-permute-start.2 = (bf16[16,128,128]{2,1,0:T(8,128)(2,1)}, bf16[16,128,128]{2,1,0:T(8,128)(2,1)}, u32[]{:S(2)}, u32[]{:S(2)}) collective-permute-start(bf16[16,128,128]{2,1,0:T(8,128)(2,1)} %refs_0_.1), channel_id=1, source_target_pairs={{0,2},{2,0},{1,3},{3,1},{4,6},{6,4},{5,7},{7,5},{8,10},{10,8},{9,1... | collective-permute-start | bytes 1572872 | tf_op jit(solution)/shard_map/ppermute | solution.py:234
  3.9 1.3 fusion.10
  8.9 6.6 %collective-permute-done.2.refs_3_ = bf16[16,128,128]{2,1,0:T(8,128)(2,1)} collective-permute-done((bf16[16,128,128]{2,1,0:T(8,128)(2,1)}, bf16[16,128,128]{2,1,0:T(8,128)(2,1)}, u32[]{:S(2)}, u32[]{:S(2)}) %collective-permute-start.2) | collective-permute-done | bytes 524320 | tf_op jit(solution)/shard_map/ppermute | solution.py:234
  15.5 2.7 %collective-permute-done.1.refs_2_.right = bf16[16,128,128]{2,1,0:T(8,128)(2,1)} collective-permute-done((bf16[16,128,128]{2,1,0:T(8,128)(2,1)}, bf16[16,128,128]{2,1,0:T(8,128)(2,1)}, u32[]{:S(2)}, u32[]{:S(2)}) %collective-permute-start.1) | collective-permute-done | bytes 524320 | tf_op jit(solution)/shard_map/ppermute | solution.py:234
  18.3 1.4 %collective-permute-start.5 = (bf16[16,128,128]{2,1,0:T(8,128)(2,1)}, bf16[16,128,128]{2,1,0:T(8,128)(2,1)}, u32[]{:S(2)}, u32[]{:S(2)}) collective-permute-start(bf16[16,128,128]{2,1,0:T(8,128)(2,1)} %collective-permute-done.refs_1_.left), channel_id=1, source_target_pairs={{0,2},{2,0},{1,3},{3,1},{4,6},{6,4},{5,7},{7,5},{8,10},{10,8},{9,1... | collective-permute-start | bytes 1572872 | tf_op jit(solution)/shard_map/ppermute | solution.py:234
  19.7 2.1 %collective-permute-start.6 = (bf16[16,128,128]{2,1,0:T(8,128)(2,1)}, bf16[16,128,128]{2,1,0:T(8,128)(2,1)}, u32[]{:S(2)}, u32[]{:S(2)}) collective-permute-start(bf16[16,128,128]{2,1,0:T(8,128)(2,1)} %collective-permute-done.1.refs_2_.right), channel_id=1, source_target_pairs={{0,194},{2,64},{64,2},{66,128},{128,66},{130,192},{192,130},{194,0... | collective-permute-start | bytes 1572872 | tf_op jit(solution)/shard_map/ppermute | solution.py:238
  21.8 1.8 %shard_map.69 = (bf16[8,128,128]{2,1,0:T(8,128)(2,1)}, bf16[8,128,128]{2,1,0:T(8,128)(2,1)}) custom-call(bf16[16,128,128]{2,1,0:T(8,128)(2,1)} %collective-permute-done.refs_1_.left, bf16[16,128,128]{2,1,0:T(8,128)(2,1)} %collective-permute-done.1.refs_2_.right), custom_call_target="tpu_custom_call" | custom-call | tf_op jit(solution)/shard_map/pallas_call | solution.py:291
  23.6 1.7 %collective-permute-start.7 = (bf16[8,128,128]{2,1,0:T(8,128)(2,1)}, bf16[8,128,128]{2,1,0:T(8,128)(2,1)S(1)}, u32[]{:S(2)}, u32[]{:S(2)}) collective-permute-start(bf16[8,128,128]{2,1,0:T(8,128)(2,1)} %get-tuple-element.73), channel_id=1, source_target_pairs={{0,12},{4,8},{8,4},{12,0},{1,13},{5,9},{9,5},{13,1},{2,14},{6,10},... | collective-permute-start | bytes 786440 | tf_op jit(solution)/shard_map/ppermute | solution.py:234
  25.4 4.2 %shard_map.68 = (bf16[192,8192]{1,0:T(8,128)(2,1)S(1)}, bf16[192,8192]{1,0:T(8,128)(2,1)S(1)}, bf16[256,128,128]{2,1,0:T(8,128)(2,1)S(1)}) custom-call(s32[4]{0:T(128)S(1)} %pad_add_fusion.1.where, bf16[192,8192]{1,0:T(8,128)(2,1)} %x_hbm.1, bf16[192,8192]{1,0:T(8,128)(2,1)} %g_hbm.1, bf16[16,128,128]{2,1,0:T(8,128)(2,1)} %refs_0_.1, ...), custom_call_target="tpu_custom_call" | custom-call | tf_op jit(solution)/shard_map/pallas_call | solution.py:275
  29.6 3.6 %collective-permute-done.7.refs_2_ = bf16[8,128,128]{2,1,0:T(8,128)(2,1)S(1)} collective-permute-done((bf16[8,128,128]{2,1,0:T(8,128)(2,1)}, bf16[8,128,128]{2,1,0:T(8,128)(2,1)S(1)}, u32[]{:S(2)}, u32[]{:S(2)}) %collective-permute-start.7) | collective-permute-done | bytes 262176 | tf_op jit(solution)/shard_map/ppermute | solution.py:234
  34.9 3.9 %collective-permute-start.10 = (bf16[8,128,128]{2,1,0:T(8,128)(2,1)S(1)}, bf16[8,128,128]{2,1,0:T(8,128)(2,1)S(1)}, u32[]{:S(2)}, u32[]{:S(2)}) collective-permute-start(bf16[8,128,128]{2,1,0:T(8,128)(2,1)S(1)} %collective-permute-done.7.refs_2_), channel_id=1, source_target_pairs={{0,2},{2,0},{1,3},{3,1},{4,6},{6,4},{5,7},{7,5},{8,10},{10,8},{9,1... | collective-permute-start | bytes 786440 | tf_op jit(solution)/shard_map/ppermute | solution.py:234
  40.9 2.1 %shard_map.70.given = bf16[256,128,128]{2,1,0:T(8,128)(2,1)S(1)} custom-call(s32[4]{0:T(128)S(1)} %pad_add_fusion.1.where, bf16[256,128,128]{2,1,0:T(8,128)(2,1)S(1)} %get-tuple-element.78.given, bf16[16,128,128]{2,1,0:T(8,128)(2,1)} %collective-permute-done.5.refs_0_, ...), custom_call_target="tpu_custom_call", output_to_operand_aliasing={{}: (1, {})} | custom-call | tf_op jit(solution)/shard_map/pallas_call | solution.py:308
  43.0 2.7 %collective-permute-done.10.refs_0_ = bf16[8,128,128]{2,1,0:T(8,128)(2,1)S(1)} collective-permute-done((bf16[8,128,128]{2,1,0:T(8,128)(2,1)S(1)}, bf16[8,128,128]{2,1,0:T(8,128)(2,1)S(1)}, u32[]{:S(2)}, u32[]{:S(2)}) %collective-permute-start.10) | collective-permute-done | bytes 262176 | tf_op jit(solution)/shard_map/ppermute | solution.py:234
  45.7 1.7 %collective-permute-done.11.refs_1_ = bf16[8,128,128]{2,1,0:T(8,128)(2,1)S(1)} collective-permute-done((bf16[8,128,128]{2,1,0:T(8,128)(2,1)}, bf16[8,128,128]{2,1,0:T(8,128)(2,1)S(1)}, u32[]{:S(2)}, u32[]{:S(2)}) %collective-permute-start.11) | collective-permute-done | bytes 262176 | tf_op jit(solution)/shard_map/ppermute | solution.py:238
  47.9 1.8 %collective-permute-done.16.refs_3_ = bf16[8,128,128]{2,1,0:T(8,128)(2,1)S(1)} collective-permute-done((bf16[8,128,128]{2,1,0:T(8,128)(2,1)S(1)}, bf16[8,128,128]{2,1,0:T(8,128)(2,1)S(1)}, u32[]{:S(2)}, u32[]{:S(2)}) %collective-permute-start.16) | collective-permute-done | bytes 262176 | tf_op jit(solution)/shard_map/ppermute | solution.py:234
  50.1 5.9 %shard_map.71 = (bf16[64,192,128]{2,1,0:T(8,128)(2,1)S(1)}, bf16[256,128,128]{2,1,0:T(8,128)(2,1)S(1)}) custom-call(s32[4]{0:T(128)S(1)} %pad_add_fusion.1.where, s32[256]{0:T(256)S(1)} %select_reduce_fusion.place, s32[64]{0:T(128)S(1)} %xor.28.blocks, bf16[192,8192]{1,0:T(8,128)(2,1)S(1)} %get-tuple-element.70.x_ref.mine_ref, ...), custom_call_target="tpu_custom_call", output_to_operand_aliasing={{1}: (5, {})} | custom-call | tf_op jit(solution)/shard_map/pallas_call | solution.py:320
  56.2 5.8 %shard_map.72.xt_ref = bf16[64,128,384]{2,1,0:T(8,128)(2,1)S(1)} custom-call(bf16[192,8192]{1,0:T(8,128)(2,1)S(1)} %get-tuple-element.70.x_ref.mine_ref, bf16[192,8192]{1,0:T(8,128)(2,1)S(1)} %collective-permute-done.3.other_ref), custom_call_target="tpu_custom_call" | custom-call | tf_op jit(solution)/shard_map/pallas_call | solution.py:334
  62.0 2.5 %shard_map.73 = (bf16[16,128,128]{2,1,0:T(8,128)(2,1)S(1)}, bf16[16,128,128]{2,1,0:T(8,128)(2,1)S(1)}, bf16[16,128,128]{2,1,0:T(8,128)(2,1)S(1)}, bf16[16,128,128]{2,1,0:T(8,128)(2,1)S(1)}) custom-call(s32[256]{0:T(256)S(1)} %copy-done, s32[256]{0:T(256)S(1)} %copy-done.1, s32[4]{0:T(128)S(1)} %pad_add_fusion.1.where, ...), custom_call_target="tpu_custom_call" | custom-call | tf_op jit(solution)/shard_map/pallas_call | solution.py:342
  64.9 1.4 collective-permute-start.21
  66.3 1.6 %collective-permute-start.22 = (bf16[16,128,128]{2,1,0:T(8,128)(2,1)S(1)}, bf16[16,128,128]{2,1,0:T(8,128)(2,1)S(1)}, u32[]{:S(2)}, u32[]{:S(2)}) collective-permute-start(bf16[16,128,128]{2,1,0:T(8,128)(2,1)S(1)} %get-tuple-element.94), channel_id=1, source_target_pairs={{0,16},{16,0},{32,48},{48,32},{1,17},{17,1},{33,49},{49,33},{2,18}... | collective-permute-start | bytes 1572872 | tf_op jit(solution)/shard_map/ppermute | solution.py:234
  67.8 2.2 %collective-permute-start.23 = (bf16[16,128,128]{2,1,0:T(8,128)(2,1)S(1)}, bf16[16,128,128]{2,1,0:T(8,128)(2,1)S(1)}, u32[]{:S(2)}, u32[]{:S(2)}) collective-permute-start(bf16[16,128,128]{2,1,0:T(8,128)(2,1)S(1)} %get-tuple-element.95), channel_id=1, source_target_pairs={{0,48},{16,32},{32,16},{48,0},{1,49},{17,33},{33,17},{49,1},{2,50}... | collective-permute-start | bytes 1572872 | tf_op jit(solution)/shard_map/ppermute | solution.py:234
  70.0 2.4 %shard_map.74 = (f32[8,128,128]{2,1,0:T(8,128)S(1)}, f32[8,128,128]{2,1,0:T(8,128)S(1)}, f32[8,128,128]{2,1,0:T(8,128)S(1)}, f32[8,128,128]{2,1,0:T(8,128)S(1)},...) custom-call(s32[256]{0:T(256)S(1)} %copy-done, ...), custom_call_target="tpu_custom_call" | custom-call | tf_op jit(solution)/shard_map/pallas_call | solution.py:352
  72.5 4.2 %shard_map.75.refs_0_ = bf16[192,8192]{1,0:T(8,128)(2,1)} custom-call(s32[256]{0:T(256)S(1)} %select_reduce_fusion.place, s32[64]{0:T(128)S(1)} %xor.28.blocks, bf16[192,8192]{1,0:T(8,128)(2,1)S(1)} %get-tuple-element.72.g_ref, bf16[256,128,128]{2,1,0:T(8,128)(2,1)S(1)} %get-tuple-element.106.w_ref, bf16[64,192,128]{2,1,0:T(8,128)(2,1)S(1)} %get-tuple-element.91.s_ref), custom_call_target="tpu_custom_call" | custom-call | tf_op jit(solution)/shard_map/pallas_call | solution.py:371
  76.7 2.1 %collective-permute-done.20 = bf16[16,128,128]{2,1,0:T(8,128)(2,1)S(1)} collective-permute-done((bf16[16,128,128]{2,1,0:T(8,128)(2,1)S(1)}, bf16[16,128,128]{2,1,0:T(8,128)(2,1)S(1)}, u32[]{:S(2)}, u32[]{:S(2)}) %collective-permute-start.20) | collective-permute-done | bytes 524320 | tf_op jit(solution)/shard_map/ppermute | solution.py:234
  78.8 1.3 collective-permute-done.21
  80.2 2.5 %collective-permute-done.23 = bf16[16,128,128]{2,1,0:T(8,128)(2,1)S(1)} collective-permute-done((bf16[16,128,128]{2,1,0:T(8,128)(2,1)S(1)}, bf16[16,128,128]{2,1,0:T(8,128)(2,1)S(1)}, u32[]{:S(2)}, u32[]{:S(2)}) %collective-permute-start.23) | collective-permute-done | bytes 524320 | tf_op jit(solution)/shard_map/ppermute | solution.py:234
  84.1 2.3 %collective-permute-start.29 = (bf16[8,128,128]{2,1,0:T(8,128)(2,1)S(1)}, bf16[8,128,128]{2,1,0:T(8,128)(2,1)S(1)}, u32[]{:S(2)}, u32[]{:S(2)}) collective-permute-start(bf16[8,128,128]{2,1,0:T(8,128)(2,1)S(1)} %add_convert_fusion.1), channel_id=1, source_target_pairs={{0,48},{16,32},{32,16},{48,0},{1,49},{17,33},{33,17},{49,1},{2,50}... | collective-permute-start | bytes 786440 | tf_op jit(solution)/shard_map/ppermute | solution.py:234
  86.5 1.7 %collective-permute-start.24 = (bf16[8,128,128]{2,1,0:T(8,128)(2,1)S(1)}, bf16[8,128,128]{2,1,0:T(8,128)(2,1)S(1)}, u32[]{:S(2)}, u32[]{:S(2)}) collective-permute-start(bf16[8,128,128]{2,1,0:T(8,128)(2,1)S(1)} %add_convert_fusion.3), channel_id=1, source_target_pairs={{0,12},{4,8},{8,4},{12,0},{1,13},{5,9},{9,5},{13,1},{2,14},{6,10},... | collective-permute-start | bytes 786440 | tf_op jit(solution)/shard_map/ppermute | solution.py:234
  88.3 1.9 %collective-permute-done.25 = bf16[8,128,128]{2,1,0:T(8,128)(2,1)S(1)} collective-permute-done((bf16[8,128,128]{2,1,0:T(8,128)(2,1)S(1)}, bf16[8,128,128]{2,1,0:T(8,128)(2,1)S(1)}, u32[]{:S(2)}, u32[]{:S(2)}) %collective-permute-start.25) | collective-permute-done | bytes 262176 | tf_op jit(solution)/shard_map/ppermute | solution.py:234
  90.2 4.0 %collective-permute-done.24 = bf16[8,128,128]{2,1,0:T(8,128)(2,1)S(1)} collective-permute-done((bf16[8,128,128]{2,1,0:T(8,128)(2,1)S(1)}, bf16[8,128,128]{2,1,0:T(8,128)(2,1)S(1)}, u32[]{:S(2)}, u32[]{:S(2)}) %collective-permute-start.24) | collective-permute-done | bytes 262176 | tf_op jit(solution)/shard_map/ppermute | solution.py:234
  94.4 1.4 %collective-permute-start.26 = (bf16[4,128,128]{2,1,0:T(8,128)(2,1)S(1)}, bf16[4,128,128]{2,1,0:T(8,128)(2,1)S(1)}, u32[]{:S(2)}, u32[]{:S(2)}) collective-permute-start(bf16[4,128,128]{2,1,0:T(8,128)(2,1)S(1)} %get-tuple-element.133), channel_id=1, source_target_pairs={{0,16},{16,0},{32,48},{48,32},{1,17},{17,1},{33,49},{49,33},{2,18}... | collective-permute-start | bytes 393224 | tf_op jit(solution)/shard_map/ppermute | solution.py:234
  97.0 2.2 %collective-permute-start.27 = (bf16[4,128,128]{2,1,0:T(8,128)(2,1)S(1)}, bf16[4,128,128]{2,1,0:T(8,128)(2,1)S(1)}, u32[]{:S(2)}, u32[]{:S(2)}) collective-permute-start(bf16[4,128,128]{2,1,0:T(8,128)(2,1)S(1)} %get-tuple-element.135), channel_id=1, source_target_pairs={{0,48},{16,32},{32,16},{48,0},{1,49},{17,33},{33,17},{49,1},{2,50}... | collective-permute-start | bytes 393224 | tf_op jit(solution)/shard_map/ppermute | solution.py:234
  99.5 2.9 %collective-permute-done.28 = bf16[4,128,128]{2,1,0:T(8,128)(2,1)S(1)} collective-permute-done((bf16[4,128,128]{2,1,0:T(8,128)(2,1)S(1)}, bf16[4,128,128]{2,1,0:T(8,128)(2,1)S(1)}, u32[]{:S(2)}, u32[]{:S(2)}) %collective-permute-start.28) | collective-permute-done | bytes 131104 | tf_op jit(solution)/shard_map/ppermute | solution.py:234
  102.4 1.3 collective-permute-done.27
  103.8 1.6 %collective-permute-start.34 = (f32[4,128,128]{2,1,0:T(8,128)S(1)}, f32[4,128,128]{2,1,0:T(8,128)S(1)}, u32[]{:S(2)}, u32[]{:S(2)}) collective-permute-start(f32[4,128,128]{2,1,0:T(8,128)S(1)} %fusion.4), channel_id=1, source_target_pairs={{0,2},{2,0},{1,3},{3,1},{4,6},{6,4},{5,7},{7,5},{8,10},{10,8},{9,1... | collective-permute-start | bytes 786440 | tf_op jit(solution)/shard_map/ppermute | solution.py:234
  105.6 3.1 %collective-permute-start.33 = (bf16[4,128,128]{2,1,0:T(8,128)(2,1)S(1)}, bf16[4,128,128]{2,1,0:T(8,128)(2,1)S(1)}, u32[]{:S(2)}, u32[]{:S(2)}) collective-permute-start(bf16[4,128,128]{2,1,0:T(8,128)(2,1)S(1)} %get-tuple-element.131), channel_id=1, source_target_pairs={{0,8},{4,12},{8,0},{12,4},{1,9},{5,13},{9,1},{13,5},{2,10},{6,14},... | collective-permute-start | bytes 393224 | tf_op jit(solution)/shard_map/ppermute | solution.py:234
  108.7 1.6 %collective-permute-start.32 = (bf16[4,128,128]{2,1,0:T(8,128)(2,1)S(1)}, bf16[4,128,128]{2,1,0:T(8,128)(2,1)S(1)}, u32[]{:S(2)}, u32[]{:S(2)}) collective-permute-start(bf16[4,128,128]{2,1,0:T(8,128)(2,1)S(1)} %get-tuple-element.132), channel_id=1, source_target_pairs={{0,12},{4,8},{8,4},{12,0},{1,13},{5,9},{9,5},{13,1},{2,14},{6,10},... | collective-permute-start | bytes 393224 | tf_op jit(solution)/shard_map/ppermute | solution.py:234
  110.6 2.5 %collective-permute-done.33 = bf16[4,128,128]{2,1,0:T(8,128)(2,1)S(1)} collective-permute-done((bf16[4,128,128]{2,1,0:T(8,128)(2,1)S(1)}, bf16[4,128,128]{2,1,0:T(8,128)(2,1)S(1)}, u32[]{:S(2)}, u32[]{:S(2)}) %collective-permute-start.33) | collective-permute-done | bytes 131104 | tf_op jit(solution)/shard_map/ppermute | solution.py:234
  113.0 1.8 %collective-permute-done.32 = bf16[4,128,128]{2,1,0:T(8,128)(2,1)S(1)} collective-permute-done((bf16[4,128,128]{2,1,0:T(8,128)(2,1)S(1)}, bf16[4,128,128]{2,1,0:T(8,128)(2,1)S(1)}, u32[]{:S(2)}, u32[]{:S(2)}) %collective-permute-start.32) | collective-permute-done | bytes 131104 | tf_op jit(solution)/shard_map/ppermute | solution.py:234
  115.0 3.0 %collective-permute-start.37 = (bf16[4,128,128]{2,1,0:T(8,128)(2,1)S(1)}, bf16[4,128,128]{2,1,0:T(8,128)(2,1)S(1)}, u32[]{:S(2)}, u32[]{:S(2)}) collective-permute-start(bf16[4,128,128]{2,1,0:T(8,128)(2,1)S(1)} %fusion.7.a), channel_id=1, source_target_pairs={{0,192},{64,128},{128,64},{192,0},{1,193},{65,129},{129,65},{193,1... | collective-permute-start | bytes 393224 | tf_op jit(solution)/shard_map/ppermute | solution.py:234
  118.0 1.6 %collective-permute-start.36 = (bf16[4,128,128]{2,1,0:T(8,128)(2,1)S(1)}, bf16[4,128,128]{2,1,0:T(8,128)(2,1)S(1)}, u32[]{:S(2)}, u32[]{:S(2)}) collective-permute-start(bf16[4,128,128]{2,1,0:T(8,128)(2,1)S(1)} %fusion.7.a), channel_id=1, source_target_pairs={{0,128},{64,192},{128,0},{192,64},{1,129},{65,193},{129,1},{193,65... | collective-permute-start | bytes 393224 | tf_op jit(solution)/shard_map/ppermute | solution.py:234
  119.6 2.0 %collective-permute-start.35 = (bf16[4,128,128]{2,1,0:T(8,128)(2,1)S(1)}, bf16[4,128,128]{2,1,0:T(8,128)(2,1)S(1)}, u32[]{:S(2)}, u32[]{:S(2)}) collective-permute-start(bf16[4,128,128]{2,1,0:T(8,128)(2,1)S(1)} %fusion.7.a), channel_id=1, source_target_pairs={{0,64},{64,0},{128,192},{192,128},{1,65},{65,1},{129,193},{193,129... | collective-permute-start | bytes 393224 | tf_op jit(solution)/shard_map/ppermute | solution.py:234
  121.6 4.2 %shard_map.76 = bf16[192,8192]{1,0:T(8,128)(2,1)} custom-call(s32[256]{0:T(256)S(1)} %select_reduce_fusion.place, s32[64]{0:T(128)S(1)} %xor.28.blocks, bf16[192,8192]{1,0:T(8,128)(2,1)S(1)} %get-tuple-element.72.g_ref, bf16[256,128,128]{2,1,0:T(8,128)(2,1)S(1)} %get-tuple-element.106.w_ref, ...), custom_call_target="tpu_custom_call", output_to_operand_aliasing={{}: (5, {})} | custom-call | tf_op jit(solution)/shard_map/pallas_call | solution.py:397
  128.3 1.9 %collective-permute-start.40 = (bf16[4,128,128]{2,1,0:T(8,128)(2,1)S(1)}, bf16[4,128,128]{2,1,0:T(8,128)(2,1)S(1)}, u32[]{:S(2)}, u32[]{:S(2)}) collective-permute-start(bf16[4,128,128]{2,1,0:T(8,128)(2,1)S(1)} %shard_map.77.refs_0_), channel_id=1, source_target_pairs={{0,48},{16,32},{32,16},{48,0},{1,49},{17,33},{33,17},{49,1},{2,50}... | collective-permute-start | bytes 393224 | tf_op jit(solution)/shard_map/ppermute | solution.py:234
  130.8 1.7 %collective-permute-start.38 = (bf16[4,128,128]{2,1,0:T(8,128)(2,1)S(1)}, bf16[4,128,128]{2,1,0:T(8,128)(2,1)S(1)}, u32[]{:S(2)}, u32[]{:S(2)}) collective-permute-start(bf16[4,128,128]{2,1,0:T(8,128)(2,1)S(1)} %shard_map.77.refs_0_), channel_id=1, source_target_pairs={{0,16},{16,0},{32,48},{48,32},{1,17},{17,1},{33,49},{49,33},{2,18}... | collective-permute-start | bytes 393224 | tf_op jit(solution)/shard_map/ppermute | solution.py:234
  132.5 2.1 %collective-permute-done.40.refs_3_ = bf16[4,128,128]{2,1,0:T(8,128)(2,1)S(1)} collective-permute-done((bf16[4,128,128]{2,1,0:T(8,128)(2,1)S(1)}, bf16[4,128,128]{2,1,0:T(8,128)(2,1)S(1)}, u32[]{:S(2)}, u32[]{:S(2)}) %collective-permute-start.40) | collective-permute-done | bytes 131104 | tf_op jit(solution)/shard_map/ppermute | solution.py:234
  134.6 2.1 %collective-permute-done.39.refs_2_ = bf16[4,128,128]{2,1,0:T(8,128)(2,1)S(1)} collective-permute-done((bf16[4,128,128]{2,1,0:T(8,128)(2,1)S(1)}, bf16[4,128,128]{2,1,0:T(8,128)(2,1)S(1)}, u32[]{:S(2)}, u32[]{:S(2)}) %collective-permute-start.39) | collective-permute-done | bytes 131104 | tf_op jit(solution)/shard_map/ppermute | solution.py:234
  136.8 1.6 %shard_map.78 = f32[16,128,128]{2,1,0:T(8,128)} custom-call(s32[4]{0:T(128)S(1)} %pad_add_fusion.1.where, bf16[4,128,128]{2,1,0:T(8,128)(2,1)S(1)} %shard_map.77.refs_0_, bf16[4,128,128]{2,1,0:T(8,128)(2,1)S(1)} %collective-permute-done.38.refs_1_, bf16[4,128,128]{2,1,0:T(8,128)(2,1)S(1)} %collective-permute-done.39.refs_2_, ...), custom_call_target="tpu_custom_call" | custom-call | tf_op jit(solution)/shard_map/pallas_call | solution.py:411
  (73 shorter events, 15.8 us)
Async XLA Ops:
  0.6 17.5 %collective-permute-start.3 = (bf16[192,8192]{1,0:T(8,128)(2,1)}, bf16[192,8192]{1,0:T(8,128)(2,1)S(1)}, u32[]{:S(2)}, u32[]{:S(2)}) collective-permute-start(bf16[192,8192]{1,0:T(8,128)(2,1)} %x_hbm.1), channel_id=1, source_target_pairs={{0,1},{1,0},{2,3},{3,2},{4,5},{5,4},{6,7},{7,6},{8,9},{9,8},{10,11... | collective-permute-start | bytes 9437192 | tf_op jit(solution)/shard_map/ppermute | solution.py:234
  0.7 14.7 %collective-permute-start.2 = (bf16[16,128,128]{2,1,0:T(8,128)(2,1)}, bf16[16,128,128]{2,1,0:T(8,128)(2,1)}, u32[]{:S(2)}, u32[]{:S(2)}) collective-permute-start(bf16[16,128,128]{2,1,0:T(8,128)(2,1)} %refs_0_.1), channel_id=1, source_target_pairs={{0,2},{2,0},{1,3},{3,1},{4,6},{6,4},{5,7},{7,5},{8,10},{10,8},{9,1... | collective-permute-start | bytes 1572872 | tf_op jit(solution)/shard_map/ppermute | solution.py:234
  2.7 15.5 %collective-permute-start.1 = (bf16[16,128,128]{2,1,0:T(8,128)(2,1)}, bf16[16,128,128]{2,1,0:T(8,128)(2,1)}, u32[]{:S(2)}, u32[]{:S(2)}) collective-permute-start(bf16[16,128,128]{2,1,0:T(8,128)(2,1)} %refs_0_.1), channel_id=1, source_target_pairs={{0,12},{4,8},{8,4},{12,0},{1,13},{5,9},{9,5},{13,1},{2,14},{6,10},... | collective-permute-start | bytes 1572872 | tf_op jit(solution)/shard_map/ppermute | solution.py:234
  3.7 14.5 %collective-permute-start = (bf16[16,128,128]{2,1,0:T(8,128)(2,1)}, bf16[16,128,128]{2,1,0:T(8,128)(2,1)}, u32[]{:S(2)}, u32[]{:S(2)}) collective-permute-start(bf16[16,128,128]{2,1,0:T(8,128)(2,1)} %refs_0_.1), channel_id=1, source_target_pairs={{0,4},{4,0},{8,12},{12,8},{1,5},{5,1},{9,13},{13,9},{2,6},{6,2},{1... | collective-permute-start | bytes 1572872 | tf_op jit(solution)/shard_map/ppermute | solution.py:234
  3.9 14.3 %collective-permute-start.4 = (bf16[16,128,128]{2,1,0:T(8,128)(2,1)}, bf16[16,128,128]{2,1,0:T(8,128)(2,1)}, u32[]{:S(2)}, u32[]{:S(2)}) collective-permute-start(bf16[16,128,128]{2,1,0:T(8,128)(2,1)} %refs_0_.1), channel_id=1, source_target_pairs={{0,1},{1,0},{2,3},{3,2},{4,5},{5,4},{6,7},{7,6},{8,9},{9,8},{10,11... | collective-permute-start | bytes 1572872 | tf_op jit(solution)/shard_map/ppermute | solution.py:234
  18.2 15.2 %collective-permute-start.9 = (bf16[16,128,128]{2,1,0:T(8,128)(2,1)}, bf16[16,128,128]{2,1,0:T(8,128)(2,1)}, u32[]{:S(2)}, u32[]{:S(2)}) collective-permute-start(bf16[16,128,128]{2,1,0:T(8,128)(2,1)} %collective-permute-done.refs_1_.left), channel_id=1, source_target_pairs={{0,1},{1,0},{2,3},{3,2},{4,5},{5,4},{6,7},{7,6},{8,9},{9,8},{10,11... | collective-permute-start | bytes 1572872 | tf_op jit(solution)/shard_map/ppermute | solution.py:234
  18.3 15.1 %collective-permute-start.5 = (bf16[16,128,128]{2,1,0:T(8,128)(2,1)}, bf16[16,128,128]{2,1,0:T(8,128)(2,1)}, u32[]{:S(2)}, u32[]{:S(2)}) collective-permute-start(bf16[16,128,128]{2,1,0:T(8,128)(2,1)} %collective-permute-done.refs_1_.left), channel_id=1, source_target_pairs={{0,2},{2,0},{1,3},{3,1},{4,6},{6,4},{5,7},{7,5},{8,10},{10,8},{9,1... | collective-permute-start | bytes 1572872 | tf_op jit(solution)/shard_map/ppermute | solution.py:234
  19.7 14.6 %collective-permute-start.6 = (bf16[16,128,128]{2,1,0:T(8,128)(2,1)}, bf16[16,128,128]{2,1,0:T(8,128)(2,1)}, u32[]{:S(2)}, u32[]{:S(2)}) collective-permute-start(bf16[16,128,128]{2,1,0:T(8,128)(2,1)} %collective-permute-done.1.refs_2_.right), channel_id=1, source_target_pairs={{0,194},{2,64},{64,2},{66,128},{128,66},{130,192},{192,130},{194,0... | collective-permute-start | bytes 1572872 | tf_op jit(solution)/shard_map/ppermute | solution.py:238
  23.6 9.6 %collective-permute-start.7 = (bf16[8,128,128]{2,1,0:T(8,128)(2,1)}, bf16[8,128,128]{2,1,0:T(8,128)(2,1)S(1)}, u32[]{:S(2)}, u32[]{:S(2)}) collective-permute-start(bf16[8,128,128]{2,1,0:T(8,128)(2,1)} %get-tuple-element.73), channel_id=1, source_target_pairs={{0,12},{4,8},{8,4},{12,0},{1,13},{5,9},{9,5},{13,1},{2,14},{6,10},... | collective-permute-start | bytes 786440 | tf_op jit(solution)/shard_map/ppermute | solution.py:234
  25.3 8.1 %collective-permute-start.8 = (bf16[8,128,128]{2,1,0:T(8,128)(2,1)}, bf16[8,128,128]{2,1,0:T(8,128)(2,1)}, u32[]{:S(2)}, u32[]{:S(2)}) collective-permute-start(bf16[8,128,128]{2,1,0:T(8,128)(2,1)} %get-tuple-element.74), channel_id=1, source_target_pairs={{0,4},{4,0},{8,12},{12,8},{1,5},{5,1},{9,13},{13,9},{2,6},{6,2},{1... | collective-permute-start | bytes 786440 | tf_op jit(solution)/shard_map/ppermute | solution.py:234
  34.4 6.4 %collective-permute-start.12 = (bf16[16,128,128]{2,1,0:T(8,128)(2,1)}, bf16[16,128,128]{2,1,0:T(8,128)(2,1)S(1)}, u32[]{:S(2)}, u32[]{:S(2)}) collective-permute-start(bf16[16,128,128]{2,1,0:T(8,128)(2,1)} %collective-permute-done.1.refs_2_.right), channel_id=1, source_target_pairs={{0,1},{1,0},{2,3},{3,2},{4,5},{5,4},{6,7},{7,6},{8,9},{9,8},{10,11... | collective-permute-start | bytes 1572872 | tf_op jit(solution)/shard_map/ppermute | solution.py:234
  34.4 6.5 %collective-permute-start.13 = (bf16[16,128,128]{2,1,0:T(8,128)(2,1)}, bf16[16,128,128]{2,1,0:T(8,128)(2,1)S(1)}, u32[]{:S(2)}, u32[]{:S(2)}) collective-permute-start(bf16[16,128,128]{2,1,0:T(8,128)(2,1)} %collective-permute-done.2.refs_3_), channel_id=1, source_target_pairs={{0,1},{1,0},{2,3},{3,2},{4,5},{5,4},{6,7},{7,6},{8,9},{9,8},{10,11... | collective-permute-start | bytes 1572872 | tf_op jit(solution)/shard_map/ppermute | solution.py:234
  34.9 6.0 %collective-permute-start.14 = (bf16[16,128,128]{2,1,0:T(8,128)(2,1)}, bf16[16,128,128]{2,1,0:T(8,128)(2,1)S(1)}, u32[]{:S(2)}, u32[]{:S(2)}) collective-permute-start(bf16[16,128,128]{2,1,0:T(8,128)(2,1)} %collective-permute-done.5.refs_0_), channel_id=1, source_target_pairs={{0,1},{1,0},{2,3},{3,2},{4,5},{5,4},{6,7},{7,6},{8,9},{9,8},{10,11... | collective-permute-start | bytes 1572872 | tf_op jit(solution)/shard_map/ppermute | solution.py:234
  34.9 10.9 %collective-permute-start.10 = (bf16[8,128,128]{2,1,0:T(8,128)(2,1)S(1)}, bf16[8,128,128]{2,1,0:T(8,128)(2,1)S(1)}, u32[]{:S(2)}, u32[]{:S(2)}) collective-permute-start(bf16[8,128,128]{2,1,0:T(8,128)(2,1)S(1)} %collective-permute-done.7.refs_2_), channel_id=1, source_target_pairs={{0,2},{2,0},{1,3},{3,1},{4,6},{6,4},{5,7},{7,5},{8,10},{10,8},{9,1... | collective-permute-start | bytes 786440 | tf_op jit(solution)/shard_map/ppermute | solution.py:234
  38.8 8.6 %collective-permute-start.11 = (bf16[8,128,128]{2,1,0:T(8,128)(2,1)}, bf16[8,128,128]{2,1,0:T(8,128)(2,1)S(1)}, u32[]{:S(2)}, u32[]{:S(2)}) collective-permute-start(bf16[8,128,128]{2,1,0:T(8,128)(2,1)} %collective-permute-done.8.refs_3_), channel_id=1, source_target_pairs={{0,194},{2,64},{64,2},{66,128},{128,66},{130,192},{192,130},{194,0... | collective-permute-start | bytes 786440 | tf_op jit(solution)/shard_map/ppermute | solution.py:238
  40.8 7.1 %collective-permute-start.15 = (bf16[16,128,128]{2,1,0:T(8,128)(2,1)}, bf16[16,128,128]{2,1,0:T(8,128)(2,1)S(1)}, u32[]{:S(2)}, u32[]{:S(2)}) collective-permute-start(bf16[16,128,128]{2,1,0:T(8,128)(2,1)} %collective-permute-done.6.refs_1_), channel_id=1, source_target_pairs={{0,1},{1,0},{2,3},{3,2},{4,5},{5,4},{6,7},{7,6},{8,9},{9,8},{10,11... | collective-permute-start | bytes 1572872 | tf_op jit(solution)/shard_map/ppermute | solution.py:234
  47.4 2.7 %collective-permute-start.18 = (bf16[16,128,128]{2,1,0:T(8,128)(2,1)S(1)}, bf16[16,128,128]{2,1,0:T(8,128)(2,1)S(1)}, u32[]{:S(2)}, u32[]{:S(2)}) collective-permute-start(bf16[16,128,128]{2,1,0:T(8,128)(2,1)S(1)} %pad_maximum_fusion.2), channel_id=1, source_target_pairs={{0,1},{1,0},{2,3},{3,2},{4,5},{5,4},{6,7},{7,6},{8,9},{9,8},{10,11... | collective-permute-start | bytes 1572872 | tf_op jit(solution)/shard_map/ppermute | solution.py:234
  47.4 2.3 %collective-permute-start.16 = (bf16[8,128,128]{2,1,0:T(8,128)(2,1)S(1)}, bf16[8,128,128]{2,1,0:T(8,128)(2,1)S(1)}, u32[]{:S(2)}, u32[]{:S(2)}) collective-permute-start(bf16[8,128,128]{2,1,0:T(8,128)(2,1)S(1)} %collective-permute-done.10.refs_0_), channel_id=1, source_target_pairs={{0,1},{1,0},{2,3},{3,2},{4,5},{5,4},{6,7},{7,6},{8,9},{9,8},{10,11... | collective-permute-start | bytes 786440 | tf_op jit(solution)/shard_map/ppermute | solution.py:234
  47.9 2.1 %collective-permute-start.17 = (bf16[8,128,128]{2,1,0:T(8,128)(2,1)S(1)}, bf16[8,128,128]{2,1,0:T(8,128)(2,1)S(1)}, u32[]{:S(2)}, u32[]{:S(2)}) collective-permute-start(bf16[8,128,128]{2,1,0:T(8,128)(2,1)S(1)} %collective-permute-done.11.refs_1_), channel_id=1, source_target_pairs={{0,1},{1,0},{2,3},{3,2},{4,5},{5,4},{6,7},{7,6},{8,9},{9,8},{10,11... | collective-permute-start | bytes 786440 | tf_op jit(solution)/shard_map/ppermute | solution.py:234
  56.0 6.0 %copy-start = (s32[256]{0:T(256)S(1)}, s32[256]{0:T(256)}, u32[]{:S(2)}) copy-start(s32[256]{0:T(256)} %rows.3) | copy-start | bytes 3076
  56.0 6.0 %copy-start.1 = (s32[256]{0:T(256)S(1)}, s32[256]{0:T(256)}, u32[]{:S(2)}) copy-start(s32[256]{0:T(256)} %cols.3) | copy-start | bytes 3076
  56.0 6.0 %collective-permute-start.19 = (bf16[64,192,128]{2,1,0:T(8,128)(2,1)S(1)}, bf16[64,192,128]{2,1,0:T(8,128)(2,1)S(1)}, u32[]{:S(2)}, u32[]{:S(2)}) collective-permute-start(bf16[64,192,128]{2,1,0:T(8,128)(2,1)S(1)} %get-tuple-element.91.s_ref), channel_id=1, source_target_pairs={{0,1},{1,0},{2,3},{3,2},{4,5},{5,4},{6,7},{7,6},{8,9},{9,8},{10,11... | collective-permute-start | bytes 9437192 | tf_op jit(solution)/shard_map/ppermute | solution.py:234
  64.5 14.3 %collective-permute-start.20 = (bf16[16,128,128]{2,1,0:T(8,128)(2,1)S(1)}, bf16[16,128,128]{2,1,0:T(8,128)(2,1)S(1)}, u32[]{:S(2)}, u32[]{:S(2)}) collective-permute-start(bf16[16,128,128]{2,1,0:T(8,128)(2,1)S(1)} %get-tuple-element.92), channel_id=1, source_target_pairs={{0,4},{4,0},{8,12},{12,8},{1,5},{5,1},{9,13},{13,9},{2,6},{6,2},{1... | collective-permute-start | bytes 1572872 | tf_op jit(solution)/shard_map/ppermute | solution.py:234
  64.9 15.2 %collective-permute-start.21 = (bf16[16,128,128]{2,1,0:T(8,128)(2,1)S(1)}, bf16[16,128,128]{2,1,0:T(8,128)(2,1)S(1)}, u32[]{:S(2)}, u32[]{:S(2)}) collective-permute-start(bf16[16,128,128]{2,1,0:T(8,128)(2,1)S(1)} %get-tuple-element.93), channel_id=1, source_target_pairs={{0,12},{4,8},{8,4},{12,0},{1,13},{5,9},{9,5},{13,1},{2,14},{6,10},... | collective-permute-start | bytes 1572872 | tf_op jit(solution)/shard_map/ppermute | solution.py:234
  66.3 13.9 %collective-permute-start.22 = (bf16[16,128,128]{2,1,0:T(8,128)(2,1)S(1)}, bf16[16,128,128]{2,1,0:T(8,128)(2,1)S(1)}, u32[]{:S(2)}, u32[]{:S(2)}) collective-permute-start(bf16[16,128,128]{2,1,0:T(8,128)(2,1)S(1)} %get-tuple-element.94), channel_id=1, source_target_pairs={{0,16},{16,0},{32,48},{48,32},{1,17},{17,1},{33,49},{49,33},{2,18}... | collective-permute-start | bytes 1572872 | tf_op jit(solution)/shard_map/ppermute | solution.py:234
  67.8 14.8 %collective-permute-start.23 = (bf16[16,128,128]{2,1,0:T(8,128)(2,1)S(1)}, bf16[16,128,128]{2,1,0:T(8,128)(2,1)S(1)}, u32[]{:S(2)}, u32[]{:S(2)}) collective-permute-start(bf16[16,128,128]{2,1,0:T(8,128)(2,1)S(1)} %get-tuple-element.95), channel_id=1, source_target_pairs={{0,48},{16,32},{32,16},{48,0},{1,49},{17,33},{33,17},{49,1},{2,50}... | collective-permute-start | bytes 1572872 | tf_op jit(solution)/shard_map/ppermute | solution.py:234
  82.8 16.4 %collective-permute-start.30 = (bf16[8,128,128]{2,1,0:T(8,128)(2,1)S(1)}, bf16[8,128,128]{2,1,0:T(8,128)(2,1)S(1)}, u32[]{:S(2)}, u32[]{:S(2)}) collective-permute-start(bf16[8,128,128]{2,1,0:T(8,128)(2,1)S(1)} %add_convert_fusion), channel_id=1, source_target_pairs={{0,16},{16,0},{32,48},{48,32},{1,17},{17,1},{33,49},{49,33},{2,18}... | collective-permute-start | bytes 786440 | tf_op jit(solution)/shard_map/ppermute | solution.py:234
  82.9 7.2 %collective-permute-start.25 = (bf16[8,128,128]{2,1,0:T(8,128)(2,1)S(1)}, bf16[8,128,128]{2,1,0:T(8,128)(2,1)S(1)}, u32[]{:S(2)}, u32[]{:S(2)}) collective-permute-start(bf16[8,128,128]{2,1,0:T(8,128)(2,1)S(1)} %add_convert_fusion.2), channel_id=1, source_target_pairs={{0,4},{4,0},{8,12},{12,8},{1,5},{5,1},{9,13},{13,9},{2,6},{6,2},{1... | collective-permute-start | bytes 786440 | tf_op jit(solution)/shard_map/ppermute | solution.py:234
  84.1 15.1 %collective-permute-start.29 = (bf16[8,128,128]{2,1,0:T(8,128)(2,1)S(1)}, bf16[8,128,128]{2,1,0:T(8,128)(2,1)S(1)}, u32[]{:S(2)}, u32[]{:S(2)}) collective-permute-start(bf16[8,128,128]{2,1,0:T(8,128)(2,1)S(1)} %add_convert_fusion.1), channel_id=1, source_target_pairs={{0,48},{16,32},{32,16},{48,0},{1,49},{17,33},{33,17},{49,1},{2,50}... | collective-permute-start | bytes 786440 | tf_op jit(solution)/shard_map/ppermute | solution.py:234
  86.5 7.7 %collective-permute-start.24 = (bf16[8,128,128]{2,1,0:T(8,128)(2,1)S(1)}, bf16[8,128,128]{2,1,0:T(8,128)(2,1)S(1)}, u32[]{:S(2)}, u32[]{:S(2)}) collective-permute-start(bf16[8,128,128]{2,1,0:T(8,128)(2,1)S(1)} %add_convert_fusion.3), channel_id=1, source_target_pairs={{0,12},{4,8},{8,4},{12,0},{1,13},{5,9},{9,5},{13,1},{2,14},{6,10},... | collective-permute-start | bytes 786440 | tf_op jit(solution)/shard_map/ppermute | solution.py:234
  94.4 5.1 %collective-permute-start.26 = (bf16[4,128,128]{2,1,0:T(8,128)(2,1)S(1)}, bf16[4,128,128]{2,1,0:T(8,128)(2,1)S(1)}, u32[]{:S(2)}, u32[]{:S(2)}) collective-permute-start(bf16[4,128,128]{2,1,0:T(8,128)(2,1)S(1)} %get-tuple-element.133), channel_id=1, source_target_pairs={{0,16},{16,0},{32,48},{48,32},{1,17},{17,1},{33,49},{49,33},{2,18}... | collective-permute-start | bytes 393224 | tf_op jit(solution)/shard_map/ppermute | solution.py:234
  95.8 6.5 %collective-permute-start.28 = (bf16[4,128,128]{2,1,0:T(8,128)(2,1)S(1)}, bf16[4,128,128]{2,1,0:T(8,128)(2,1)S(1)}, u32[]{:S(2)}, u32[]{:S(2)}) collective-permute-start(bf16[4,128,128]{2,1,0:T(8,128)(2,1)S(1)} %get-tuple-element.134), channel_id=1, source_target_pairs={{0,32},{16,48},{32,0},{48,16},{1,33},{17,49},{33,1},{49,17},{2,34}... | collective-permute-start | bytes 393224 | tf_op jit(solution)/shard_map/ppermute | solution.py:234
  97.0 6.8 %collective-permute-start.27 = (bf16[4,128,128]{2,1,0:T(8,128)(2,1)S(1)}, bf16[4,128,128]{2,1,0:T(8,128)(2,1)S(1)}, u32[]{:S(2)}, u32[]{:S(2)}) collective-permute-start(bf16[4,128,128]{2,1,0:T(8,128)(2,1)S(1)} %get-tuple-element.135), channel_id=1, source_target_pairs={{0,48},{16,32},{32,16},{48,0},{1,49},{17,33},{33,17},{49,1},{2,50}... | collective-permute-start | bytes 393224 | tf_op jit(solution)/shard_map/ppermute | solution.py:234
  103.8 11.1 %collective-permute-start.34 = (f32[4,128,128]{2,1,0:T(8,128)S(1)}, f32[4,128,128]{2,1,0:T(8,128)S(1)}, u32[]{:S(2)}, u32[]{:S(2)}) collective-permute-start(f32[4,128,128]{2,1,0:T(8,128)S(1)} %fusion.4), channel_id=1, source_target_pairs={{0,2},{2,0},{1,3},{3,1},{4,6},{6,4},{5,7},{7,5},{8,10},{10,8},{9,1... | collective-permute-start | bytes 786440 | tf_op jit(solution)/shard_map/ppermute | solution.py:234
  105.5 5.1 %collective-permute-start.31 = (bf16[4,128,128]{2,1,0:T(8,128)(2,1)S(1)}, bf16[4,128,128]{2,1,0:T(8,128)(2,1)S(1)}, u32[]{:S(2)}, u32[]{:S(2)}) collective-permute-start(bf16[4,128,128]{2,1,0:T(8,128)(2,1)S(1)} %get-tuple-element.130), channel_id=1, source_target_pairs={{0,4},{4,0},{8,12},{12,8},{1,5},{5,1},{9,13},{13,9},{2,6},{6,2},{1... | collective-permute-start | bytes 393224 | tf_op jit(solution)/shard_map/ppermute | solution.py:234
  105.6 7.4 %collective-permute-start.33 = (bf16[4,128,128]{2,1,0:T(8,128)(2,1)S(1)}, bf16[4,128,128]{2,1,0:T(8,128)(2,1)S(1)}, u32[]{:S(2)}, u32[]{:S(2)}) collective-permute-start(bf16[4,128,128]{2,1,0:T(8,128)(2,1)S(1)} %get-tuple-element.131), channel_id=1, source_target_pairs={{0,8},{4,12},{8,0},{12,4},{1,9},{5,13},{9,1},{13,5},{2,10},{6,14},... | collective-permute-start | bytes 393224 | tf_op jit(solution)/shard_map/ppermute | solution.py:234
  108.7 6.2 %collective-permute-start.32 = (bf16[4,128,128]{2,1,0:T(8,128)(2,1)S(1)}, bf16[4,128,128]{2,1,0:T(8,128)(2,1)S(1)}, u32[]{:S(2)}, u32[]{:S(2)}) collective-permute-start(bf16[4,128,128]{2,1,0:T(8,128)(2,1)S(1)} %get-tuple-element.132), channel_id=1, source_target_pairs={{0,12},{4,8},{8,4},{12,0},{1,13},{5,9},{9,5},{13,1},{2,14},{6,10},... | collective-permute-start | bytes 393224 | tf_op jit(solution)/shard_map/ppermute | solution.py:234
  115.0 10.8 %collective-permute-start.37 = (bf16[4,128,128]{2,1,0:T(8,128)(2,1)S(1)}, bf16[4,128,128]{2,1,0:T(8,128)(2,1)S(1)}, u32[]{:S(2)}, u32[]{:S(2)}) collective-permute-start(bf16[4,128,128]{2,1,0:T(8,128)(2,1)S(1)} %fusion.7.a), channel_id=1, source_target_pairs={{0,192},{64,128},{128,64},{192,0},{1,193},{65,129},{129,65},{193,1... | collective-permute-start | bytes 393224 | tf_op jit(solution)/shard_map/ppermute | solution.py:234
  118.0 9.0 %collective-permute-start.36 = (bf16[4,128,128]{2,1,0:T(8,128)(2,1)S(1)}, bf16[4,128,128]{2,1,0:T(8,128)(2,1)S(1)}, u32[]{:S(2)}, u32[]{:S(2)}) collective-permute-start(bf16[4,128,128]{2,1,0:T(8,128)(2,1)S(1)} %fusion.7.a), channel_id=1, source_target_pairs={{0,128},{64,192},{128,0},{192,64},{1,129},{65,193},{129,1},{193,65... | collective-permute-start | bytes 393224 | tf_op jit(solution)/shard_map/ppermute | solution.py:234
  119.6 8.4 %collective-permute-start.35 = (bf16[4,128,128]{2,1,0:T(8,128)(2,1)S(1)}, bf16[4,128,128]{2,1,0:T(8,128)(2,1)S(1)}, u32[]{:S(2)}, u32[]{:S(2)}) collective-permute-start(bf16[4,128,128]{2,1,0:T(8,128)(2,1)S(1)} %fusion.7.a), channel_id=1, source_target_pairs={{0,64},{64,0},{128,192},{192,128},{1,65},{65,1},{129,193},{193,129... | collective-permute-start | bytes 393224 | tf_op jit(solution)/shard_map/ppermute | solution.py:234
  128.3 6.3 %collective-permute-start.40 = (bf16[4,128,128]{2,1,0:T(8,128)(2,1)S(1)}, bf16[4,128,128]{2,1,0:T(8,128)(2,1)S(1)}, u32[]{:S(2)}, u32[]{:S(2)}) collective-permute-start(bf16[4,128,128]{2,1,0:T(8,128)(2,1)S(1)} %shard_map.77.refs_0_), channel_id=1, source_target_pairs={{0,48},{16,32},{32,16},{48,0},{1,49},{17,33},{33,17},{49,1},{2,50}... | collective-permute-start | bytes 393224 | tf_op jit(solution)/shard_map/ppermute | solution.py:234
  130.2 6.5 %collective-permute-start.39 = (bf16[4,128,128]{2,1,0:T(8,128)(2,1)S(1)}, bf16[4,128,128]{2,1,0:T(8,128)(2,1)S(1)}, u32[]{:S(2)}, u32[]{:S(2)}) collective-permute-start(bf16[4,128,128]{2,1,0:T(8,128)(2,1)S(1)} %shard_map.77.refs_0_), channel_id=1, source_target_pairs={{0,32},{16,48},{32,0},{48,16},{1,33},{17,49},{33,1},{49,17},{2,34}... | collective-permute-start | bytes 393224 | tf_op jit(solution)/shard_map/ppermute | solution.py:234
  130.8 6.0 %collective-permute-start.38 = (bf16[4,128,128]{2,1,0:T(8,128)(2,1)S(1)}, bf16[4,128,128]{2,1,0:T(8,128)(2,1)S(1)}, u32[]{:S(2)}, u32[]{:S(2)}) collective-permute-start(bf16[4,128,128]{2,1,0:T(8,128)(2,1)S(1)} %shard_map.77.refs_0_), channel_id=1, source_target_pairs={{0,16},{16,0},{32,48},{48,32},{1,17},{17,1},{33,49},{49,33},{2,18}... | collective-permute-start | bytes 393224 | tf_op jit(solution)/shard_map/ppermute | solution.py:234

commit v6 on v5

--- a/solution.py
+++ b/solution.py
@@ -399,7 +399,8 @@
         in_specs=[SMEM] * 2 + [VMEM] * 3 + [ANY],
         input_output_aliases={5: 0},
     )(place, blocks, near(grad_near), near(whole), near(slopes), grad_features)
-    across = [swap(mine, "zh", r) for r in (1, 2, 3)]
+    across = {r: swap(mine, "zh", r) for r in (1, 3, 2)}
+    across = [across[r] for r in (1, 2, 3)]
     across, grad_features = lax.optimization_barrier((across, grad_features))
     group = pl.pallas_call(
         normalize_kernel,
@@ -408,13 +409,14 @@
         out_specs=VMEM,
         compiler_params=PARAMS,
     )(mine, *across)
+    spread = {r: swap(group, "y", r) for r in (1, 3, 2)}
     tile_update = pl.pallas_call(
         finish_kernel,
         out_shape=shape((16, SIDE, SIDE), f32),
         in_specs=[SMEM] + [VMEM] * 4,
         out_specs=VMEM,
         compiler_params=PARAMS,
-    )(where, group, *(swap(group, "y", r) for r in (1, 2, 3)))
+    )(where, group, *(spread[r] for r in (1, 2, 3)))
     return grad_features, tile_update
 
 

time: 140 us -> 140 us (level)
  no operation moved by 1% of the time
where the time goes in v6:
time: 140 us; the launch traced here: 138 us
  waiting for transfers between devices  47.8 us (34%)
  starting transfers between devices  47.5 us (34%)
  Pallas kernels  35 us (25%)
  other arithmetic  5.08 us (4%)
  between operations  2.91 us (2%)
    ppermute x39, waiting for transfers between devices, swap(): return lax.ppermute(value, axis, [(i, i ^ mask) for i in range(size)])  45.2 us
    ppermute x39, starting transfers between devices, swap(): return lax.ppermute(value, axis, [(i, i ^ mask) for i in range(size)])  44.4 us
    pallas_call x1, Pallas kernels, on_device(): pl.pallas_call(forward_kernel, out_shape=[pltpu.VMEM((64, rows_here, SIDE...  5.86 us
    pallas_call x1, Pallas kernels, on_device(): pl.pallas_call(transpose_kernel, out_shape=pltpu.VMEM((64, SIDE, 2 * rows...  5.76 us
    pallas_call x1, Pallas kernels, on_device(): pl.pallas_call(load_kernel, out_shape=[pltpu.VMEM(features.shape, bf16),...  4.24 us
    pallas_call x1, Pallas kernels, on_device(): backward(functools.partial(backward_kernel, 1), in_specs=[SMEM] * 2 + [VM...  4.2 us
    pallas_call x1, Pallas kernels, on_device(): backward(functools.partial(backward_kernel, 0), in_specs=[SMEM] * 2 + [VM...  4.2 us
    ppermute x2, starting transfers between devices, cross(): lax.ppermute(value, Z, [(z, (z + 1) % 8 if z % 2 else (z - 1) % 8) for z...  3.07 us
  transfers between devices with their start and end apart: 41, of which 25 were waited for; matrix products, arithmetic and copies ran while one was open for 4% of the time, Pallas kernels for 18%

profile of v6, /device:TPU:32, one launch (start us, length us, event | category | flops | bytes accessed | tf_op | source)
XLA Modules:
  0.0 138.4 jit_solution(5179063260029585848)
XLA Ops:
  0.7 1.9 %collective-permute-start.2 = (bf16[16,128,128]{2,1,0:T(8,128)(2,1)}, bf16[16,128,128]{2,1,0:T(8,128)(2,1)}, u32[]{:S(2)}, u32[]{:S(2)}) collective-permute-start(bf16[16,128,128]{2,1,0:T(8,128)(2,1)} %refs_0_.1), channel_id=1, source_target_pairs={{0,2},{2,0},{1,3},{3,1},{4,6},{6,4},{5,7},{7,5},{8,10},{10,8},{9,1... | collective-permute-start | bytes 1572872 | tf_op jit(solution)/shard_map/ppermute | solution.py:234
  3.9 1.3 fusion.10
  8.9 6.6 %collective-permute-done.2.refs_3_ = bf16[16,128,128]{2,1,0:T(8,128)(2,1)} collective-permute-done((bf16[16,128,128]{2,1,0:T(8,128)(2,1)}, bf16[16,128,128]{2,1,0:T(8,128)(2,1)}, u32[]{:S(2)}, u32[]{:S(2)}) %collective-permute-start.2) | collective-permute-done | bytes 524320 | tf_op jit(solution)/shard_map/ppermute | solution.py:234
  15.5 2.7 %collective-permute-done.1.refs_2_.right = bf16[16,128,128]{2,1,0:T(8,128)(2,1)} collective-permute-done((bf16[16,128,128]{2,1,0:T(8,128)(2,1)}, bf16[16,128,128]{2,1,0:T(8,128)(2,1)}, u32[]{:S(2)}, u32[]{:S(2)}) %collective-permute-start.1) | collective-permute-done | bytes 524320 | tf_op jit(solution)/shard_map/ppermute | solution.py:234
  18.3 1.4 %collective-permute-start.5 = (bf16[16,128,128]{2,1,0:T(8,128)(2,1)}, bf16[16,128,128]{2,1,0:T(8,128)(2,1)}, u32[]{:S(2)}, u32[]{:S(2)}) collective-permute-start(bf16[16,128,128]{2,1,0:T(8,128)(2,1)} %collective-permute-done.refs_1_.left), channel_id=1, source_target_pairs={{0,2},{2,0},{1,3},{3,1},{4,6},{6,4},{5,7},{7,5},{8,10},{10,8},{9,1... | collective-permute-start | bytes 1572872 | tf_op jit(solution)/shard_map/ppermute | solution.py:234
  19.7 2.1 %collective-permute-start.6 = (bf16[16,128,128]{2,1,0:T(8,128)(2,1)}, bf16[16,128,128]{2,1,0:T(8,128)(2,1)}, u32[]{:S(2)}, u32[]{:S(2)}) collective-permute-start(bf16[16,128,128]{2,1,0:T(8,128)(2,1)} %collective-permute-done.1.refs_2_.right), channel_id=1, source_target_pairs={{0,194},{2,64},{64,2},{66,128},{128,66},{130,192},{192,130},{194,0... | collective-permute-start | bytes 1572872 | tf_op jit(solution)/shard_map/ppermute | solution.py:238
  21.8 1.8 %shard_map.69 = (bf16[8,128,128]{2,1,0:T(8,128)(2,1)}, bf16[8,128,128]{2,1,0:T(8,128)(2,1)}) custom-call(bf16[16,128,128]{2,1,0:T(8,128)(2,1)} %collective-permute-done.refs_1_.left, bf16[16,128,128]{2,1,0:T(8,128)(2,1)} %collective-permute-done.1.refs_2_.right), custom_call_target="tpu_custom_call" | custom-call | tf_op jit(solution)/shard_map/pallas_call | solution.py:291
  23.6 1.7 %collective-permute-start.7 = (bf16[8,128,128]{2,1,0:T(8,128)(2,1)}, bf16[8,128,128]{2,1,0:T(8,128)(2,1)S(1)}, u32[]{:S(2)}, u32[]{:S(2)}) collective-permute-start(bf16[8,128,128]{2,1,0:T(8,128)(2,1)} %get-tuple-element.73), channel_id=1, source_target_pairs={{0,12},{4,8},{8,4},{12,0},{1,13},{5,9},{9,5},{13,1},{2,14},{6,10},... | collective-permute-start | bytes 786440 | tf_op jit(solution)/shard_map/ppermute | solution.py:234
  25.4 4.2 %shard_map.68 = (bf16[192,8192]{1,0:T(8,128)(2,1)S(1)}, bf16[192,8192]{1,0:T(8,128)(2,1)S(1)}, bf16[256,128,128]{2,1,0:T(8,128)(2,1)S(1)}) custom-call(s32[4]{0:T(128)S(1)} %pad_add_fusion.1.where, bf16[192,8192]{1,0:T(8,128)(2,1)} %x_hbm.1, bf16[192,8192]{1,0:T(8,128)(2,1)} %g_hbm.1, bf16[16,128,128]{2,1,0:T(8,128)(2,1)} %refs_0_.1, ...), custom_call_target="tpu_custom_call" | custom-call | tf_op jit(solution)/shard_map/pallas_call | solution.py:275
  29.6 3.6 %collective-permute-done.7.refs_2_ = bf16[8,128,128]{2,1,0:T(8,128)(2,1)S(1)} collective-permute-done((bf16[8,128,128]{2,1,0:T(8,128)(2,1)}, bf16[8,128,128]{2,1,0:T(8,128)(2,1)S(1)}, u32[]{:S(2)}, u32[]{:S(2)}) %collective-permute-start.7) | collective-permute-done | bytes 262176 | tf_op jit(solution)/shard_map/ppermute | solution.py:234
  34.9 3.9 %collective-permute-start.10 = (bf16[8,128,128]{2,1,0:T(8,128)(2,1)S(1)}, bf16[8,128,128]{2,1,0:T(8,128)(2,1)S(1)}, u32[]{:S(2)}, u32[]{:S(2)}) collective-permute-start(bf16[8,128,128]{2,1,0:T(8,128)(2,1)S(1)} %collective-permute-done.7.refs_2_), channel_id=1, source_target_pairs={{0,2},{2,0},{1,3},{3,1},{4,6},{6,4},{5,7},{7,5},{8,10},{10,8},{9,1... | collective-permute-start | bytes 786440 | tf_op jit(solution)/shard_map/ppermute | solution.py:234
  40.9 2.1 %shard_map.70.given = bf16[256,128,128]{2,1,0:T(8,128)(2,1)S(1)} custom-call(s32[4]{0:T(128)S(1)} %pad_add_fusion.1.where, bf16[256,128,128]{2,1,0:T(8,128)(2,1)S(1)} %get-tuple-element.78.given, bf16[16,128,128]{2,1,0:T(8,128)(2,1)} %collective-permute-done.5.refs_0_, ...), custom_call_target="tpu_custom_call", output_to_operand_aliasing={{}: (1, {})} | custom-call | tf_op jit(solution)/shard_map/pallas_call | solution.py:308
  43.0 2.7 %collective-permute-done.10.refs_0_ = bf16[8,128,128]{2,1,0:T(8,128)(2,1)S(1)} collective-permute-done((bf16[8,128,128]{2,1,0:T(8,128)(2,1)S(1)}, bf16[8,128,128]{2,1,0:T(8,128)(2,1)S(1)}, u32[]{:S(2)}, u32[]{:S(2)}) %collective-permute-start.10) | collective-permute-done | bytes 262176 | tf_op jit(solution)/shard_map/ppermute | solution.py:234
  45.7 1.7 %collective-permute-done.11.refs_1_ = bf16[8,128,128]{2,1,0:T(8,128)(2,1)S(1)} collective-permute-done((bf16[8,128,128]{2,1,0:T(8,128)(2,1)}, bf16[8,128,128]{2,1,0:T(8,128)(2,1)S(1)}, u32[]{:S(2)}, u32[]{:S(2)}) %collective-permute-start.11) | collective-permute-done | bytes 262176 | tf_op jit(solution)/shard_map/ppermute | solution.py:238
  47.9 1.8 %collective-permute-done.16.refs_3_ = bf16[8,128,128]{2,1,0:T(8,128)(2,1)S(1)} collective-permute-done((bf16[8,128,128]{2,1,0:T(8,128)(2,1)S(1)}, bf16[8,128,128]{2,1,0:T(8,128)(2,1)S(1)}, u32[]{:S(2)}, u32[]{:S(2)}) %collective-permute-start.16) | collective-permute-done | bytes 262176 | tf_op jit(solution)/shard_map/ppermute | solution.py:234
  50.1 5.9 %shard_map.71 = (bf16[64,192,128]{2,1,0:T(8,128)(2,1)S(1)}, bf16[256,128,128]{2,1,0:T(8,128)(2,1)S(1)}) custom-call(s32[4]{0:T(128)S(1)} %pad_add_fusion.1.where, s32[256]{0:T(256)S(1)} %select_reduce_fusion.place, s32[64]{0:T(128)S(1)} %xor.28.blocks, bf16[192,8192]{1,0:T(8,128)(2,1)S(1)} %get-tuple-element.70.x_ref.mine_ref, ...), custom_call_target="tpu_custom_call", output_to_operand_aliasing={{1}: (5, {})} | custom-call | tf_op jit(solution)/shard_map/pallas_call | solution.py:320
  56.2 5.8 %shard_map.72.xt_ref = bf16[64,128,384]{2,1,0:T(8,128)(2,1)S(1)} custom-call(bf16[192,8192]{1,0:T(8,128)(2,1)S(1)} %get-tuple-element.70.x_ref.mine_ref, bf16[192,8192]{1,0:T(8,128)(2,1)S(1)} %collective-permute-done.3.other_ref), custom_call_target="tpu_custom_call" | custom-call | tf_op jit(solution)/shard_map/pallas_call | solution.py:334
  62.0 2.5 %shard_map.73 = (bf16[16,128,128]{2,1,0:T(8,128)(2,1)S(1)}, bf16[16,128,128]{2,1,0:T(8,128)(2,1)S(1)}, bf16[16,128,128]{2,1,0:T(8,128)(2,1)S(1)}, bf16[16,128,128]{2,1,0:T(8,128)(2,1)S(1)}) custom-call(s32[256]{0:T(256)S(1)} %copy-done, s32[256]{0:T(256)S(1)} %copy-done.1, s32[4]{0:T(128)S(1)} %pad_add_fusion.1.where, ...), custom_call_target="tpu_custom_call" | custom-call | tf_op jit(solution)/shard_map/pallas_call | solution.py:342
  64.9 1.4 collective-permute-start.21
  66.2 1.6 %collective-permute-start.22 = (bf16[16,128,128]{2,1,0:T(8,128)(2,1)S(1)}, bf16[16,128,128]{2,1,0:T(8,128)(2,1)S(1)}, u32[]{:S(2)}, u32[]{:S(2)}) collective-permute-start(bf16[16,128,128]{2,1,0:T(8,128)(2,1)S(1)} %get-tuple-element.94), channel_id=1, source_target_pairs={{0,16},{16,0},{32,48},{48,32},{1,17},{17,1},{33,49},{49,33},{2,18}... | collective-permute-start | bytes 1572872 | tf_op jit(solution)/shard_map/ppermute | solution.py:234
  67.8 2.2 %collective-permute-start.23 = (bf16[16,128,128]{2,1,0:T(8,128)(2,1)S(1)}, bf16[16,128,128]{2,1,0:T(8,128)(2,1)S(1)}, u32[]{:S(2)}, u32[]{:S(2)}) collective-permute-start(bf16[16,128,128]{2,1,0:T(8,128)(2,1)S(1)} %get-tuple-element.95), channel_id=1, source_target_pairs={{0,48},{16,32},{32,16},{48,0},{1,49},{17,33},{33,17},{49,1},{2,50}... | collective-permute-start | bytes 1572872 | tf_op jit(solution)/shard_map/ppermute | solution.py:234
  70.0 2.4 %shard_map.74 = (f32[8,128,128]{2,1,0:T(8,128)S(1)}, f32[8,128,128]{2,1,0:T(8,128)S(1)}, f32[8,128,128]{2,1,0:T(8,128)S(1)}, f32[8,128,128]{2,1,0:T(8,128)S(1)},...) custom-call(s32[256]{0:T(256)S(1)} %copy-done, ...), custom_call_target="tpu_custom_call" | custom-call | tf_op jit(solution)/shard_map/pallas_call | solution.py:352
  72.4 4.2 %shard_map.75.refs_0_ = bf16[192,8192]{1,0:T(8,128)(2,1)} custom-call(s32[256]{0:T(256)S(1)} %select_reduce_fusion.place, s32[64]{0:T(128)S(1)} %xor.28.blocks, bf16[192,8192]{1,0:T(8,128)(2,1)S(1)} %get-tuple-element.72.g_ref, bf16[256,128,128]{2,1,0:T(8,128)(2,1)S(1)} %get-tuple-element.106.w_ref, bf16[64,192,128]{2,1,0:T(8,128)(2,1)S(1)} %get-tuple-element.91.s_ref), custom_call_target="tpu_custom_call" | custom-call | tf_op jit(solution)/shard_map/pallas_call | solution.py:371
  76.6 2.1 %collective-permute-done.20 = bf16[16,128,128]{2,1,0:T(8,128)(2,1)S(1)} collective-permute-done((bf16[16,128,128]{2,1,0:T(8,128)(2,1)S(1)}, bf16[16,128,128]{2,1,0:T(8,128)(2,1)S(1)}, u32[]{:S(2)}, u32[]{:S(2)}) %collective-permute-start.20) | collective-permute-done | bytes 524320 | tf_op jit(solution)/shard_map/ppermute | solution.py:234
  78.7 1.3 collective-permute-done.21
  80.2 2.5 %collective-permute-done.23 = bf16[16,128,128]{2,1,0:T(8,128)(2,1)S(1)} collective-permute-done((bf16[16,128,128]{2,1,0:T(8,128)(2,1)S(1)}, bf16[16,128,128]{2,1,0:T(8,128)(2,1)S(1)}, u32[]{:S(2)}, u32[]{:S(2)}) %collective-permute-start.23) | collective-permute-done | bytes 524320 | tf_op jit(solution)/shard_map/ppermute | solution.py:234
  84.1 2.3 %collective-permute-start.29 = (bf16[8,128,128]{2,1,0:T(8,128)(2,1)S(1)}, bf16[8,128,128]{2,1,0:T(8,128)(2,1)S(1)}, u32[]{:S(2)}, u32[]{:S(2)}) collective-permute-start(bf16[8,128,128]{2,1,0:T(8,128)(2,1)S(1)} %add_convert_fusion.1), channel_id=1, source_target_pairs={{0,48},{16,32},{32,16},{48,0},{1,49},{17,33},{33,17},{49,1},{2,50}... | collective-permute-start | bytes 786440 | tf_op jit(solution)/shard_map/ppermute | solution.py:234
  86.5 1.7 %collective-permute-start.24 = (bf16[8,128,128]{2,1,0:T(8,128)(2,1)S(1)}, bf16[8,128,128]{2,1,0:T(8,128)(2,1)S(1)}, u32[]{:S(2)}, u32[]{:S(2)}) collective-permute-start(bf16[8,128,128]{2,1,0:T(8,128)(2,1)S(1)} %add_convert_fusion.3), channel_id=1, source_target_pairs={{0,12},{4,8},{8,4},{12,0},{1,13},{5,9},{9,5},{13,1},{2,14},{6,10},... | collective-permute-start | bytes 786440 | tf_op jit(solution)/shard_map/ppermute | solution.py:234
  88.3 1.9 %collective-permute-done.25 = bf16[8,128,128]{2,1,0:T(8,128)(2,1)S(1)} collective-permute-done((bf16[8,128,128]{2,1,0:T(8,128)(2,1)S(1)}, bf16[8,128,128]{2,1,0:T(8,128)(2,1)S(1)}, u32[]{:S(2)}, u32[]{:S(2)}) %collective-permute-start.25) | collective-permute-done | bytes 262176 | tf_op jit(solution)/shard_map/ppermute | solution.py:234
  90.2 4.0 %collective-permute-done.24 = bf16[8,128,128]{2,1,0:T(8,128)(2,1)S(1)} collective-permute-done((bf16[8,128,128]{2,1,0:T(8,128)(2,1)S(1)}, bf16[8,128,128]{2,1,0:T(8,128)(2,1)S(1)}, u32[]{:S(2)}, u32[]{:S(2)}) %collective-permute-start.24) | collective-permute-done | bytes 262176 | tf_op jit(solution)/shard_map/ppermute | solution.py:234
  94.4 1.4 %collective-permute-start.26 = (bf16[4,128,128]{2,1,0:T(8,128)(2,1)S(1)}, bf16[4,128,128]{2,1,0:T(8,128)(2,1)S(1)}, u32[]{:S(2)}, u32[]{:S(2)}) collective-permute-start(bf16[4,128,128]{2,1,0:T(8,128)(2,1)S(1)} %get-tuple-element.133), channel_id=1, source_target_pairs={{0,16},{16,0},{32,48},{48,32},{1,17},{17,1},{33,49},{49,33},{2,18}... | collective-permute-start | bytes 393224 | tf_op jit(solution)/shard_map/ppermute | solution.py:234
  96.9 2.2 %collective-permute-start.27 = (bf16[4,128,128]{2,1,0:T(8,128)(2,1)S(1)}, bf16[4,128,128]{2,1,0:T(8,128)(2,1)S(1)}, u32[]{:S(2)}, u32[]{:S(2)}) collective-permute-start(bf16[4,128,128]{2,1,0:T(8,128)(2,1)S(1)} %get-tuple-element.135), channel_id=1, source_target_pairs={{0,48},{16,32},{32,16},{48,0},{1,49},{17,33},{33,17},{49,1},{2,50}... | collective-permute-start | bytes 393224 | tf_op jit(solution)/shard_map/ppermute | solution.py:234
  99.5 2.9 %collective-permute-done.28 = bf16[4,128,128]{2,1,0:T(8,128)(2,1)S(1)} collective-permute-done((bf16[4,128,128]{2,1,0:T(8,128)(2,1)S(1)}, bf16[4,128,128]{2,1,0:T(8,128)(2,1)S(1)}, u32[]{:S(2)}, u32[]{:S(2)}) %collective-permute-start.28) | collective-permute-done | bytes 131104 | tf_op jit(solution)/shard_map/ppermute | solution.py:234
  102.4 1.3 collective-permute-done.27
  103.8 1.6 %collective-permute-start.34 = (f32[4,128,128]{2,1,0:T(8,128)S(1)}, f32[4,128,128]{2,1,0:T(8,128)S(1)}, u32[]{:S(2)}, u32[]{:S(2)}) collective-permute-start(f32[4,128,128]{2,1,0:T(8,128)S(1)} %fusion.4), channel_id=1, source_target_pairs={{0,2},{2,0},{1,3},{3,1},{4,6},{6,4},{5,7},{7,5},{8,10},{10,8},{9,1... | collective-permute-start | bytes 786440 | tf_op jit(solution)/shard_map/ppermute | solution.py:234
  105.6 3.1 %collective-permute-start.33 = (bf16[4,128,128]{2,1,0:T(8,128)(2,1)S(1)}, bf16[4,128,128]{2,1,0:T(8,128)(2,1)S(1)}, u32[]{:S(2)}, u32[]{:S(2)}) collective-permute-start(bf16[4,128,128]{2,1,0:T(8,128)(2,1)S(1)} %get-tuple-element.131), channel_id=1, source_target_pairs={{0,8},{4,12},{8,0},{12,4},{1,9},{5,13},{9,1},{13,5},{2,10},{6,14},... | collective-permute-start | bytes 393224 | tf_op jit(solution)/shard_map/ppermute | solution.py:234
  108.7 1.6 %collective-permute-start.32 = (bf16[4,128,128]{2,1,0:T(8,128)(2,1)S(1)}, bf16[4,128,128]{2,1,0:T(8,128)(2,1)S(1)}, u32[]{:S(2)}, u32[]{:S(2)}) collective-permute-start(bf16[4,128,128]{2,1,0:T(8,128)(2,1)S(1)} %get-tuple-element.132), channel_id=1, source_target_pairs={{0,12},{4,8},{8,4},{12,0},{1,13},{5,9},{9,5},{13,1},{2,14},{6,10},... | collective-permute-start | bytes 393224 | tf_op jit(solution)/shard_map/ppermute | solution.py:234
  110.5 2.5 %collective-permute-done.33 = bf16[4,128,128]{2,1,0:T(8,128)(2,1)S(1)} collective-permute-done((bf16[4,128,128]{2,1,0:T(8,128)(2,1)S(1)}, bf16[4,128,128]{2,1,0:T(8,128)(2,1)S(1)}, u32[]{:S(2)}, u32[]{:S(2)}) %collective-permute-start.33) | collective-permute-done | bytes 131104 | tf_op jit(solution)/shard_map/ppermute | solution.py:234
  113.0 1.8 %collective-permute-done.32 = bf16[4,128,128]{2,1,0:T(8,128)(2,1)S(1)} collective-permute-done((bf16[4,128,128]{2,1,0:T(8,128)(2,1)S(1)}, bf16[4,128,128]{2,1,0:T(8,128)(2,1)S(1)}, u32[]{:S(2)}, u32[]{:S(2)}) %collective-permute-start.32) | collective-permute-done | bytes 131104 | tf_op jit(solution)/shard_map/ppermute | solution.py:234
  115.0 3.0 %collective-permute-start.37 = (bf16[4,128,128]{2,1,0:T(8,128)(2,1)S(1)}, bf16[4,128,128]{2,1,0:T(8,128)(2,1)S(1)}, u32[]{:S(2)}, u32[]{:S(2)}) collective-permute-start(bf16[4,128,128]{2,1,0:T(8,128)(2,1)S(1)} %fusion.7.a), channel_id=1, source_target_pairs={{0,192},{64,128},{128,64},{192,0},{1,193},{65,129},{129,65},{193,1... | collective-permute-start | bytes 393224 | tf_op jit(solution)/shard_map/ppermute | solution.py:234
  118.0 1.6 %collective-permute-start.36 = (bf16[4,128,128]{2,1,0:T(8,128)(2,1)S(1)}, bf16[4,128,128]{2,1,0:T(8,128)(2,1)S(1)}, u32[]{:S(2)}, u32[]{:S(2)}) collective-permute-start(bf16[4,128,128]{2,1,0:T(8,128)(2,1)S(1)} %fusion.7.a), channel_id=1, source_target_pairs={{0,128},{64,192},{128,0},{192,64},{1,129},{65,193},{129,1},{193,65... | collective-permute-start | bytes 393224 | tf_op jit(solution)/shard_map/ppermute | solution.py:234
  119.6 2.0 %collective-permute-start.35 = (bf16[4,128,128]{2,1,0:T(8,128)(2,1)S(1)}, bf16[4,128,128]{2,1,0:T(8,128)(2,1)S(1)}, u32[]{:S(2)}, u32[]{:S(2)}) collective-permute-start(bf16[4,128,128]{2,1,0:T(8,128)(2,1)S(1)} %fusion.7.a), channel_id=1, source_target_pairs={{0,64},{64,0},{128,192},{192,128},{1,65},{65,1},{129,193},{193,129... | collective-permute-start | bytes 393224 | tf_op jit(solution)/shard_map/ppermute | solution.py:234
  121.5 4.2 %shard_map.76 = bf16[192,8192]{1,0:T(8,128)(2,1)} custom-call(s32[256]{0:T(256)S(1)} %select_reduce_fusion.place, s32[64]{0:T(128)S(1)} %xor.28.blocks, bf16[192,8192]{1,0:T(8,128)(2,1)S(1)} %get-tuple-element.72.g_ref, bf16[256,128,128]{2,1,0:T(8,128)(2,1)S(1)} %get-tuple-element.106.w_ref, ...), custom_call_target="tpu_custom_call", output_to_operand_aliasing={{}: (5, {})} | custom-call | tf_op jit(solution)/shard_map/pallas_call | solution.py:397
  128.3 1.9 %collective-permute-start.40 = (bf16[4,128,128]{2,1,0:T(8,128)(2,1)S(1)}, bf16[4,128,128]{2,1,0:T(8,128)(2,1)S(1)}, u32[]{:S(2)}, u32[]{:S(2)}) collective-permute-start(bf16[4,128,128]{2,1,0:T(8,128)(2,1)S(1)} %shard_map.77.refs_0_), channel_id=1, source_target_pairs={{0,48},{16,32},{32,16},{48,0},{1,49},{17,33},{33,17},{49,1},{2,50}... | collective-permute-start | bytes 393224 | tf_op jit(solution)/shard_map/ppermute | solution.py:234
  130.7 1.8 %collective-permute-start.38 = (bf16[4,128,128]{2,1,0:T(8,128)(2,1)S(1)}, bf16[4,128,128]{2,1,0:T(8,128)(2,1)S(1)}, u32[]{:S(2)}, u32[]{:S(2)}) collective-permute-start(bf16[4,128,128]{2,1,0:T(8,128)(2,1)S(1)} %shard_map.77.refs_0_), channel_id=1, source_target_pairs={{0,16},{16,0},{32,48},{48,32},{1,17},{17,1},{33,49},{49,33},{2,18}... | collective-permute-start | bytes 393224 | tf_op jit(solution)/shard_map/ppermute | solution.py:234
  132.5 2.1 %collective-permute-done.40.refs_3_ = bf16[4,128,128]{2,1,0:T(8,128)(2,1)S(1)} collective-permute-done((bf16[4,128,128]{2,1,0:T(8,128)(2,1)S(1)}, bf16[4,128,128]{2,1,0:T(8,128)(2,1)S(1)}, u32[]{:S(2)}, u32[]{:S(2)}) %collective-permute-start.40) | collective-permute-done | bytes 131104 | tf_op jit(solution)/shard_map/ppermute | solution.py:234
  134.6 2.1 %collective-permute-done.39.refs_2_ = bf16[4,128,128]{2,1,0:T(8,128)(2,1)S(1)} collective-permute-done((bf16[4,128,128]{2,1,0:T(8,128)(2,1)S(1)}, bf16[4,128,128]{2,1,0:T(8,128)(2,1)S(1)}, u32[]{:S(2)}, u32[]{:S(2)}) %collective-permute-start.39) | collective-permute-done | bytes 131104 | tf_op jit(solution)/shard_map/ppermute | solution.py:234
  136.8 1.6 %shard_map.78 = f32[16,128,128]{2,1,0:T(8,128)} custom-call(s32[4]{0:T(128)S(1)} %pad_add_fusion.1.where, bf16[4,128,128]{2,1,0:T(8,128)(2,1)S(1)} %shard_map.77.refs_0_, bf16[4,128,128]{2,1,0:T(8,128)(2,1)S(1)} %collective-permute-done.38.refs_1_, bf16[4,128,128]{2,1,0:T(8,128)(2,1)S(1)} %collective-permute-done.39.refs_2_, ...), custom_call_target="tpu_custom_call" | custom-call | tf_op jit(solution)/shard_map/pallas_call | solution.py:413
  (73 shorter events, 15.6 us)
Async XLA Ops:
  0.6 17.5 %collective-permute-start.3 = (bf16[192,8192]{1,0:T(8,128)(2,1)}, bf16[192,8192]{1,0:T(8,128)(2,1)S(1)}, u32[]{:S(2)}, u32[]{:S(2)}) collective-permute-start(bf16[192,8192]{1,0:T(8,128)(2,1)} %x_hbm.1), channel_id=1, source_target_pairs={{0,1},{1,0},{2,3},{3,2},{4,5},{5,4},{6,7},{7,6},{8,9},{9,8},{10,11... | collective-permute-start | bytes 9437192 | tf_op jit(solution)/shard_map/ppermute | solution.py:234
  0.7 14.7 %collective-permute-start.2 = (bf16[16,128,128]{2,1,0:T(8,128)(2,1)}, bf16[16,128,128]{2,1,0:T(8,128)(2,1)}, u32[]{:S(2)}, u32[]{:S(2)}) collective-permute-start(bf16[16,128,128]{2,1,0:T(8,128)(2,1)} %refs_0_.1), channel_id=1, source_target_pairs={{0,2},{2,0},{1,3},{3,1},{4,6},{6,4},{5,7},{7,5},{8,10},{10,8},{9,1... | collective-permute-start | bytes 1572872 | tf_op jit(solution)/shard_map/ppermute | solution.py:234
  2.7 15.5 %collective-permute-start.1 = (bf16[16,128,128]{2,1,0:T(8,128)(2,1)}, bf16[16,128,128]{2,1,0:T(8,128)(2,1)}, u32[]{:S(2)}, u32[]{:S(2)}) collective-permute-start(bf16[16,128,128]{2,1,0:T(8,128)(2,1)} %refs_0_.1), channel_id=1, source_target_pairs={{0,12},{4,8},{8,4},{12,0},{1,13},{5,9},{9,5},{13,1},{2,14},{6,10},... | collective-permute-start | bytes 1572872 | tf_op jit(solution)/shard_map/ppermute | solution.py:234
  3.7 14.5 %collective-permute-start = (bf16[16,128,128]{2,1,0:T(8,128)(2,1)}, bf16[16,128,128]{2,1,0:T(8,128)(2,1)}, u32[]{:S(2)}, u32[]{:S(2)}) collective-permute-start(bf16[16,128,128]{2,1,0:T(8,128)(2,1)} %refs_0_.1), channel_id=1, source_target_pairs={{0,4},{4,0},{8,12},{12,8},{1,5},{5,1},{9,13},{13,9},{2,6},{6,2},{1... | collective-permute-start | bytes 1572872 | tf_op jit(solution)/shard_map/ppermute | solution.py:234
  3.9 14.3 %collective-permute-start.4 = (bf16[16,128,128]{2,1,0:T(8,128)(2,1)}, bf16[16,128,128]{2,1,0:T(8,128)(2,1)}, u32[]{:S(2)}, u32[]{:S(2)}) collective-permute-start(bf16[16,128,128]{2,1,0:T(8,128)(2,1)} %refs_0_.1), channel_id=1, source_target_pairs={{0,1},{1,0},{2,3},{3,2},{4,5},{5,4},{6,7},{7,6},{8,9},{9,8},{10,11... | collective-permute-start | bytes 1572872 | tf_op jit(solution)/shard_map/ppermute | solution.py:234
  18.2 15.2 %collective-permute-start.9 = (bf16[16,128,128]{2,1,0:T(8,128)(2,1)}, bf16[16,128,128]{2,1,0:T(8,128)(2,1)}, u32[]{:S(2)}, u32[]{:S(2)}) collective-permute-start(bf16[16,128,128]{2,1,0:T(8,128)(2,1)} %collective-permute-done.refs_1_.left), channel_id=1, source_target_pairs={{0,1},{1,0},{2,3},{3,2},{4,5},{5,4},{6,7},{7,6},{8,9},{9,8},{10,11... | collective-permute-start | bytes 1572872 | tf_op jit(solution)/shard_map/ppermute | solution.py:234
  18.3 15.1 %collective-permute-start.5 = (bf16[16,128,128]{2,1,0:T(8,128)(2,1)}, bf16[16,128,128]{2,1,0:T(8,128)(2,1)}, u32[]{:S(2)}, u32[]{:S(2)}) collective-permute-start(bf16[16,128,128]{2,1,0:T(8,128)(2,1)} %collective-permute-done.refs_1_.left), channel_id=1, source_target_pairs={{0,2},{2,0},{1,3},{3,1},{4,6},{6,4},{5,7},{7,5},{8,10},{10,8},{9,1... | collective-permute-start | bytes 1572872 | tf_op jit(solution)/shard_map/ppermute | solution.py:234
  19.7 14.6 %collective-permute-start.6 = (bf16[16,128,128]{2,1,0:T(8,128)(2,1)}, bf16[16,128,128]{2,1,0:T(8,128)(2,1)}, u32[]{:S(2)}, u32[]{:S(2)}) collective-permute-start(bf16[16,128,128]{2,1,0:T(8,128)(2,1)} %collective-permute-done.1.refs_2_.right), channel_id=1, source_target_pairs={{0,194},{2,64},{64,2},{66,128},{128,66},{130,192},{192,130},{194,0... | collective-permute-start | bytes 1572872 | tf_op jit(solution)/shard_map/ppermute | solution.py:238
  23.6 9.6 %collective-permute-start.7 = (bf16[8,128,128]{2,1,0:T(8,128)(2,1)}, bf16[8,128,128]{2,1,0:T(8,128)(2,1)S(1)}, u32[]{:S(2)}, u32[]{:S(2)}) collective-permute-start(bf16[8,128,128]{2,1,0:T(8,128)(2,1)} %get-tuple-element.73), channel_id=1, source_target_pairs={{0,12},{4,8},{8,4},{12,0},{1,13},{5,9},{9,5},{13,1},{2,14},{6,10},... | collective-permute-start | bytes 786440 | tf_op jit(solution)/shard_map/ppermute | solution.py:234
  25.3 8.1 %collective-permute-start.8 = (bf16[8,128,128]{2,1,0:T(8,128)(2,1)}, bf16[8,128,128]{2,1,0:T(8,128)(2,1)}, u32[]{:S(2)}, u32[]{:S(2)}) collective-permute-start(bf16[8,128,128]{2,1,0:T(8,128)(2,1)} %get-tuple-element.74), channel_id=1, source_target_pairs={{0,4},{4,0},{8,12},{12,8},{1,5},{5,1},{9,13},{13,9},{2,6},{6,2},{1... | collective-permute-start | bytes 786440 | tf_op jit(solution)/shard_map/ppermute | solution.py:234
  34.4 6.4 %collective-permute-start.12 = (bf16[16,128,128]{2,1,0:T(8,128)(2,1)}, bf16[16,128,128]{2,1,0:T(8,128)(2,1)S(1)}, u32[]{:S(2)}, u32[]{:S(2)}) collective-permute-start(bf16[16,128,128]{2,1,0:T(8,128)(2,1)} %collective-permute-done.1.refs_2_.right), channel_id=1, source_target_pairs={{0,1},{1,0},{2,3},{3,2},{4,5},{5,4},{6,7},{7,6},{8,9},{9,8},{10,11... | collective-permute-start | bytes 1572872 | tf_op jit(solution)/shard_map/ppermute | solution.py:234
  34.4 6.5 %collective-permute-start.13 = (bf16[16,128,128]{2,1,0:T(8,128)(2,1)}, bf16[16,128,128]{2,1,0:T(8,128)(2,1)S(1)}, u32[]{:S(2)}, u32[]{:S(2)}) collective-permute-start(bf16[16,128,128]{2,1,0:T(8,128)(2,1)} %collective-permute-done.2.refs_3_), channel_id=1, source_target_pairs={{0,1},{1,0},{2,3},{3,2},{4,5},{5,4},{6,7},{7,6},{8,9},{9,8},{10,11... | collective-permute-start | bytes 1572872 | tf_op jit(solution)/shard_map/ppermute | solution.py:234
  34.9 6.0 %collective-permute-start.14 = (bf16[16,128,128]{2,1,0:T(8,128)(2,1)}, bf16[16,128,128]{2,1,0:T(8,128)(2,1)S(1)}, u32[]{:S(2)}, u32[]{:S(2)}) collective-permute-start(bf16[16,128,128]{2,1,0:T(8,128)(2,1)} %collective-permute-done.5.refs_0_), channel_id=1, source_target_pairs={{0,1},{1,0},{2,3},{3,2},{4,5},{5,4},{6,7},{7,6},{8,9},{9,8},{10,11... | collective-permute-start | bytes 1572872 | tf_op jit(solution)/shard_map/ppermute | solution.py:234
  34.9 10.9 %collective-permute-start.10 = (bf16[8,128,128]{2,1,0:T(8,128)(2,1)S(1)}, bf16[8,128,128]{2,1,0:T(8,128)(2,1)S(1)}, u32[]{:S(2)}, u32[]{:S(2)}) collective-permute-start(bf16[8,128,128]{2,1,0:T(8,128)(2,1)S(1)} %collective-permute-done.7.refs_2_), channel_id=1, source_target_pairs={{0,2},{2,0},{1,3},{3,1},{4,6},{6,4},{5,7},{7,5},{8,10},{10,8},{9,1... | collective-permute-start | bytes 786440 | tf_op jit(solution)/shard_map/ppermute | solution.py:234
  38.8 8.6 %collective-permute-start.11 = (bf16[8,128,128]{2,1,0:T(8,128)(2,1)}, bf16[8,128,128]{2,1,0:T(8,128)(2,1)S(1)}, u32[]{:S(2)}, u32[]{:S(2)}) collective-permute-start(bf16[8,128,128]{2,1,0:T(8,128)(2,1)} %collective-permute-done.8.refs_3_), channel_id=1, source_target_pairs={{0,194},{2,64},{64,2},{66,128},{128,66},{130,192},{192,130},{194,0... | collective-permute-start | bytes 786440 | tf_op jit(solution)/shard_map/ppermute | solution.py:238
  40.8 7.1 %collective-permute-start.15 = (bf16[16,128,128]{2,1,0:T(8,128)(2,1)}, bf16[16,128,128]{2,1,0:T(8,128)(2,1)S(1)}, u32[]{:S(2)}, u32[]{:S(2)}) collective-permute-start(bf16[16,128,128]{2,1,0:T(8,128)(2,1)} %collective-permute-done.6.refs_1_), channel_id=1, source_target_pairs={{0,1},{1,0},{2,3},{3,2},{4,5},{5,4},{6,7},{7,6},{8,9},{9,8},{10,11... | collective-permute-start | bytes 1572872 | tf_op jit(solution)/shard_map/ppermute | solution.py:234
  47.4 2.7 %collective-permute-start.18 = (bf16[16,128,128]{2,1,0:T(8,128)(2,1)S(1)}, bf16[16,128,128]{2,1,0:T(8,128)(2,1)S(1)}, u32[]{:S(2)}, u32[]{:S(2)}) collective-permute-start(bf16[16,128,128]{2,1,0:T(8,128)(2,1)S(1)} %pad_maximum_fusion.2), channel_id=1, source_target_pairs={{0,1},{1,0},{2,3},{3,2},{4,5},{5,4},{6,7},{7,6},{8,9},{9,8},{10,11... | collective-permute-start | bytes 1572872 | tf_op jit(solution)/shard_map/ppermute | solution.py:234
  47.4 2.3 %collective-permute-start.16 = (bf16[8,128,128]{2,1,0:T(8,128)(2,1)S(1)}, bf16[8,128,128]{2,1,0:T(8,128)(2,1)S(1)}, u32[]{:S(2)}, u32[]{:S(2)}) collective-permute-start(bf16[8,128,128]{2,1,0:T(8,128)(2,1)S(1)} %collective-permute-done.10.refs_0_), channel_id=1, source_target_pairs={{0,1},{1,0},{2,3},{3,2},{4,5},{5,4},{6,7},{7,6},{8,9},{9,8},{10,11... | collective-permute-start | bytes 786440 | tf_op jit(solution)/shard_map/ppermute | solution.py:234
  47.9 2.1 %collective-permute-start.17 = (bf16[8,128,128]{2,1,0:T(8,128)(2,1)S(1)}, bf16[8,128,128]{2,1,0:T(8,128)(2,1)S(1)}, u32[]{:S(2)}, u32[]{:S(2)}) collective-permute-start(bf16[8,128,128]{2,1,0:T(8,128)(2,1)S(1)} %collective-permute-done.11.refs_1_), channel_id=1, source_target_pairs={{0,1},{1,0},{2,3},{3,2},{4,5},{5,4},{6,7},{7,6},{8,9},{9,8},{10,11... | collective-permute-start | bytes 786440 | tf_op jit(solution)/shard_map/ppermute | solution.py:234
  55.9 6.0 %copy-start = (s32[256]{0:T(256)S(1)}, s32[256]{0:T(256)}, u32[]{:S(2)}) copy-start(s32[256]{0:T(256)} %rows.3) | copy-start | bytes 3076
  56.0 6.0 %copy-start.1 = (s32[256]{0:T(256)S(1)}, s32[256]{0:T(256)}, u32[]{:S(2)}) copy-start(s32[256]{0:T(256)} %cols.3) | copy-start | bytes 3076
  56.0 6.0 %collective-permute-start.19 = (bf16[64,192,128]{2,1,0:T(8,128)(2,1)S(1)}, bf16[64,192,128]{2,1,0:T(8,128)(2,1)S(1)}, u32[]{:S(2)}, u32[]{:S(2)}) collective-permute-start(bf16[64,192,128]{2,1,0:T(8,128)(2,1)S(1)} %get-tuple-element.91.s_ref), channel_id=1, source_target_pairs={{0,1},{1,0},{2,3},{3,2},{4,5},{5,4},{6,7},{7,6},{8,9},{9,8},{10,11... | collective-permute-start | bytes 9437192 | tf_op jit(solution)/shard_map/ppermute | solution.py:234
  64.5 14.3 %collective-permute-start.20 = (bf16[16,128,128]{2,1,0:T(8,128)(2,1)S(1)}, bf16[16,128,128]{2,1,0:T(8,128)(2,1)S(1)}, u32[]{:S(2)}, u32[]{:S(2)}) collective-permute-start(bf16[16,128,128]{2,1,0:T(8,128)(2,1)S(1)} %get-tuple-element.92), channel_id=1, source_target_pairs={{0,4},{4,0},{8,12},{12,8},{1,5},{5,1},{9,13},{13,9},{2,6},{6,2},{1... | collective-permute-start | bytes 1572872 | tf_op jit(solution)/shard_map/ppermute | solution.py:234
  64.9 15.2 %collective-permute-start.21 = (bf16[16,128,128]{2,1,0:T(8,128)(2,1)S(1)}, bf16[16,128,128]{2,1,0:T(8,128)(2,1)S(1)}, u32[]{:S(2)}, u32[]{:S(2)}) collective-permute-start(bf16[16,128,128]{2,1,0:T(8,128)(2,1)S(1)} %get-tuple-element.93), channel_id=1, source_target_pairs={{0,12},{4,8},{8,4},{12,0},{1,13},{5,9},{9,5},{13,1},{2,14},{6,10},... | collective-permute-start | bytes 1572872 | tf_op jit(solution)/shard_map/ppermute | solution.py:234
  66.2 13.9 %collective-permute-start.22 = (bf16[16,128,128]{2,1,0:T(8,128)(2,1)S(1)}, bf16[16,128,128]{2,1,0:T(8,128)(2,1)S(1)}, u32[]{:S(2)}, u32[]{:S(2)}) collective-permute-start(bf16[16,128,128]{2,1,0:T(8,128)(2,1)S(1)} %get-tuple-element.94), channel_id=1, source_target_pairs={{0,16},{16,0},{32,48},{48,32},{1,17},{17,1},{33,49},{49,33},{2,18}... | collective-permute-start | bytes 1572872 | tf_op jit(solution)/shard_map/ppermute | solution.py:234
  67.8 14.8 %collective-permute-start.23 = (bf16[16,128,128]{2,1,0:T(8,128)(2,1)S(1)}, bf16[16,128,128]{2,1,0:T(8,128)(2,1)S(1)}, u32[]{:S(2)}, u32[]{:S(2)}) collective-permute-start(bf16[16,128,128]{2,1,0:T(8,128)(2,1)S(1)} %get-tuple-element.95), channel_id=1, source_target_pairs={{0,48},{16,32},{32,16},{48,0},{1,49},{17,33},{33,17},{49,1},{2,50}... | collective-permute-start | bytes 1572872 | tf_op jit(solution)/shard_map/ppermute | solution.py:234
  82.7 16.4 %collective-permute-start.30 = (bf16[8,128,128]{2,1,0:T(8,128)(2,1)S(1)}, bf16[8,128,128]{2,1,0:T(8,128)(2,1)S(1)}, u32[]{:S(2)}, u32[]{:S(2)}) collective-permute-start(bf16[8,128,128]{2,1,0:T(8,128)(2,1)S(1)} %add_convert_fusion), channel_id=1, source_target_pairs={{0,16},{16,0},{32,48},{48,32},{1,17},{17,1},{33,49},{49,33},{2,18}... | collective-permute-start | bytes 786440 | tf_op jit(solution)/shard_map/ppermute | solution.py:234
  82.9 7.2 %collective-permute-start.25 = (bf16[8,128,128]{2,1,0:T(8,128)(2,1)S(1)}, bf16[8,128,128]{2,1,0:T(8,128)(2,1)S(1)}, u32[]{:S(2)}, u32[]{:S(2)}) collective-permute-start(bf16[8,128,128]{2,1,0:T(8,128)(2,1)S(1)} %add_convert_fusion.2), channel_id=1, source_target_pairs={{0,4},{4,0},{8,12},{12,8},{1,5},{5,1},{9,13},{13,9},{2,6},{6,2},{1... | collective-permute-start | bytes 786440 | tf_op jit(solution)/shard_map/ppermute | solution.py:234
  84.1 15.2 %collective-permute-start.29 = (bf16[8,128,128]{2,1,0:T(8,128)(2,1)S(1)}, bf16[8,128,128]{2,1,0:T(8,128)(2,1)S(1)}, u32[]{:S(2)}, u32[]{:S(2)}) collective-permute-start(bf16[8,128,128]{2,1,0:T(8,128)(2,1)S(1)} %add_convert_fusion.1), channel_id=1, source_target_pairs={{0,48},{16,32},{32,16},{48,0},{1,49},{17,33},{33,17},{49,1},{2,50}... | collective-permute-start | bytes 786440 | tf_op jit(solution)/shard_map/ppermute | solution.py:234
  86.5 7.7 %collective-permute-start.24 = (bf16[8,128,128]{2,1,0:T(8,128)(2,1)S(1)}, bf16[8,128,128]{2,1,0:T(8,128)(2,1)S(1)}, u32[]{:S(2)}, u32[]{:S(2)}) collective-permute-start(bf16[8,128,128]{2,1,0:T(8,128)(2,1)S(1)} %add_convert_fusion.3), channel_id=1, source_target_pairs={{0,12},{4,8},{8,4},{12,0},{1,13},{5,9},{9,5},{13,1},{2,14},{6,10},... | collective-permute-start | bytes 786440 | tf_op jit(solution)/shard_map/ppermute | solution.py:234
  94.4 5.1 %collective-permute-start.26 = (bf16[4,128,128]{2,1,0:T(8,128)(2,1)S(1)}, bf16[4,128,128]{2,1,0:T(8,128)(2,1)S(1)}, u32[]{:S(2)}, u32[]{:S(2)}) collective-permute-start(bf16[4,128,128]{2,1,0:T(8,128)(2,1)S(1)} %get-tuple-element.133), channel_id=1, source_target_pairs={{0,16},{16,0},{32,48},{48,32},{1,17},{17,1},{33,49},{49,33},{2,18}... | collective-permute-start | bytes 393224 | tf_op jit(solution)/shard_map/ppermute | solution.py:234
  95.8 6.5 %collective-permute-start.28 = (bf16[4,128,128]{2,1,0:T(8,128)(2,1)S(1)}, bf16[4,128,128]{2,1,0:T(8,128)(2,1)S(1)}, u32[]{:S(2)}, u32[]{:S(2)}) collective-permute-start(bf16[4,128,128]{2,1,0:T(8,128)(2,1)S(1)} %get-tuple-element.134), channel_id=1, source_target_pairs={{0,32},{16,48},{32,0},{48,16},{1,33},{17,49},{33,1},{49,17},{2,34}... | collective-permute-start | bytes 393224 | tf_op jit(solution)/shard_map/ppermute | solution.py:234
  96.9 6.8 %collective-permute-start.27 = (bf16[4,128,128]{2,1,0:T(8,128)(2,1)S(1)}, bf16[4,128,128]{2,1,0:T(8,128)(2,1)S(1)}, u32[]{:S(2)}, u32[]{:S(2)}) collective-permute-start(bf16[4,128,128]{2,1,0:T(8,128)(2,1)S(1)} %get-tuple-element.135), channel_id=1, source_target_pairs={{0,48},{16,32},{32,16},{48,0},{1,49},{17,33},{33,17},{49,1},{2,50}... | collective-permute-start | bytes 393224 | tf_op jit(solution)/shard_map/ppermute | solution.py:234
  103.8 11.1 %collective-permute-start.34 = (f32[4,128,128]{2,1,0:T(8,128)S(1)}, f32[4,128,128]{2,1,0:T(8,128)S(1)}, u32[]{:S(2)}, u32[]{:S(2)}) collective-permute-start(f32[4,128,128]{2,1,0:T(8,128)S(1)} %fusion.4), channel_id=1, source_target_pairs={{0,2},{2,0},{1,3},{3,1},{4,6},{6,4},{5,7},{7,5},{8,10},{10,8},{9,1... | collective-permute-start | bytes 786440 | tf_op jit(solution)/shard_map/ppermute | solution.py:234
  105.5 5.1 %collective-permute-start.31 = (bf16[4,128,128]{2,1,0:T(8,128)(2,1)S(1)}, bf16[4,128,128]{2,1,0:T(8,128)(2,1)S(1)}, u32[]{:S(2)}, u32[]{:S(2)}) collective-permute-start(bf16[4,128,128]{2,1,0:T(8,128)(2,1)S(1)} %get-tuple-element.130), channel_id=1, source_target_pairs={{0,4},{4,0},{8,12},{12,8},{1,5},{5,1},{9,13},{13,9},{2,6},{6,2},{1... | collective-permute-start | bytes 393224 | tf_op jit(solution)/shard_map/ppermute | solution.py:234
  105.6 7.4 %collective-permute-start.33 = (bf16[4,128,128]{2,1,0:T(8,128)(2,1)S(1)}, bf16[4,128,128]{2,1,0:T(8,128)(2,1)S(1)}, u32[]{:S(2)}, u32[]{:S(2)}) collective-permute-start(bf16[4,128,128]{2,1,0:T(8,128)(2,1)S(1)} %get-tuple-element.131), channel_id=1, source_target_pairs={{0,8},{4,12},{8,0},{12,4},{1,9},{5,13},{9,1},{13,5},{2,10},{6,14},... | collective-permute-start | bytes 393224 | tf_op jit(solution)/shard_map/ppermute | solution.py:234
  108.7 6.2 %collective-permute-start.32 = (bf16[4,128,128]{2,1,0:T(8,128)(2,1)S(1)}, bf16[4,128,128]{2,1,0:T(8,128)(2,1)S(1)}, u32[]{:S(2)}, u32[]{:S(2)}) collective-permute-start(bf16[4,128,128]{2,1,0:T(8,128)(2,1)S(1)} %get-tuple-element.132), channel_id=1, source_target_pairs={{0,12},{4,8},{8,4},{12,0},{1,13},{5,9},{9,5},{13,1},{2,14},{6,10},... | collective-permute-start | bytes 393224 | tf_op jit(solution)/shard_map/ppermute | solution.py:234
  115.0 10.8 %collective-permute-start.37 = (bf16[4,128,128]{2,1,0:T(8,128)(2,1)S(1)}, bf16[4,128,128]{2,1,0:T(8,128)(2,1)S(1)}, u32[]{:S(2)}, u32[]{:S(2)}) collective-permute-start(bf16[4,128,128]{2,1,0:T(8,128)(2,1)S(1)} %fusion.7.a), channel_id=1, source_target_pairs={{0,192},{64,128},{128,64},{192,0},{1,193},{65,129},{129,65},{193,1... | collective-permute-start | bytes 393224 | tf_op jit(solution)/shard_map/ppermute | solution.py:234
  118.0 9.0 %collective-permute-start.36 = (bf16[4,128,128]{2,1,0:T(8,128)(2,1)S(1)}, bf16[4,128,128]{2,1,0:T(8,128)(2,1)S(1)}, u32[]{:S(2)}, u32[]{:S(2)}) collective-permute-start(bf16[4,128,128]{2,1,0:T(8,128)(2,1)S(1)} %fusion.7.a), channel_id=1, source_target_pairs={{0,128},{64,192},{128,0},{192,64},{1,129},{65,193},{129,1},{193,65... | collective-permute-start | bytes 393224 | tf_op jit(solution)/shard_map/ppermute | solution.py:234
  119.6 8.4 %collective-permute-start.35 = (bf16[4,128,128]{2,1,0:T(8,128)(2,1)S(1)}, bf16[4,128,128]{2,1,0:T(8,128)(2,1)S(1)}, u32[]{:S(2)}, u32[]{:S(2)}) collective-permute-start(bf16[4,128,128]{2,1,0:T(8,128)(2,1)S(1)} %fusion.7.a), channel_id=1, source_target_pairs={{0,64},{64,0},{128,192},{192,128},{1,65},{65,1},{129,193},{193,129... | collective-permute-start | bytes 393224 | tf_op jit(solution)/shard_map/ppermute | solution.py:234
  128.3 6.3 %collective-permute-start.40 = (bf16[4,128,128]{2,1,0:T(8,128)(2,1)S(1)}, bf16[4,128,128]{2,1,0:T(8,128)(2,1)S(1)}, u32[]{:S(2)}, u32[]{:S(2)}) collective-permute-start(bf16[4,128,128]{2,1,0:T(8,128)(2,1)S(1)} %shard_map.77.refs_0_), channel_id=1, source_target_pairs={{0,48},{16,32},{32,16},{48,0},{1,49},{17,33},{33,17},{49,1},{2,50}... | collective-permute-start | bytes 393224 | tf_op jit(solution)/shard_map/ppermute | solution.py:234
  130.2 6.5 %collective-permute-start.39 = (bf16[4,128,128]{2,1,0:T(8,128)(2,1)S(1)}, bf16[4,128,128]{2,1,0:T(8,128)(2,1)S(1)}, u32[]{:S(2)}, u32[]{:S(2)}) collective-permute-start(bf16[4,128,128]{2,1,0:T(8,128)(2,1)S(1)} %shard_map.77.refs_0_), channel_id=1, source_target_pairs={{0,32},{16,48},{32,0},{48,16},{1,33},{17,49},{33,1},{49,17},{2,34}... | collective-permute-start | bytes 393224 | tf_op jit(solution)/shard_map/ppermute | solution.py:234
  130.7 6.1 %collective-permute-start.38 = (bf16[4,128,128]{2,1,0:T(8,128)(2,1)S(1)}, bf16[4,128,128]{2,1,0:T(8,128)(2,1)S(1)}, u32[]{:S(2)}, u32[]{:S(2)}) collective-permute-start(bf16[4,128,128]{2,1,0:T(8,128)(2,1)S(1)} %shard_map.77.refs_0_), channel_id=1, source_target_pairs={{0,16},{16,0},{32,48},{48,32},{1,17},{17,1},{33,49},{49,33},{2,18}... | collective-permute-start | bytes 393224 | tf_op jit(solution)/shard_map/ppermute | solution.py:234
